TPU v7x, 32 devices: a whole 2x2x4 slice. The times are simulated.
32 devices in a mesh: dp: 8 (over z, y), seq: 4 (over x, core).
Axes of the slice: x: 2, y: 2, z: 4, core: 2. Of those that a mesh axis runs over, the one named last changes fastest.
Arguments:
- tokens: bfloat16 [16384, 1024], P(('dp', 'seq')), may hold values from -6 to 6
- attn_gain: bfloat16 [1024], replicated, may hold values from 0.25 to 1.75
- w_query: bfloat16 [1024, 256], replicated, may hold values from -0.1875 to 0.1875
- w_key: bfloat16 [1024, 256], replicated, may hold values from -0.1875 to 0.1875
- w_value: bfloat16 [1024, 1024], replicated, may hold values from -0.1875 to 0.1875
- w_output: bfloat16 [1024, 1024], replicated, may hold values from -0.75 to 0.75
- mlp_gain: bfloat16 [1024], replicated, may hold values from 0.25 to 1.75
- w_gate: bfloat16 [1024, 2752], P(('dp', 'seq')), may hold values from -0.1875 to 0.1875
- w_up: bfloat16 [1024, 2752], P(('dp', 'seq')), may hold values from -0.1875 to 0.1875
- w_down: bfloat16 [1024, 2752], P(('dp', 'seq')), may hold values from -0.109375 to 0.109375
- out_grad: bfloat16 [16384, 1024], P(('dp', 'seq')), may hold values from -6 to 6
Outputs:
- layer_out: bfloat16 [16384, 1024], P(('dp', 'seq'))
- tokens_grad: float32 [16384, 1024], P(('dp', 'seq'))
- attn_gain_grad: float32 [1024], P(('dp', 'seq'))
- w_query_grad: float32 [1024, 256], P(('dp', 'seq'))
- w_key_grad: float32 [1024, 256], P(('dp', 'seq'))
- w_value_grad: float32 [1024, 1024], P(('dp', 'seq'))
- w_output_grad: float32 [1024, 1024], P(('dp', 'seq'))
- mlp_gain_grad: float32 [1024], P(('dp', 'seq'))
- w_gate_grad: float32 [1024, 2752], P(('dp', 'seq'))
- w_up_grad: float32 [1024, 2752], P(('dp', 'seq'))
- w_down_grad: float32 [1024, 2752], P(('dp', 'seq'))
All inputs are finite; a program needn't handle non-finite values.
Results may differ from a plain program's by a relative error of at most 0.012.
Values may be sent and summed in bfloat16 or wider, within the bound.
A program may use at most 192 MiB of HBM per device.

v0:
```python
import math

import jax
import jax.numpy as jnp
from jax import lax
from jax.sharding import PartitionSpec as P

KD = 16
VD = 64
GROUP = 512
FEAT = 273


epsilon = 1e-05
quad_scale = 1.0 / (4.0 * math.sqrt(2.0))


def lowered(value):
    rounded = lax.optimization_barrier(value.astype(jnp.bfloat16)).astype(jnp.float32)
    return value + lax.stop_gradient(rounded - value)


def product(left, right):
    return jnp.dot(left, right, precision=lax.Precision.HIGHEST, preferred_element_type=jnp.float32)


def project(left, right):
    return jnp.dot(left, right, preferred_element_type=jnp.float32)


def project_back(left, right):
    return lax.dot_general(
        left, right, (((1,), (1,)), ((), ())), preferred_element_type=jnp.float32
    )


def outer_sum(left, right):
    return lax.dot_general(
        left, right, (((0,), (0,)), ((), ())), preferred_element_type=jnp.float32
    )


def rms_norm(inputs, gain):
    return inputs * lax.rsqrt(jnp.mean(inputs * inputs, axis=-1, keepdims=True) + epsilon) * gain


def features(vectors):
    count = vectors.shape[0]
    square = (vectors[:, :, None] * vectors[:, None, :]).reshape(count, -1) * quad_scale
    return jnp.concatenate([jnp.ones((count, 1), jnp.float32), vectors * 0.5, square], axis=1)


def block_step(carry, block):
    state, total = carry
    queries, keys, values = block
    width = queries.shape[0]
    score = product(queries, keys.T) * 0.25
    weight = 1.0 + score + 0.5 * score * score
    later = lax.broadcasted_iota(jnp.int32, (width, width), 0) >= lax.broadcasted_iota(
        jnp.int32, (width, width), 1
    )
    weight = jnp.where(later, weight, 0.0)
    query_feat = lowered(features(queries))
    key_feat = lowered(features(keys))
    numer = product(lowered(weight), values) + product(query_feat, lowered(state))
    denom = jnp.sum(weight, axis=1) + product(query_feat, total)
    state = state + product(key_feat.T, values)
    total = total + jnp.sum(key_feat, axis=0)
    return ((state, total), numer / denom[:, None])


def head_attention(queries, keys, values):
    length = queries.shape[0]
    blocks = length // GROUP
    split = (
        queries.reshape(blocks, GROUP, -1),
        keys.reshape(blocks, GROUP, -1),
        values.reshape(blocks, GROUP, -1),
    )
    start = (jnp.zeros((FEAT, values.shape[1]), jnp.float32), jnp.zeros((FEAT,), jnp.float32))
    final_carry, mixed = lax.scan(jax.checkpoint(block_step), start, split)
    return mixed.reshape(length, -1)


def all_heads(queries, keys, values):
    return jax.vmap(head_attention, in_axes=1, out_axes=1)(queries, keys, values)


def gated(gate_in, up_in):
    return jax.nn.silu(gate_in) * up_in


def shards(
    tokens, attn_gain, w_query, w_key, w_value, w_output, mlp_gain, w_gate, w_up, w_down, out_grad
):
    tok_rows = tokens.shape[0]
    head_count = w_query.shape[1] // KD
    inputs = tokens.astype(jnp.float32)
    normed, first_back = jax.vjp(rms_norm, inputs, attn_gain.astype(jnp.float32))
    normed_low = normed.astype(jnp.bfloat16)
    queries = project(normed_low, w_query).astype(jnp.bfloat16).reshape(tok_rows, head_count, KD)
    keys = project(normed_low, w_key).astype(jnp.bfloat16).reshape(tok_rows, head_count, KD)
    values = project(normed_low, w_value).astype(jnp.bfloat16).reshape(tok_rows, head_count, VD)
    head_query, head_keys, head_values = (
        lax.all_to_all(queries, "seq", split_axis=1, concat_axis=0, tiled=True),
        lax.all_to_all(keys, "seq", split_axis=1, concat_axis=0, tiled=True),
        lax.all_to_all(values, "seq", split_axis=1, concat_axis=0, tiled=True),
    )
    mixed, attn_back = jax.vjp(
        all_heads,
        head_query.astype(jnp.float32),
        head_keys.astype(jnp.float32),
        head_values.astype(jnp.float32),
    )
    mixed_tok = lax.all_to_all(
        mixed.astype(jnp.bfloat16), "seq", split_axis=0, concat_axis=1, tiled=True
    ).reshape(tok_rows, -1)
    middle = inputs + project(mixed_tok, w_output)
    normed_mlp, second_back = jax.vjp(rms_norm, middle, mlp_gain.astype(jnp.float32))
    mlp_low = normed_mlp.astype(jnp.bfloat16)
    gate_full, up_full, down_full = (
        lax.all_gather(w_gate, ("dp", "seq"), axis=0, tiled=True),
        lax.all_gather(w_up, ("dp", "seq"), axis=0, tiled=True),
        lax.all_gather(w_down, ("dp", "seq"), axis=0, tiled=True),
    )
    gate = project(mlp_low, gate_full)
    upward = project(mlp_low, up_full)
    hidden_val, gated_back = jax.vjp(gated, gate, upward)
    hidden = hidden_val.astype(jnp.bfloat16)
    layer_out = (middle + project_back(hidden, down_full)).astype(jnp.bfloat16)
    gate_full, up_full, down_full = (
        lax.all_gather(w_gate, ("dp", "seq"), axis=0, tiled=True),
        lax.all_gather(w_up, ("dp", "seq"), axis=0, tiled=True),
        lax.all_gather(w_down, ("dp", "seq"), axis=0, tiled=True),
    )
    d_hidden = project(out_grad, down_full)
    down_grad = outer_sum(out_grad, hidden)
    d_gate_f, d_up_f = gated_back(d_hidden)
    d_gate = d_gate_f.astype(jnp.bfloat16)
    d_up = d_up_f.astype(jnp.bfloat16)
    gate_grad = outer_sum(mlp_low, d_gate)
    up_grad = outer_sum(mlp_low, d_up)
    d_normed_mlp = project_back(d_gate, gate_full) + project_back(d_up, up_full)
    d_middle_norm, mlp_gain_part = second_back(d_normed_mlp)
    d_middle = out_grad.astype(jnp.float32) + d_middle_norm
    d_branch = d_middle.astype(jnp.bfloat16)
    output_grad = outer_sum(mixed_tok, d_branch)
    d_mixed = (
        project_back(d_branch, w_output).astype(jnp.bfloat16).reshape(tok_rows, head_count, VD)
    )
    ffn_sums = (
        lax.psum_scatter(gate_grad, ("dp", "seq"), scatter_dimension=0, tiled=True),
        lax.psum_scatter(up_grad, ("dp", "seq"), scatter_dimension=0, tiled=True),
        lax.psum_scatter(down_grad, ("dp", "seq"), scatter_dimension=0, tiled=True),
        lax.psum_scatter(output_grad, ("dp", "seq"), scatter_dimension=0, tiled=True),
        lax.psum_scatter(mlp_gain_part, ("dp", "seq"), scatter_dimension=0, tiled=True),
    )
    head_grad = lax.all_to_all(d_mixed, "seq", split_axis=1, concat_axis=0, tiled=True)
    d_query_h, d_keys_h, d_values_h = attn_back(head_grad.astype(jnp.float32))
    back_query, back_keys, back_values = (
        lax.all_to_all(
            d_query_h.astype(jnp.bfloat16), "seq", split_axis=0, concat_axis=1, tiled=True
        ),
        lax.all_to_all(
            d_keys_h.astype(jnp.bfloat16), "seq", split_axis=0, concat_axis=1, tiled=True
        ),
        lax.all_to_all(
            d_values_h.astype(jnp.bfloat16), "seq", split_axis=0, concat_axis=1, tiled=True
        ),
    )
    back_query = back_query.reshape(tok_rows, -1)
    back_keys = back_keys.reshape(tok_rows, -1)
    back_values = back_values.reshape(tok_rows, -1)
    d_normed = (
        project_back(back_query, w_query)
        + project_back(back_keys, w_key)
        + project_back(back_values, w_value)
    )
    query_grad = outer_sum(normed_low, back_query)
    key_grad = outer_sum(normed_low, back_keys)
    value_grad = outer_sum(normed_low, back_values)
    d_inputs_norm, attn_gain_part = first_back(d_normed)
    tokens_grad = d_middle + d_inputs_norm
    attn_sums = (
        lax.psum_scatter(query_grad, ("dp", "seq"), scatter_dimension=0, tiled=True),
        lax.psum_scatter(key_grad, ("dp", "seq"), scatter_dimension=0, tiled=True),
        lax.psum_scatter(value_grad, ("dp", "seq"), scatter_dimension=0, tiled=True),
        lax.psum_scatter(attn_gain_part, ("dp", "seq"), scatter_dimension=0, tiled=True),
    )
    return (
        layer_out,
        tokens_grad,
        attn_sums[3],
        attn_sums[0],
        attn_sums[1],
        attn_sums[2],
        ffn_sums[3],
        ffn_sums[4],
        ffn_sums[0],
        ffn_sums[1],
        ffn_sums[2],
    )


def solution(mesh):
    in_specs = (
        P(("dp", "seq"), None),
        P(),
        P(),
        P(),
        P(),
        P(),
        P(),
        P(("dp", "seq"), None),
        P(("dp", "seq"), None),
        P(("dp", "seq"), None),
        P(("dp", "seq"), None),
    )
    out_specs = (
        P(("dp", "seq"), None),
        P(("dp", "seq"), None),
        P(("dp", "seq")),
        P(("dp", "seq"), None),
        P(("dp", "seq"), None),
        P(("dp", "seq"), None),
        P(("dp", "seq"), None),
        P(("dp", "seq")),
        P(("dp", "seq"), None),
        P(("dp", "seq"), None),
        P(("dp", "seq"), None),
    )
    return jax.shard_map(shards, mesh=mesh, in_specs=in_specs, out_specs=out_specs, check_vma=False)
```

profile of v0, /device:TPU:0, one launch (start us, length us, event | category | flops | bytes accessed | tf_op | source)
XLA Modules:
  0.0 1544.4 jit_solution(14137388592473766231)
XLA Ops:
  13.6 4.2 all-to-all-start
  20.2 3.7 all-to-all-done
  23.8 4.1 all-to-all-start.2
  27.9 3.9 convolution_convert_fusion.1
  34.1 4.2 all-to-all-start.1
  52.0 5.7 all-to-all-done.1
  61.0 4.0 reshape.266
  65.0 3.6 reshape.262
  73.4 93.1 %while.45 = (s32[]{:T(128)}, f32[4,273,64]{1,2,0:T(8,128)S(1)}, f32[4,273]{1,0:T(4,128)S(1)}, bf16[4,4,512,64]{2,3,1,0:T(8,128)(2,1)}, f32[4,4,273,64]{2,3,1,0:T...) while((s32[]{:T(128)}, f32[4,273,64]{1,2,0:T(8,128)S(1)}, ...), condition=%wide.region_4.5_spmd.clone, body=%wide.region_1.4_spmd.clone.sunk | while | flops 1904537728 | bytes 60333960 | solution.py:81
  75.4 5.6 fusion.180
  96.4 5.6 fusion.180
  117.4 5.6 fusion.180
  138.4 5.6 fusion.180
  168.9 4.0 copy.125
  172.9 4.4 reshape.285
  177.3 4.2 all-to-all-start.3
  181.5 17.6 %all-to-all-done.3 = bf16[4,2,65536]{2,1,0:T(2,128)(2,1)} async-done(((bf16[4,2,65536]{2,1,0:T(2,128)(2,1)}), bf16[4,2,65536]{2,1,0:T(2,128)(2,1)}, u32[]{:S(2)}, u32[]{:S(2)}) %all-to-all-start.3) | async-done | bytes 1048608 | tf_op jit(solution)/shard_map/all_to_all | solution.py:115
  199.2 4.3 reshape.286
  203.5 4.0 copy.127
  211.7 9.3 fusion.83
  221.0 9.2 fusion.84
  230.3 13.0 multiply_convert_fusion
  243.3 7.5 fusion.85
  250.9 4.1 multiply_reduce_fusion.4
  263.2 14.4 all-to-all-done.4
  286.0 223.1 %while.46 = (s32[]{:T(128)}, f32[4,273,64]{1,2,0:T(8,128)S(1)}, f32[4,273]{1,0:T(4,128)S(1)}, bf16[4,4,512,16]{2,3,1,0:T(8,128)(2,1)}, bf16[4,4,512,16]{2,3,1,0:...) while((s32[]{:T(128)}, f32[4,273,64]{1,2,0:T(8,128)S(1)}, ...), condition=%wide.region_14.15_spmd.clone, body=%wide.region_7.14_spmd.clone.sunk | while | flops 5250492416 | bytes 107629728 | solution.py:81
  292.5 4.6 fusion.197
  307.0 4.2 fusion.200
  316.2 5.3 fusion.204
  327.5 4.0 fusion.206
  331.6 5.5 fusion.207
  346.1 4.6 fusion.197
  360.6 4.2 fusion.200
  369.8 5.4 fusion.204
  381.3 3.8 fusion.206
  385.1 5.5 fusion.207
  399.7 4.6 fusion.197
  414.4 4.2 fusion.200
  423.6 5.2 fusion.204
  434.9 3.8 fusion.206
  438.7 5.5 fusion.207
  453.4 4.6 fusion.197
  467.9 4.2 fusion.200
  477.2 5.3 fusion.204
  488.5 4.0 fusion.206
  492.5 5.5 fusion.207
  513.9 9.1 all_to_all.96
  532.0 9.5 all_to_all.97
  546.7 4.4 fusion.67
  559.0 19.5 %all_to_all.98 = bf16[4,2,65536]{2,1,0:T(2,128)(2,1)} all-to-all(bf16[4,2,65536]{2,1,0:T(2,128)(2,1)} %reshape.287), channel_id=1, replica_groups=mesh['dp'=8,'seq'=4] {'seq'}, dimensions={0} | all-to-all | bytes 2097152 | tf_op jit(solution)/shard_map/all_to_all | solution.py:167
  583.9 4.7 fusion.72
  589.8 7.8 fusion.88
  597.7 8.0 fusion.89
  607.0 7.6 convolution_bitcast_fusion
  614.6 11.9 copy.167
  628.1 7.8 add_convert_fusion
  640.8 40.2 %all-reduce.2 = (f32[1024]{0:T(1024)S(1)}, f32[1024]{0:T(1024)S(1)}) all-reduce(f32[1024]{0:T(1024)S(1)} %get-tuple-element.658, f32[1024]{0:T(1024)S(1)} %copy-done.35), channel_id=2, replica_groups=mesh['dp'=8,'seq'=4] {'dp','seq'}, use_global_device_ids=true, to_apply=%region_17.18.clone | all-reduce | flops 2048 | bytes 16384
  682.2 4.2 fusion.64
  686.4 110.7 %reduce-scatter.12.cloned.1.call-done = f32[32,256]{1,0:T(8,128)} async-done(((f32[1024,256]{1,0:T(8,128)}), f32[32,256]{1,0:T(8,128)}) %reduce-scatter.12.cloned.1.call-update) | async-done | bytes 32784 | tf_op jit(solution)/shard_map/reduce_scatter | solution.py:186
  797.2 139.4 %reduce-scatter.16.cloned.1.call-done = f32[32,1024]{1,0:T(8,128)} async-done(((f32[1024,1024]{1,0:T(8,128)}), f32[32,1024]{1,0:T(8,128)}) %reduce-scatter.16.cloned.1.call-update) | async-done | bytes 131088 | tf_op jit(solution)/shard_map/reduce_scatter | solution.py:155
  936.6 139.6 %reduce-scatter.14.cloned.1.call-done = f32[32,1024]{1,0:T(8,128)} async-done(((f32[1024,1024]{1,0:T(8,128)}), f32[32,1024]{1,0:T(8,128)}) %reduce-scatter.14.cloned.1.call-update) | async-done | bytes 131088 | tf_op jit(solution)/shard_map/reduce_scatter | solution.py:187
  1076.2 153.8 %reduce-scatter.18.cloned.1.call-done = f32[32,2752]{1,0:T(8,128)} async-done(((f32[1024,2752]{1,0:T(8,128)}), f32[32,2752]{1,0:T(8,128)}) %reduce-scatter.18.cloned.1.call-update) | async-done | bytes 352272 | tf_op jit(solution)/shard_map/reduce_scatter | solution.py:152
  1229.9 153.7 %reduce-scatter.20.cloned.1.call-done = f32[32,2752]{1,0:T(8,128)} async-done(((f32[1024,2752]{1,0:T(8,128)}), f32[32,2752]{1,0:T(8,128)}) %reduce-scatter.20.cloned.1.call-update) | async-done | bytes 352272 | tf_op jit(solution)/shard_map/reduce_scatter | solution.py:153
  1383.6 153.6 %reduce-scatter.22.cloned.1.call-done = f32[32,2752]{1,0:T(8,128)} async-done(((f32[1024,2752]{1,0:T(8,128)}), f32[32,2752]{1,0:T(8,128)}) %reduce-scatter.22.cloned.1.call-update) | async-done | bytes 352272
  (388 shorter events, 277.2 us)
Async XLA Ops:
  7.2 200.3 %copy-start = (bf16[1024,1024]{1,0:T(8,128)(2,1)S(1)}, bf16[1024,1024]{1,0:T(8,128)(2,1)}, u32[]{:S(2)}) copy-start(bf16[1024,1024]{1,0:T(8,128)(2,1)} %param.20) | copy-start | bytes 6291460
  7.2 10.6 copy-start.8
  7.2 204.5 %all-gather.4.cloned.1.call-start = ((), (), s32[]{:S(2)}) async-start(), calls=%async_computation.15 | async-start | bytes 5947392 | tf_op jit(solution)/shard_map/all_gather | solution.py:122
  7.9 213.1 %all-gather.6.cloned.1.call-start = ((), (), s32[]{:S(2)}) async-start(), calls=%async_computation.16 | async-start | bytes 5947392 | tf_op jit(solution)/shard_map/all_gather | solution.py:123
  9.4 18.5 %copy-start.29 = (f32[1024]{0:T(1024)}, f32[1024]{0:T(1024)S(1)}, u32[]{:S(2)}) copy-start(f32[1024]{0:T(1024)S(1)} %convert_element_type.270) | copy-start | bytes 12292
  10.9 2.7 copy-start.33
  10.9 17.0 %copy-start.31 = (f32[512]{0:T(512)}, f32[512]{0:T(512)S(1)}, u32[]{:S(2)}) copy-start(f32[512]{0:T(512)S(1)} %fusion.70) | copy-start | bytes 6148
  13.6 10.2 all-to-all-start
  23.8 7.9 copy-start.15
  23.8 10.2 all-to-all-start.2
  34.1 23.6 %all-to-all-start.1 = ((bf16[512,16,64]{0,2,1:T(8,128)(2,1)}), bf16[512,16,64]{0,2,1:T(8,128)(2,1)}, u32[]{:S(2)}, u32[]{:S(2)}) async-start(bf16[512,16,64]{0,2,1:T(8,128)(2,1)} %bitcast.315), calls=%async_computation.1 | async-start | bytes 2097152 | tf_op jit(solution)/shard_map/all_to_all | solution.py:107
  38.3 192.0 %all-gather.8.cloned.1.call-start = ((), (), s32[]{:S(2)}) async-start(), calls=%async_computation.17 | async-start | bytes 5947392 | tf_op jit(solution)/shard_map/all_gather | solution.py:124
  75.4 5.6 copy-start.2
  87.0 2.1 copy-start.12
  91.7 2.9 copy-start.13
  96.4 5.6 copy-start.2
  108.0 2.1 copy-start.12
  112.7 2.9 copy-start.13
  117.4 5.6 copy-start.2
  129.0 2.1 copy-start.12
  133.6 2.9 copy-start.13
  138.3 5.6 copy-start.2
  149.9 2.1 copy-start.12
  154.6 2.9 copy-start.13
  172.9 8.6 copy-start.36
  177.3 21.9 %all-to-all-start.3 = ((bf16[4,2,65536]{2,1,0:T(2,128)(2,1)}), bf16[4,2,65536]{2,1,0:T(2,128)(2,1)}, u32[]{:S(2)}, u32[]{:S(2)}) async-start(bf16[4,2,65536]{2,1,0:T(2,128)(2,1)} %reshape.285), calls=%async_computation.3 | async-start | bytes 2097152 | tf_op jit(solution)/shard_map/all_to_all | solution.py:115
  211.7 9.4 copy-start.16
  243.3 7.6 copy-start.40
  243.3 7.6 copy-start.39
  243.3 7.6 copy-start.4
  243.3 7.6 copy-start.37
  250.9 4.1 copy-start.23
  259.6 18.0 %all-to-all-start.4 = ((bf16[512,16,64]{0,2,1:T(8,128)(2,1)}), bf16[512,16,64]{0,2,1:T(8,128)(2,1)S(1)}, u32[]{:S(2)}, u32[]{:S(2)}) async-start(bf16[512,16,64]{0,2,1:T(8,128)(2,1)} %bitcast.21), calls=%async_computation.4 | async-start | bytes 2097152 | tf_op jit(solution)/shard_map/all_to_all | solution.py:158
  263.1 423.4 %reduce-scatter.10.cloned.1.call-start = ((), (), s32[]{:S(2)}) async-start(), calls=%async_computation.18 | async-start | bytes 1081344 | tf_op jit(solution)/shard_map/reduce_scatter | solution.py:185
  325.2 2.3 copy-start.20
  327.5 4.1 copy-start.19
  331.6 5.6 copy-start.21
  379.0 2.3 copy-start.20
  381.3 3.8 copy-start.19
  385.1 5.6 copy-start.21
  432.5 2.3 copy-start.20
  434.9 3.9 copy-start.19
  438.7 5.6 copy-start.21
  486.1 2.3 copy-start.20
  488.4 4.1 copy-start.19
  492.5 5.6 copy-start.21
  509.1 4.7 copy-start.10
  523.0 3.7 copy-start.9
  523.0 3.7 copy-start.30
  523.0 3.7 copy-start.32
  526.6 1.7 copy-start.25
  526.6 1.7 copy-start.22
  528.3 268.9 %reduce-scatter.12.cloned.1.call-start = ((), (), s32[]{:S(2)}) async-start(), calls=%async_computation.19 | async-start | bytes 1081344 | tf_op jit(solution)/shard_map/reduce_scatter | solution.py:186
  546.6 390.0 %reduce-scatter.16.cloned.1.call-start = ((), (), s32[]{:S(2)}) async-start(), calls=%async_computation.21 | async-start | bytes 4325376 | tf_op jit(solution)/shard_map/reduce_scatter | solution.py:155
  551.1 525.1 %reduce-scatter.14.cloned.1.call-start = ((), (), s32[]{:S(2)}) async-start(), calls=%async_computation.20 | async-start | bytes 4325376 | tf_op jit(solution)/shard_map/reduce_scatter | solution.py:187
  588.6 641.3 %reduce-scatter.18.cloned.1.call-start = ((), (), s32[]{:S(2)}) async-start(), calls=%async_computation.22 | async-start | bytes 11894784 | tf_op jit(solution)/shard_map/reduce_scatter | solution.py:152
  597.7 785.9 %reduce-scatter.20.cloned.1.call-start = ((), (), s32[]{:S(2)}) async-start(), calls=%async_computation.23 | async-start | bytes 11894784 | tf_op jit(solution)/shard_map/reduce_scatter | solution.py:153
  605.8 931.4 %reduce-scatter.22.cloned.1.call-start = ((), (), s32[]{:S(2)}) async-start(), calls=%async_computation.24 | async-start | bytes 11894784
  628.1 7.8 copy-start.26
  628.1 7.8 copy-start.28
  628.1 8.3 copy-start.38
  638.5 2.4 copy-start.35
  638.5 43.7 %copy-start.34 = (f32[512]{0:T(512)S(1)}, f32[512]{0:T(512)}, u32[]{:S(2)}) copy-start(f32[512]{0:T(512)} %copy-done.33) | copy-start | bytes 6148
  682.2 855.0 %copy-start.1 = (bf16[1024,1024]{1,0:T(8,128)(2,1)S(1)}, bf16[1024,1024]{1,0:T(8,128)(2,1)}, u32[]{:S(2)}) copy-start(bf16[1024,1024]{1,0:T(8,128)(2,1)} %param.20) | copy-start | bytes 6291460
  (13 other events, 17.3 us)
Sparse Core Ops, SparseCore 0:
  10.9 73.1 all-gather.3
  86.9 66.1 all-gather.5
  156.0 68.6 all-gather.7
  528.4 135.1 reduce-scatter.9
  666.4 130.7 reduce-scatter.11
  799.9 136.6 reduce-scatter.15
  939.5 136.6 reduce-scatter.13
  1079.1 150.8 reduce-scatter.17
  1232.8 150.7 reduce-scatter.19
  1386.3 150.7 reduce-scatter.21
where the time goes:
time: 1550 us; the launch traced here: 1540 us
  waiting for transfers between devices  894 us (58%)
  matrix products  339 us (22%)
  local copies, waits for them, and re-layouts  130 us (8%)
  blocking collectives  78.2 us (5%)
  other arithmetic  46.9 us (3%)
  starting transfers between devices  20.7 us (1%)
  loops' own time  20.5 us (1%)
    dot_general x72, matrix products, product(): jnp.dot(left, right, precision=lax.Precision.HIGHEST, preferred_element_t...  235 us
    unnamed x11, waiting for transfers between devices  156 us
    reduce_scatter x1, waiting for transfers between devices, shards(): lax.psum_scatter(gate_grad, ('dp', 'seq'), scatter_dimension=0, tiled=True)  154 us
    reduce_scatter x1, waiting for transfers between devices, shards(): lax.psum_scatter(up_grad, ('dp', 'seq'), scatter_dimension=0, tiled=True)  154 us
    reduce_scatter x1, waiting for transfers between devices, shards(): lax.psum_scatter(value_grad, ('dp', 'seq'), scatter_dimension=0, tiled=True)  140 us
    reduce_scatter x1, waiting for transfers between devices, shards(): lax.psum_scatter(output_grad, ('dp', 'seq'), scatter_dimension=0, tiled=T...  139 us
    reduce_scatter x1, waiting for transfers between devices, shards(): lax.psum_scatter(key_grad, ('dp', 'seq'), scatter_dimension=0, tiled=True)  111 us
    unnamed x82, local copies, waits for them, and re-layouts  52.9 us
  transfers between devices with their start and end apart: 15, of which 10 were waited for; matrix products, arithmetic and copies ran while one was open for 16% of the time, Pallas kernels for 0%

commit v1 on v0

v1 whole, which is shorter than its diff:
```python
import math

import jax
import jax.numpy as jnp
import numpy as np
from jax import lax
from jax.experimental import pallas as pl
from jax.experimental.pallas import tpu as pltpu
from jax.sharding import PartitionSpec as P

KD = 16
VD = 64
LANES = 128
FEATS = 256
EPS = 1e-05
QUAD = 1.0 / (4.0 * math.sqrt(2.0))
F32 = jnp.float32
BF16 = jnp.bfloat16
VMEM_LIMIT = 58 << 20


def feature_tables():
    pick_a = np.zeros((LANES, FEATS), np.float32)
    pick_b = np.zeros((LANES, FEATS), np.float32)
    rows = np.zeros((8, FEATS), np.float32)
    spot = 0
    for a in range(KD):
        for b in range(a, KD):
            pick_a[a::KD, spot] = 1.0
            pick_b[b::KD, spot] = 1.0
            rows[2, spot] = QUAD
            rows[3, spot] = 1.0 if a == b else 2.0
            spot += 1
    for a in range(KD):
        pick_a[a::KD, spot] = 1.0
        rows[1, spot] = 1.0
        rows[2, spot] = 0.5
        rows[3, spot] = 1.0
        spot += 1
    rows[0:4, spot] = 1.0
    return jnp.asarray(pick_a, BF16), jnp.asarray(pick_b, BF16), jnp.asarray(rows)


def dot(left, right):
    return jnp.dot(left, right, preferred_element_type=F32)


def dot_nt(left, right):
    return lax.dot_general(left, right, (((1,), (1,)), ((), ())), preferred_element_type=F32)


def dot_tn(left, right):
    return lax.dot_general(left, right, (((0,), (0,)), ((), ())), preferred_element_type=F32)


def tile_at(index):
    return pl.ds(pl.multiple_of(index * LANES, LANES), LANES)


def head_lanes(rows, spot):
    return lax.broadcasted_iota(jnp.int32, (rows, LANES), 1) // KD == spot


def half_lanes(rows, half):
    return lax.broadcasted_iota(jnp.int32, (rows, LANES), 1) // VD == half


def halves_of(masked, pick_a, pick_b, rows):
    first = dot(masked, pick_a) + rows[0:1, :]
    second = dot(masked, pick_b) + rows[1:2, :]
    return first, second


def features_of(masked, pick_a, pick_b, rows):
    first, second = halves_of(masked, pick_a, pick_b, rows)
    return (first * second * rows[2:3, :]).astype(BF16)


def only(mask, value):
    return jnp.where(mask, value, jnp.zeros_like(value))


def project_body(tok, gain, wq, wk, wv, normed, query, keys, values):
    x = tok[...].astype(F32)
    scale = lax.rsqrt(jnp.mean(x * x, axis=-1, keepdims=True) + EPS)
    normed[...] = (x * scale * gain[...]).astype(BF16)
    query[...] = dot(normed[...], wq[...]).astype(BF16)
    keys[...] = dot(normed[...], wk[...]).astype(BF16)
    values[...] = dot(normed[...], wv[...]).astype(BF16)


def state_body(keys, values, pick_a, pick_b, rows, state, total):
    pairs = values.shape[1] // LANES
    count = keys.shape[0]

    def step(pair, carry):
        turned = values[:, tile_at(pair)].T
        for half in range(2):
            head = pair * 2 + half
            masked = only(head_lanes(count, head % 8), keys[:, tile_at(head // 8)])
            feat = features_of(masked, pick_a[...], pick_b[...], rows[...])
            sums = dot(turned[half * VD : (half + 1) * VD, :], feat)
            state[head] = (sums * rows[3:4, :]).astype(BF16)
            total[head] = jnp.sum(feat.astype(F32), axis=0, keepdims=True) * rows[3:4, :]
        return carry

    lax.fori_loop(0, pairs, step, 0)


def causal(rows, columns, row_start, column_start):
    row = lax.broadcasted_iota(jnp.int32, (rows, columns), 0) + row_start
    column = lax.broadcasted_iota(jnp.int32, (rows, columns), 1) + column_start
    return row >= column


def attend_body(query, keys, values, pick_a, pick_b, rows, state, total, mixed, inverse, block=256):
    pairs = values.shape[1] // LANES
    count = keys.shape[0]

    def step(pair, carry):
        vals = values[:, tile_at(pair)]
        for start in range(0, count, block):
            stop = start + block
            numer = None
            for half in range(2):
                head = pair * 2 + half
                masked = only(head_lanes(block, head % 8), query[start:stop, tile_at(head // 8)])
                score = dot_nt(masked, keys[0:stop, tile_at(head // 8)]) * 0.25
                weight = 1.0 + score + 0.5 * score * score
                weight = jnp.where(causal(block, stop, start, 0), weight, 0.0)
                feat = features_of(masked, pick_a[...], pick_b[...], rows[...])
                inter = feat.astype(F32) * total[head]
                denom = jnp.sum(weight, axis=1, keepdims=True) + jnp.sum(
                    inter, axis=1, keepdims=True
                )
                across = dot_nt(feat, state[head])
                both = dot(weight.astype(BF16), vals[0:stop, :])
                across = jnp.concatenate([across, across], axis=1)
                whole = (both + across) / denom
                flip = jnp.broadcast_to(1.0 / denom, (block, LANES))
                if half == 0:
                    numer, invs = whole, flip
                else:
                    mask = half_lanes(block, 0)
                    numer = jnp.where(mask, numer, whole)
                    invs = jnp.where(mask, invs, flip)
            mixed[start:stop, tile_at(pair)] = numer.astype(BF16)
            inverse[start:stop, tile_at(pair)] = invs
        return carry

    lax.fori_loop(0, pairs, step, 0)


def back_state_body(query, mixed, inverse, d_mixed, pick_a, pick_b, rows, d_state, d_total):
    pairs = mixed.shape[1] // LANES
    count = query.shape[0]

    def step(pair, carry):
        spot = tile_at(pair)
        d_numer = d_mixed[:, spot].astype(F32) * inverse[:, spot]
        lost = d_numer * mixed[:, spot].astype(F32)
        turned = d_numer.astype(BF16).T
        for half in range(2):
            head = pair * 2 + half
            masked = only(head_lanes(count, head % 8), query[:, tile_at(head // 8)])
            feat = features_of(masked, pick_a[...], pick_b[...], rows[...])
            d_denom = -jnp.sum(only(half_lanes(count, half), lost), axis=1, keepdims=True)
            sums = dot(turned[half * VD : (half + 1) * VD, :], feat)
            d_state[head] = (sums * rows[3:4, :]).astype(BF16)
            d_total[head] = (
                jnp.sum(feat.astype(F32) * d_denom, axis=0, keepdims=True) * rows[3:4, :]
            )
        return carry

    lax.fori_loop(0, pairs, step, 0)


def feature_back(d_feat, first, second, pick_a, pick_b, rows):
    scaled = d_feat * rows[2:3, :]
    return dot_nt((scaled * second).astype(BF16), pick_a) + dot_nt(
        (scaled * first).astype(BF16), pick_b
    )


def attend_back_body(
    query,
    keys,
    values,
    mixed,
    inverse,
    d_mixed,
    pick_a,
    pick_b,
    rows,
    state,
    total,
    d_state,
    d_total,
    d_query,
    d_keys,
    d_values,
    q_sum,
    k_sum,
    v_sum,
    block=256,
):
    pairs = values.shape[1] // LANES
    count = keys.shape[0]
    q_sum[...] = jnp.zeros_like(q_sum)
    k_sum[...] = jnp.zeros_like(k_sum)

    def step(pair, carry):
        spot = tile_at(pair)
        d_numer = d_mixed[:, spot].astype(F32) * inverse[:, spot]
        lost = d_numer * mixed[:, spot].astype(F32)
        d_low = d_numer.astype(BF16)
        turned = pltpu.roll(lost, VD, 1)
        vals = values[:, spot]
        for half in range(2):
            head = pair * 2 + half
            place = tile_at(head // 8)
            mine = half_lanes(count, half)
            lanes = head_lanes(count, head % 8)
            d_denom = -jnp.sum(only(mine, lost), axis=1, keepdims=True)
            d_wide = jnp.where(mine, d_numer, -turned).astype(BF16)
            v_wide = jnp.where(mine, vals, jnp.ones_like(vals))
            q_mask = only(lanes, query[:, place])
            k_mask = only(lanes, keys[:, place])
            grads_q, grads_k, grads_v = [], [], []
            for start in range(0, count, block):
                stop = start + block
                score = dot_nt(q_mask[start:stop], k_mask[0:stop]) * 0.25
                d_weight = dot_nt(d_wide[start:stop], v_wide[0:stop])
                d_score = only(causal(block, stop, start, 0), d_weight * (1.0 + score))
                grads_q.append(dot(d_score.astype(BF16), k_mask[0:stop]))
                rest = count - start
                score = dot_nt(k_mask[start:stop], q_mask[start:count]) * 0.25
                mask = causal(rest, block, 0, 0)
                mask = (
                    lax.broadcasted_iota(jnp.int32, (block, rest), 0)
                    <= lax.broadcasted_iota(jnp.int32, (block, rest), 1)
                )
                weight = only(mask, 1.0 + score + 0.5 * score * score)
                d_weight = dot_nt(v_wide[start:stop], d_wide[start:count])
                d_score = only(mask, d_weight * (1.0 + score))
                grads_k.append(dot(d_score.astype(BF16), q_mask[start:count]))
                grads_v.append(dot(weight.astype(BF16), d_low[start:count]))
            first, second = halves_of(q_mask, pick_a[...], pick_b[...], rows[...])
            d_feat = dot(d_low[:, half * VD : (half + 1) * VD], state[head]) + d_denom * total[head]
            inter_q = feature_back(d_feat, first, second, pick_a[...], pick_b[...], rows[...])
            first, second = halves_of(k_mask, pick_a[...], pick_b[...], rows[...])
            feat = (first * second * rows[2:3, :]).astype(BF16)
            d_feat = dot(vals[:, half * VD : (half + 1) * VD], d_state[head]) + d_total[head]
            inter_k = feature_back(d_feat, first, second, pick_a[...], pick_b[...], rows[...])
            inter_v = dot_nt(feat, d_state[head])
            inter_v = jnp.concatenate([inter_v, inter_v], axis=1)
            whole_v = jnp.concatenate(grads_v, axis=0) + inter_v
            v_sum[...] = whole_v if half == 0 else jnp.where(mine, whole_v, v_sum[...])
            q_sum[:, place] += jnp.concatenate(grads_q, axis=0) * 0.25 + only(lanes, inter_q)
            k_sum[:, place] += jnp.concatenate(grads_k, axis=0) * 0.25 + only(lanes, inter_k)
        d_values[:, spot] = v_sum[...].astype(BF16)
        return carry

    lax.fori_loop(0, pairs, step, 0)
    d_query[...] = q_sum[...].astype(BF16)
    d_keys[...] = k_sum[...].astype(BF16)


def call(body, shapes, *operands, scratch=()):
    return pl.pallas_call(
        body,
        out_shape=[jax.ShapeDtypeStruct(shape, kind) for shape, kind in shapes],
        scratch_shapes=list(scratch),
        compiler_params=pltpu.CompilerParams(vmem_limit_bytes=VMEM_LIMIT),
    )(*operands)


def rms_norm(inputs, gain):
    return inputs * lax.rsqrt(jnp.mean(inputs * inputs, axis=-1, keepdims=True) + EPS) * gain


def gated(gate_in, up_in):
    return jax.nn.silu(gate_in) * up_in


def before(parts, axis, reverse=False):
    place = lax.axis_index(axis)
    order = jnp.arange(parts.shape[0])
    chosen = order > place if reverse else order < place
    chosen = chosen.reshape((-1,) + (1,) * (parts.ndim - 1))
    return jnp.sum(jnp.where(chosen, parts.astype(F32), 0.0), axis=0)


def shards(
    tokens, attn_gain, w_query, w_key, w_value, w_output, mlp_gain, w_gate, w_up, w_down, out_grad
):
    count, width = tokens.shape
    heads = w_query.shape[1] // KD
    all_values = heads * VD
    tables = feature_tables()
    inputs = tokens.astype(F32)
    gain = attn_gain.astype(F32).reshape(1, width)
    gate_full, up_full, down_full = (
        lax.all_gather(w, ("dp", "seq"), axis=0, tiled=True) for w in (w_gate, w_up, w_down)
    )
    normed, query, keys, values = call(
        project_body,
        [
            ((count, width), BF16),
            ((count, heads * KD), BF16),
            ((count, heads * KD), BF16),
            ((count, all_values), BF16),
        ],
        tokens,
        gain,
        w_query,
        w_key,
        w_value,
    )
    state_shapes = [((heads, VD, FEATS), BF16), ((heads, 1, FEATS), F32)]
    state, total = call(state_body, state_shapes, keys, values, *tables)
    state = before(lax.all_gather(state, "seq"), "seq").astype(BF16)
    total = before(lax.all_gather(total, "seq"), "seq")
    mixed, inverse = call(
        attend_body,
        [((count, all_values), BF16), ((count, all_values), F32)],
        query,
        keys,
        values,
        *tables,
        state,
        total,
    )
    middle = inputs + dot(mixed, w_output)
    normed_mlp, second_back = jax.vjp(rms_norm, middle, mlp_gain.astype(F32))
    mlp_low = normed_mlp.astype(BF16)
    gate = dot(mlp_low, gate_full)
    upward = dot(mlp_low, up_full)
    hidden_val, gated_back = jax.vjp(gated, gate, upward)
    hidden = hidden_val.astype(BF16)
    layer_out = (middle + dot_nt(hidden, down_full)).astype(BF16)
    d_hidden = dot(out_grad, down_full)
    down_grad = dot_tn(out_grad, hidden).astype(BF16)
    d_gate_f, d_up_f = gated_back(d_hidden)
    d_gate = d_gate_f.astype(BF16)
    d_up = d_up_f.astype(BF16)
    gate_grad = dot_tn(mlp_low, d_gate).astype(BF16)
    up_grad = dot_tn(mlp_low, d_up).astype(BF16)
    d_normed_mlp = dot_nt(d_gate, gate_full) + dot_nt(d_up, up_full)
    d_middle_norm, mlp_gain_part = second_back(d_normed_mlp)
    d_middle = out_grad.astype(F32) + d_middle_norm
    d_branch = d_middle.astype(BF16)
    output_grad = dot_tn(mixed, d_branch).astype(BF16)
    d_mixed = dot_nt(d_branch, w_output).astype(BF16)
    d_state, d_total = call(
        back_state_body, state_shapes, query, mixed, inverse, d_mixed, *tables
    )
    d_state = before(lax.all_gather(d_state, "seq"), "seq", True).astype(BF16)
    d_total = before(lax.all_gather(d_total, "seq"), "seq", True)
    d_query, d_keys, d_values = call(
        attend_back_body,
        [
            ((count, heads * KD), BF16),
            ((count, heads * KD), BF16),
            ((count, all_values), BF16),
        ],
        query,
        keys,
        values,
        mixed,
        inverse,
        d_mixed,
        *tables,
        state,
        total,
        d_state,
        d_total,
        scratch=[
            pltpu.VMEM((count, heads * KD), F32),
            pltpu.VMEM((count, heads * KD), F32),
            pltpu.VMEM((count, LANES), F32),
        ],
    )
    d_normed = dot_nt(d_query, w_query) + dot_nt(d_keys, w_key) + dot_nt(d_values, w_value)
    query_grad = dot_tn(normed, d_query).astype(BF16)
    key_grad = dot_tn(normed, d_keys).astype(BF16)
    value_grad = dot_tn(normed, d_values).astype(BF16)
    _, first_back = jax.vjp(rms_norm, inputs, attn_gain.astype(F32))
    d_inputs_norm, attn_gain_part = first_back(d_normed)
    tokens_grad = d_middle + d_inputs_norm
    parts = [query_grad, key_grad, value_grad, output_grad, gate_grad, up_grad, down_grad]
    joined = lax.psum_scatter(
        jnp.concatenate(parts, axis=1), ("dp", "seq"), scatter_dimension=0, tiled=True
    ).astype(F32)
    edges = np.cumsum([part.shape[1] for part in parts])[:-1]
    query_grad, key_grad, value_grad, output_grad, gate_grad, up_grad, down_grad = jnp.split(
        joined, edges, axis=1
    )
    gains = lax.psum_scatter(
        jnp.stack([attn_gain_part, mlp_gain_part], axis=1),
        ("dp", "seq"),
        scatter_dimension=0,
        tiled=True,
    )
    return (
        layer_out,
        tokens_grad,
        gains[:, 0],
        query_grad,
        key_grad,
        value_grad,
        output_grad,
        gains[:, 1],
        gate_grad,
        up_grad,
        down_grad,
    )


def solution(mesh):
    rows = P(("dp", "seq"), None)
    in_specs = (rows, P(), P(), P(), P(), P(), P(), rows, rows, rows, rows)
    out_specs = (
        rows,
        rows,
        P(("dp", "seq")),
        rows,
        rows,
        rows,
        rows,
        P(("dp", "seq")),
        rows,
        rows,
        rows,
    )
    return jax.shard_map(
        shards, mesh=mesh, in_specs=in_specs, out_specs=out_specs, check_vma=False
    )
```

time: 1550 us -> 767 us (0.49)
  waiting for transfers between devices: 894 us -> 508 us
  matrix products: 339 us -> 84.6 us
  local copies, waits for them, and re-layouts: 130 us -> 55 us
  Pallas kernels: 0 us -> 73.5 us
  blocking collectives: 78.2 us -> 12.6 us
  other arithmetic: 46.9 us -> 11.8 us
  loops' own time: 20.5 us -> 0 us
  starting transfers between devices: 20.7 us -> 0.28 us
    reduce_scatter x6 -> x0, waiting for transfers between devices: 697 us -> none  [the longest x1 154 us: shards(): lax.psum_scatter(gate_grad, ('dp', 'seq'), scatter_dimension=0, tiled=True)]
    dot_general x93 -> x18, matrix products: 339 us -> 84.6 us  [the longest x4 33.4 us: dot(): return jnp.dot(left, right, preferred_element_type=F32)]
    all_gather x3 -> x5, waiting for transfers between devices: 0.02 us -> 199 us  [the longest x3 169 us: shards(): lax.all_gather(w, ('dp', 'seq'), axis=0, tiled=True)]
    unnamed x11 -> x9, waiting for transfers between devices: 156 us -> 309 us
    pallas_call x0 -> x5, Pallas kernels: none -> 73.5 us  [call(): pl.pallas_call(body, out_shape=[jax.ShapeDtypeStruct(shape, kind) for sha...]
    all_to_all x5 -> x0, waiting for transfers between devices: 41.4 us -> none  [the longest x1 17.6 us: shards(): lax.all_to_all(mixed.astype(jnp.bfloat16), 'seq', split_axis=0, concat_ax...]
    unnamed x1 -> x0, blocking collectives: 40.2 us -> none
    all_to_all x3 -> x0, blocking collectives: 38 us -> none  [the longest x1 19.5 us: shards(): lax.all_to_all(d_values_h.astype(jnp.bfloat16), 'seq', split_axis=0, conc...]
  transfers between devices with their start and end apart: 15 -> 7, of which waited for: 10 -> 7; matrix products, arithmetic and copies ran while one was open for 16% -> 11% of each run, Pallas kernels for 0% -> 2%
where the time goes in v1:
time: 767 us; the launch traced here: 761 us
  waiting for transfers between devices  508 us (66%)
  matrix products  84.6 us (11%)
  Pallas kernels  73.5 us (10%)
  local copies, waits for them, and re-layouts  55 us (7%)
  between operations  14.7 us (2%)
  blocking collectives  12.6 us (2%)
  other arithmetic  11.8 us (2%)
    unnamed x9, waiting for transfers between devices  309 us
    all_gather x3, waiting for transfers between devices, shards(): lax.all_gather(w, ('dp', 'seq'), axis=0, tiled=True)  169 us
    pallas_call x5, Pallas kernels, call(): pl.pallas_call(body, out_shape=[jax.ShapeDtypeStruct(shape, kind) for sha...  73.5 us
    unnamed x70, local copies, waits for them, and re-layouts  49 us
    dot_general x4, matrix products, dot(): return jnp.dot(left, right, preferred_element_type=F32)  33.4 us
    dot_general x7, matrix products, dot_nt(): lax.dot_general(left, right, (((1,), (1,)), ((), ())), preferred_element_...  28.4 us
    dot_general x7, matrix products, dot_tn(): lax.dot_general(left, right, (((0,), (0,)), ((), ())), preferred_element_...  22.8 us
    all_gather x1, waiting for transfers between devices, shards(): state = before(lax.all_gather(state, 'seq'), 'seq').astype(BF16)  15.6 us
  transfers between devices with their start and end apart: 7, of which 7 were waited for; matrix products, arithmetic and copies ran while one was open for 11% of the time, Pallas kernels for 2%

profile of v1, /device:TPU:0, one launch (start us, length us, event | category | flops | bytes accessed | tf_op | source)
XLA Modules:
  0.0 760.9 jit_solution(7692940010797798600)
XLA Ops:
  7.2 1.4 convert_element_type.74
  8.7 5.2 shard_map.221
  13.9 7.6 %shard_map.222 = (bf16[16,64,256]{2,1,0:T(8,128)(2,1)}, f32[16,1,256]{2,1,0:T(1,128)}) custom-call(bf16[512,256]{1,0:T(8,128)(2,1)} %get-tuple-element.25.keys, bf16[512,1024]{1,0:T(8,128)(2,1)} %get-tuple-element.26.values, bf16[128,256]{1,0:T(8,128)(2,1)} %constant.25.clone.pick_a, bf16[128,256]{1,0:T(8,128)(2,1)} %constant.26.clone.pick_b, ...), custom_call_target="tpu_custom_call" | custom-call | tf_op jit(solution)/shard_map/pallas_call | solution.py:270
  21.6 0.7 all-gather.12.cloned.1.call-update
  22.4 0.7 all-gather.10.cloned.1.call-update
  23.1 0.5 all-gather.14.cloned.1.call-update
  23.7 7.0 all-gather.1
  30.7 0.2 fusion.18
  30.8 0.6 reduce_sum.112.total
  31.4 15.6 %all-gather.16.cloned.1.call-done = bf16[64,64,256]{2,1,0:T(8,128)(2,1)} async-done(((bf16[16,64,256]{2,1,0:T(8,128)(2,1)}), bf16[64,64,256]{2,1,0:T(8,128)(2,1)}) %all-gather.16.cloned.1.call-update) | async-done | bytes 2097168 | tf_op jit(solution)/shard_map/all_gather | solution.py:322
  47.0 3.0 fusion.7.state
  50.0 14.5 %shard_map.223 = (bf16[512,1024]{1,0:T(8,128)(2,1)}, f32[512,1024]{1,0:T(8,128)}) custom-call(bf16[512,256]{1,0:T(8,128)(2,1)} %get-tuple-element.24.query, bf16[512,256]{1,0:T(8,128)(2,1)} %get-tuple-element.25.keys, bf16[512,1024]{1,0:T(8,128)(2,1)} %get-tuple-element.26.values, bf16[128,256]{1,0:T(8,128)(2,1)} %constant.25.clone.pick_a, ...), custom_call_target="tpu_custom_call" | custom-call | tf_op jit(solution)/shard_map/pallas_call | solution.py:270
  64.6 2.6 multiply_reduce_fusion.2
  67.1 1.3 copy-done.3
  68.4 1.2 multiply_convert_fusion.2
  69.6 47.5 %all-gather.12.cloned.1.call-done = bf16[1024,2752]{1,0:T(8,128)(2,1)} async-done(((bf16[32,2752]{1,0:T(8,128)(2,1)}), bf16[1024,2752]{1,0:T(8,128)(2,1)}) %all-gather.12.cloned.1.call-update) | async-done | bytes 5636112 | tf_op jit(solution)/shard_map/all_gather | solution.py:304
  117.1 8.6 %fusion.27 = f32[512,2752]{0,1:T(8,128)} fusion(bf16[512,1024]{1,0:T(8,128)(2,1)} %multiply_convert_fusion.2, bf16[1024,2752]{1,0:T(8,128)(2,1)} %all-gather.12.cloned.1.call-done), kind=kOutput, calls=%fused_computation.65 | convolution fusion | flops 2885681152 | bytes 12320768 | tf_op jit(solution)/shard_map/dot_general | solution.py:45
  125.7 60.6 %all-gather.10.cloned.1.call-done = bf16[1024,2752]{1,0:T(8,128)(2,1)} async-done(((bf16[32,2752]{1,0:T(8,128)(2,1)}), bf16[1024,2752]{1,0:T(8,128)(2,1)}) %all-gather.10.cloned.1.call-update) | async-done | bytes 5636112 | tf_op jit(solution)/shard_map/all_gather | solution.py:304
  186.3 8.5 %fusion.26 = f32[512,2752]{0,1:T(8,128)} fusion(bf16[512,1024]{1,0:T(8,128)(2,1)} %multiply_convert_fusion.2, bf16[1024,2752]{1,0:T(8,128)(2,1)} %all-gather.10.cloned.1.call-done), kind=kOutput, calls=%fused_computation.64 | convolution fusion | flops 2885681152 | bytes 12320768 | tf_op jit(solution)/shard_map/dot_general | solution.py:45
  194.7 60.5 %all-gather.14.cloned.1.call-done = bf16[1024,2752]{1,0:T(8,128)(2,1)} async-done(((bf16[32,2752]{1,0:T(8,128)(2,1)}), bf16[1024,2752]{1,0:T(8,128)(2,1)}) %all-gather.14.cloned.1.call-update) | async-done | bytes 5636112 | tf_op jit(solution)/shard_map/all_gather | solution.py:304
  255.2 13.7 %multiply_convert_fusion = (bf16[512,2752]{0,1:T(8,128)(2,1)S(1)}, bf16[512,2752]{0,1:T(8,128)(2,1)}, bf16[512,2752]{0,1:T(8,128)(2,1)}) fusion(f32[512,2752]{0,1:T(8,128)} %fusion.26, f32[512,2752]{0,1:T(8,128)} %fusion.27, bf16[512,1024]{1,0:T(8,128)(2,1)} %param.24, bf16[1024,2752]{1,0:T(8,128)(2,1)} %all-gather.14.cloned.1.call-done), kind=kOutput, calls=%fused_computation.10 | convolution fusion | flops 2908225536 | bytes 26411008 | tf_op jit(solution)/shard_map/dot_general | solution.py:45
  269.0 6.0 fusion.28
  275.1 5.8 multiply_reduce_fusion
  280.9 0.5 fusion.8
  281.5 2.3 convolution_convert_fusion.3.d_mixed
  283.8 9.1 %shard_map.224 = (bf16[16,64,256]{2,1,0:T(8,128)(2,1)}, f32[16,1,256]{2,1,0:T(1,128)}) custom-call(bf16[512,256]{1,0:T(8,128)(2,1)} %get-tuple-element.24.query, bf16[512,1024]{1,0:T(8,128)(2,1)} %get-tuple-element.29.mixed, f32[512,1024]{1,0:T(8,128)} %get-tuple-element.30.inverse, bf16[512,1024]{1,0:T(8,128)(2,1)} %convolution_convert_fusion.3.d_mixed, ...), custom_call_target="tpu_custom_call" | custom-call | tf_op jit(solution)/shard_map/pallas_call | solution.py:270
  293.0 0.3 fusion.10
  293.2 5.7 all-gather.3
  298.9 0.1 fusion.19
  299.1 0.6 reduce_sum.117.d_total
  299.7 14.9 %all-gather.18.cloned.1.call-done = bf16[64,64,256]{2,1,0:T(8,128)(2,1)} async-done(((bf16[16,64,256]{2,1,0:T(8,128)(2,1)}), bf16[64,64,256]{2,1,0:T(8,128)(2,1)}) %all-gather.18.cloned.1.call-update) | async-done | bytes 2097168 | tf_op jit(solution)/shard_map/all_gather | solution.py:358
  314.6 3.0 fusion.6.d_state
  317.7 37.0 %shard_map.225 = (bf16[512,256]{1,0:T(8,128)(2,1)}, bf16[512,256]{1,0:T(8,128)(2,1)}, bf16[512,1024]{1,0:T(8,128)(2,1)}) custom-call(bf16[512,256]{1,0:T(8,128)(2,1)} %get-tuple-element.24.query, bf16[512,256]{1,0:T(8,128)(2,1)} %get-tuple-element.25.keys, bf16[512,1024]{1,0:T(8,128)(2,1)} %get-tuple-element.26.values, ...), custom_call_target="tpu_custom_call" | custom-call | tf_op jit(solution)/shard_map/pallas_call | solution.py:270
  354.7 1.6 fusion.29
  356.4 2.6 fusion.30
  359.0 2.3 fusion.13
  361.3 1.0 copy.39
  362.4 1.3 fusion.15
  363.7 1.3 fusion.14
  365.0 2.7 convert_dynamic-update-slice_fusion.1
  367.7 2.7 convert_dynamic-update-slice_fusion
  370.4 5.1 fusion.1
  375.5 4.9 fusion
  380.4 4.9 bitcast_dynamic-update-slice_fusion
  385.3 27.2 %copy.41 = bf16[1024,10816]{1,0:T(8,128)(2,1)} copy(bf16[1024,10816]{0,1:T(8,128)(2,1)} %bitcast_dynamic-update-slice_fusion) | data formatting | bytes 44302336
  412.4 1.6 copy-done.5
  414.0 7.8 %add_convert_fusion = bf16[512,1024]{1,0:T(8,128)(2,1)} fusion(f32[512,1024]{1,0:T(8,128)S(1)} %copy-done.5, bf16[512,2752]{0,1:T(8,128)(2,1)} %get-tuple-element.65, bf16[1024,2752]{1,0:T(8,128)(2,1)} %all-gather.14.cloned.1.call-done), kind=kOutput, calls=%fused_computation.36 | convolution fusion | flops 2886729728 | bytes 11599872 | tf_op jit(solution)/shard_map/dot_general | solution.py:49
  421.9 1.9 fusion.9
  423.8 72.8 %reduce-scatter.7.cloned.1.call-done = f32[32,2]{1,0:T(8,128)} async-done(((f32[1024,2]{1,0:T(8,128)}), f32[32,2]{1,0:T(8,128)}) %reduce-scatter.7.cloned.1.call-update) | async-done | bytes 272
  496.5 0.9 fusion.25
  497.4 0.6 copy.44
  498.0 0.6 copy.43
  498.6 234.8 %reduce-scatter.9.cloned.1.call-done = bf16[32,10816]{1,0:T(8,128)(2,1)} async-done(((bf16[1024,10816]{1,0:T(8,128)(2,1)}), bf16[32,10816]{1,0:T(8,128)(2,1)}) %reduce-scatter.9.cloned.1.call-update) | async-done | bytes 692240
  733.3 3.2 copy.42
  736.6 0.7 fusion.24
  737.3 1.1 fusion.23
  738.4 2.1 fusion.22
  740.5 1.7 copy.33
  742.2 1.6 copy.32
  743.8 1.9 copy.35
  745.7 2.0 copy.34
  747.7 2.5 copy.38
  750.2 2.5 copy.37
  752.7 1.1 copy.36
  (75 shorter events, 0.6 us)
Async XLA Ops:
  7.2 57.4 %copy-start = (bf16[1024,1024]{1,0:T(8,128)(2,1)S(1)}, bf16[1024,1024]{1,0:T(8,128)(2,1)}, u32[]{:S(2)}) copy-start(bf16[1024,1024]{1,0:T(8,128)(2,1)} %param.19) | copy-start | bytes 6291460
  7.2 39.8 %all-gather.16.cloned.1.call-start = ((), (), s32[]{:S(2)}) async-start(), calls=%async_computation.5 | async-start | bytes 2621440 | tf_op jit(solution)/shard_map/all_gather | solution.py:322
  8.7 15.0 %copy-start.21 = (bf16[1024]{0:T(1024)(128)(2,1)S(1)}, bf16[1024]{0:T(1024)(128)(2,1)}, u32[]{:S(2)}) copy-start(bf16[1024]{0:T(1024)(128)(2,1)} %param.20) | copy-start | bytes 6148
  21.6 95.6 %all-gather.12.cloned.1.call-start = ((), (), s32[]{:S(2)}) async-start(), calls=%async_computation.3 | async-start | bytes 5947392 | tf_op jit(solution)/shard_map/all_gather | solution.py:304
  22.3 42.2 %copy-start.2 = (bf16[512,1024]{1,0:T(8,128)(2,1)S(1)}, bf16[512,1024]{1,0:T(8,128)(2,1)}, u32[]{:S(2)}) copy-start(bf16[512,1024]{1,0:T(8,128)(2,1)} %tok.1) | copy-start | bytes 3145732
  22.3 163.9 %all-gather.10.cloned.1.call-start = ((), (), s32[]{:S(2)}) async-start(), calls=%async_computation.2 | async-start | bytes 5947392 | tf_op jit(solution)/shard_map/all_gather | solution.py:304
  23.1 232.2 %all-gather.14.cloned.1.call-start = ((), (), s32[]{:S(2)}) async-start(), calls=%async_computation.4 | async-start | bytes 5947392 | tf_op jit(solution)/shard_map/all_gather | solution.py:304
  23.6 291.0 %all-gather.18.cloned.1.call-start = ((), (), s32[]{:S(2)}) async-start(), calls=%async_computation.6 | async-start | bytes 2621440 | tf_op jit(solution)/shard_map/all_gather | solution.py:358
  67.1 1.3 copy-start.3
  255.2 13.8 %copy-start.22 = (bf16[1024,2752]{1,0:T(8,128)(2,1)S(1)}, bf16[1024,2752]{1,0:T(8,128)(2,1)}, u32[]{:S(2)}) copy-start(bf16[1024,2752]{1,0:T(8,128)(2,1)} %all-gather.10.cloned.1.call-done) | copy-start | bytes 16908292
  269.0 6.1 copy-start.25
  269.0 6.1 copy-start.4
  275.1 5.8 copy-start.16
  281.5 2.3 copy-start.6
  292.9 203.6 %reduce-scatter.7.cloned.1.call-start = ((), (), s32[]{:S(2)}) async-start(), calls=%async_computation.7 | async-start | bytes 540672
  317.6 37.0 %copy-start.14 = (bf16[1024,256]{1,0:T(8,128)(2,1)S(1)}, bf16[1024,256]{1,0:T(8,128)(2,1)}, u32[]{:S(2)}) copy-start(bf16[1024,256]{1,0:T(8,128)(2,1)} %wq.1) | copy-start | bytes 1572868
  354.7 1.7 copy-start.13
  356.4 2.6 copy-start.12
  356.4 2.6 copy-start.18
  356.4 2.6 copy-start.20
  359.0 3.4 copy-start.19
  359.0 3.4 copy-start.23
  362.3 371.0 %reduce-scatter.9.cloned.1.call-start = ((), (), s32[]{:S(2)}) async-start(), calls=%async_computation.8 | async-start | bytes 22978560
  362.4 2.6 copy-start.24
  365.0 2.7 copy-start.7
  365.0 2.7 copy-start.11
  367.7 2.7 copy-start.15
  367.7 2.7 copy-start.28
  370.4 5.1 copy-start.26
  375.5 4.9 copy-start.17
  375.5 4.9 copy-start.27
  412.4 1.6 copy-start.5
  414.0 7.9 %copy-start.8 = (f32[512,1024]{1,0:T(8,128)S(1)}, f32[512,1024]{1,0:T(8,128)}, u32[]{:S(2)}) copy-start(f32[512,1024]{1,0:T(8,128)} %copy-done.6) | copy-start | bytes 6291460
  414.0 7.9 %copy-start.9 = (f32[512,1024]{1,0:T(8,128)S(1)}, f32[512,1024]{1,0:T(8,128)}, u32[]{:S(2)}) copy-start(f32[512,1024]{1,0:T(8,128)} %get-tuple-element.78) | copy-start | bytes 6291460
  740.5 12.2 %copy-start.10 = (f32[32,2752]{0,1:T(8,128)S(1)}, f32[32,2752]{0,1:T(8,128)}, u32[]{:S(2)}) copy-start(f32[32,2752]{0,1:T(8,128)} %get-tuple-element.68) | copy-start | bytes 1056772
  745.6 8.2 %copy-start.1 = (bf16[1024,1024]{1,0:T(8,128)(2,1)S(1)}, bf16[1024,1024]{1,0:T(8,128)(2,1)}, u32[]{:S(2)}) copy-start(bf16[1024,1024]{1,0:T(8,128)(2,1)} %param.19) | copy-start | bytes 6291460
Sparse Core Ops, SparseCore 0:
  21.7 25.2 all-gather.15
  49.8 67.2 all-gather.11
  120.0 66.2 all-gather.9
  188.9 66.2 all-gather.13
  293.0 21.5 all-gather.17
  362.5 134.0 reduce-scatter.6
  498.9 234.3 reduce-scatter.8

commit v2 on v1

--- a/solution.py
+++ b/solution.py
@@ -291,6 +291,356 @@
     return jnp.sum(jnp.where(chosen, parts.astype(F32), 0.0), axis=0)
 
 
+MESH_ID = pl.DeviceIdType.MESH
+
+
+class Place:
+    def __init__(self):
+        self.dp, self.seq = lax.axis_index("dp"), lax.axis_index("seq")
+        self.z, self.y = self.dp // 2, self.dp % 2
+        self.x, self.core = self.seq // 2, self.seq % 2
+
+    def at(self, z=None, y=None, x=None, core=None):
+        z = self.z if z is None else z
+        y = self.y if y is None else y
+        x = self.x if x is None else x
+        core = self.core if core is None else core
+        return (z * 2 + y, x * 2 + core)
+
+    def mate(self):
+        return self.at(core=1 - self.core)
+
+    def across(self, axis):
+        return self.at(y=1 - self.y) if axis == "y" else self.at(x=1 - self.x)
+
+    def own(self, axis):
+        return self.y if axis == "y" else self.x
+
+
+def remote(source, target, sent, landed, device):
+    return pltpu.make_async_remote_copy(
+        src_ref=source,
+        dst_ref=target,
+        send_sem=sent,
+        recv_sem=landed,
+        device_id=device,
+        device_id_type=MESH_ID,
+    )
+
+
+def enter(place):
+    barrier = pltpu.get_barrier_semaphore()
+    others = [place.mate(), place.across("x"), place.across("y")]
+    for other in (1, 2, 3):
+        others.append(place.at(z=jnp.bitwise_xor(place.z, other)))
+    for device in others:
+        pl.semaphore_signal(barrier, inc=1, device_id=device, device_id_type=MESH_ID)
+    pl.semaphore_wait(barrier, len(others))
+
+
+class Piece:
+    def __init__(self, source, target, low, rows, columns, first, middle):
+        self.source, self.target = source, target
+        self.low, self.rows, self.columns = low, rows, columns
+        self.first, self.third, self.middle = first, "x" if first == "y" else "y", middle
+
+    def scratch(self):
+        block = (self.rows, self.columns)
+        unit = (2,) + block if self.middle else block
+        last = block if self.middle else (4,) + block
+        return dict(
+            mine=pltpu.VMEM((4, 2, 2) + block, BF16),
+            mates=pltpu.VMEM((4, 2, 2) + block, BF16),
+            ones=pltpu.VMEM((4, 2) + block, BF16),
+            line=pltpu.VMEM((5,) + unit, BF16),
+            last=pltpu.VMEM(last, BF16),
+            load=pltpu.SemaphoreType.DMA((4,)),
+            sent=pltpu.SemaphoreType.DMA((20,)),
+            landed=pltpu.SemaphoreType.DMA((20,)),
+        )
+
+
+def added(target, others, lead, rows, wide=False):
+    tall = min(rows, 16)
+    per = rows // tall
+    total = int(np.prod(lead, dtype=np.int64)) * per
+
+    def step(index, carry):
+        spot, rest = [], index // per
+        for size in reversed(lead):
+            spot.insert(0, rest % size)
+            rest = rest // size
+        where = tuple(spot) + (pl.ds(pl.multiple_of((index % per) * tall, tall), tall), slice(None))
+        value = target[where]
+        if wide:
+            value = value.astype(F32)
+            for other in others:
+                value = value + other[where].astype(F32)
+            target[where] = value.astype(BF16)
+        else:
+            for other in others:
+                value = value + other[where]
+            target[where] = value
+        return carry
+
+    lax.fori_loop(0, total, step, 0)
+
+
+def piece_steps(piece, refs, source, target, place):
+    mine, mates, ones, line, last = (refs[k] for k in ("mine", "mates", "ones", "line", "last"))
+    load, sent, landed = refs["load"], refs["sent"], refs["landed"]
+    rows, low = piece.rows, piece.low
+    own1, own3 = place.own(piece.first), place.own(piece.third)
+    z = place.z
+
+    def pick(ref, block, which):
+        return ref.at[block, which] if piece.first == "y" else ref.at[block, :, which]
+
+    def share(block, core):
+        return source.at[block, :, :, core, pl.ds(low, rows), :]
+
+    def fetch(block):
+        return pltpu.make_async_copy(share(block, place.core), mine.at[block], load.at[block])
+
+    def to_mate(block):
+        return remote(
+            share(block, 1 - place.core), mates.at[block], sent.at[block], landed.at[block], place.mate()
+        )
+
+    def to_first(block):
+        return remote(
+            pick(mine, block, 1 - own1),
+            ones.at[block],
+            sent.at[4 + block],
+            landed.at[4 + block],
+            place.across(piece.first),
+        )
+
+    def to_third(block):
+        spot = 8 + block
+        return remote(
+            ones.at[block, 1 - own3],
+            last.at[block],
+            sent.at[spot],
+            landed.at[spot],
+            place.across(piece.third),
+        )
+
+    def unit(block):
+        if piece.middle:
+            return ones.at[block]
+        return ones.at[block, own3]
+
+    def along(block, step):
+        slot = jnp.where(z + step == block, 4, block) if step < 0 else block
+        return remote(
+            unit(block),
+            line.at[slot],
+            sent.at[12 + block],
+            landed.at[12 + slot],
+            place.at(z=jnp.clip(z + step, 0, 3)),
+        )
+
+    def arrival(slot):
+        return remote(unit(0), line.at[slot], sent.at[12], landed.at[12 + slot], place.mate())
+
+    lead = (2,) if piece.middle else ()
+
+    def join(block):
+        fetch(block).wait()
+        to_mate(block).wait_recv()
+        added(mine.at[block], [mates.at[block]], (2, 2), rows)
+        to_first(block).start()
+
+    def merge(block):
+        to_first(block).wait_recv()
+        added(ones.at[block], [pick(mine, block, own1)], (2,), rows)
+        if not piece.middle:
+            to_third(block).start()
+
+    def turn(block):
+        if not piece.middle:
+            to_third(block).wait_recv()
+            added(unit(block), [last.at[block]], (), rows)
+
+    def pass_on(block, step):
+        heading = block > z if step > 0 else block < z
+        inner = z > 0 if step > 0 else z < 3
+
+        @pl.when(heading)
+        def _():
+            @pl.when(inner)
+            def _():
+                arrival(block).wait_recv()
+                added(unit(block), [line.at[block]], lead, rows)
+
+            along(block, step).start()
+
+    def finish():
+        @pl.when(z > 0)
+        def _():
+            arrival(z).wait_recv()
+            added(unit(z), [line.at[z]], lead, rows)
+
+        @pl.when(z < 3)
+        def _():
+            arrival(4).wait_recv()
+            added(unit(z), [line.at[4]], lead, rows)
+
+    def out(value):
+        target[pl.ds(low, rows), :] = value
+
+    for block in (3, 0, 2, 1):
+        fetch(block).start()
+        to_mate(block).start()
+    yield
+    join(3)
+    yield
+    join(0)
+    yield
+    merge(3)
+    join(2)
+    yield
+    merge(0)
+    join(1)
+    yield
+    turn(3)
+    pass_on(3, 1)
+    turn(0)
+    pass_on(0, -1)
+    yield
+    merge(2)
+    yield
+    turn(2)
+    pass_on(2, 1)
+    yield
+    merge(1)
+    yield
+    turn(1)
+    pass_on(1, -1)
+    yield
+    pass_on(1, 1)
+    yield
+    pass_on(2, -1)
+    yield
+    finish()
+    if piece.middle:
+        final = remote(
+            ones.at[z, 1 - own3], last, sent.at[8], landed.at[8], place.across(piece.third)
+        )
+        final.start()
+        yield
+        final.wait_recv()
+        out(ones[z, own3].astype(F32) + last[...].astype(F32))
+    else:
+        out(ones[z, own3].astype(F32))
+    yield
+    for block in range(4):
+        to_mate(block).wait_send()
+        to_first(block).wait_send()
+        if not piece.middle:
+            to_third(block).wait_send()
+
+        @pl.when(block > z)
+        def _():
+            along(block, 1).wait_send()
+
+        @pl.when(block < z)
+        def _():
+            along(block, -1).wait_send()
+
+    if piece.middle:
+        final.wait_send()
+
+
+def gain_steps(mine, slots, sent, landed, place):
+    partners = [place.mate(), place.across("x"), place.across("y")]
+    for other in (1, 2):
+        partners.append(place.at(z=jnp.bitwise_xor(place.z, other)))
+    for spot, partner in enumerate(partners):
+        copy = remote(mine.at[spot], slots.at[spot], sent.at[spot], landed.at[spot], partner)
+        copy.start()
+        yield
+        copy.wait()
+        mine[spot + 1] = mine[spot] + slots[spot]
+
+
+def plan(widths):
+    wide, heads_wide, narrow = widths
+    return [
+        Piece(0, 0, 0, 32, wide, "y", True),
+        Piece(1, 1, 0, 32, wide, "x", True),
+        Piece(2, 2, 0, 16, wide, "y", False),
+        Piece(2, 2, 16, 16, wide, "x", False),
+        Piece(3, 3, 0, 32, heads_wide, "y", False),
+        Piece(4, 4, 0, 32, heads_wide, "x", False),
+        Piece(5, 5, 0, 32, narrow, "y", False),
+        Piece(6, 6, 0, 32, narrow, "x", False),
+    ]
+
+
+def reduce_grads(grads, gains):
+    widths = (grads[0].shape[1], grads[3].shape[1], grads[5].shape[1])
+    pieces = plan(widths)
+    scratch = [piece.scratch() for piece in pieces]
+    names = list(scratch[0])
+    flat = [entry[name] for entry in scratch for name in names]
+    count = len(grads)
+
+    def body(*refs):
+        sources, gain = refs[:count], refs[count]
+        targets, gain_out = refs[count + 1 : 2 * count + 1], refs[2 * count + 1]
+        rest = refs[2 * count + 2 :]
+        gain_mine, gain_slots, gain_sent, gain_landed = rest[:4]
+        rest = rest[4:]
+        place = Place()
+        enter(place)
+        gain_mine[0] = gain[...]
+        gain_run = gain_steps(gain_mine, gain_slots, gain_sent, gain_landed, place)
+        runs = []
+        for spot, piece in enumerate(pieces):
+            own = dict(zip(names, rest[spot * len(names) : (spot + 1) * len(names)]))
+            runs.append(
+                piece_steps(piece, own, sources[piece.source], targets[piece.target], place)
+            )
+        starts = [0, 0, 4, 4, 6, 6, 7, 7]
+        active = True
+        slot = 0
+        while active:
+            active = False
+            for run, start in zip(runs, starts):
+                if slot >= start and next(run, "done") != "done":
+                    active = True
+                if slot < start:
+                    active = True
+            next(gain_run, None)
+            slot += 1
+        for _ in gain_run:
+            pass
+        gain_out[...] = gain_mine[5]
+
+    views = [g.reshape(4, 2, 2, 2, 32, g.shape[1]) for g in grads]
+    outs = [jax.ShapeDtypeStruct((32, g.shape[1]), F32) for g in grads]
+    outs.append(jax.ShapeDtypeStruct(gains.shape, F32))
+    return pl.pallas_call(
+        body,
+        out_shape=outs,
+        in_specs=[pl.BlockSpec(memory_space=pl.ANY)] * count
+        + [pl.BlockSpec(memory_space=pltpu.VMEM)],
+        out_specs=[pl.BlockSpec(memory_space=pltpu.VMEM)] * (count + 1),
+        scratch_shapes=[
+            pltpu.VMEM((6,) + gains.shape, F32),
+            pltpu.VMEM((5,) + gains.shape, F32),
+            pltpu.SemaphoreType.DMA((5,)),
+            pltpu.SemaphoreType.DMA((5,)),
+        ]
+        + flat,
+        compiler_params=pltpu.CompilerParams(
+            collective_id=0, has_side_effects=True, vmem_limit_bytes=VMEM_LIMIT
+        ),
+    )(*views, gains)
+
+
 def shards(
     tokens, attn_gain, w_query, w_key, w_value, w_output, mlp_gain, w_gate, w_up, w_down, out_grad
 ):
@@ -388,20 +738,21 @@
     _, first_back = jax.vjp(rms_norm, inputs, attn_gain.astype(F32))
     d_inputs_norm, attn_gain_part = first_back(d_normed)
     tokens_grad = d_middle + d_inputs_norm
-    parts = [query_grad, key_grad, value_grad, output_grad, gate_grad, up_grad, down_grad]
-    joined = lax.psum_scatter(
-        jnp.concatenate(parts, axis=1), ("dp", "seq"), scatter_dimension=0, tiled=True
-    ).astype(F32)
-    edges = np.cumsum([part.shape[1] for part in parts])[:-1]
-    query_grad, key_grad, value_grad, output_grad, gate_grad, up_grad, down_grad = jnp.split(
-        joined, edges, axis=1
-    )
-    gains = lax.psum_scatter(
-        jnp.stack([attn_gain_part, mlp_gain_part], axis=1),
-        ("dp", "seq"),
-        scatter_dimension=0,
-        tiled=True,
-    )
+    grads = [gate_grad, up_grad, down_grad, output_grad, value_grad, query_grad, key_grad]
+    gain_parts = jnp.stack([attn_gain_part, mlp_gain_part])
+    own = lax.axis_index("dp") * lax.axis_size("seq") + lax.axis_index("seq")
+    if (lax.axis_size("dp"), lax.axis_size("seq")) == (8, 4):
+        *grads, gains = reduce_grads(grads, jnp.pad(gain_parts, ((0, 6), (0, 0))))
+        share = width // 32
+        gains = lax.dynamic_slice(gains, (0, own * share), (2, share)).T
+    else:
+        joined = lax.psum_scatter(
+            jnp.concatenate(grads, axis=1), ("dp", "seq"), scatter_dimension=0, tiled=True
+        ).astype(F32)
+        edges = np.cumsum([part.shape[1] for part in grads])[:-1]
+        grads = jnp.split(joined, edges, axis=1)
+        gains = lax.psum_scatter(gain_parts.T, ("dp", "seq"), scatter_dimension=0, tiled=True)
+    gate_grad, up_grad, down_grad, output_grad, value_grad, query_grad, key_grad = grads
     return (
         layer_out,
         tokens_grad,

time: 767 us -> 571 us (0.74)
  waiting for transfers between devices: 508 us -> 186 us
  Pallas kernels: 73.5 us -> 215 us
  local copies, waits for them, and re-layouts: 55 us -> 34 us
    unnamed x9 -> x5, waiting for transfers between devices: 309 us -> 1.93 us
    pallas_call x0 -> x1, Pallas kernels: none -> 141 us  [reduce_grads(): pl.pallas_call(body, out_shape=outs, in_specs=[pl.BlockSpec(memory_space=...]
    unnamed x70 -> x71, local copies, waits for them, and re-layouts: 49 us -> 6.27 us
    convert_element_type x0 -> x3, local copies, waits for them, and re-layouts: none -> 25.2 us  [the longest x1 8.45 us: shards(): down_grad = dot_tn(out_grad, hidden).astype(BF16)]
    all_gather x1, waiting for transfers between devices: 14.9 us -> 0.01 us  [shards(): d_state = before(lax.all_gather(d_state, 'seq'), 'seq', True).astype(BF16)]
  transfers between devices with their start and end apart: 7 -> 5, of which waited for: 7 -> 4; matrix products, arithmetic and copies ran while one was open for 11% -> 15% of each run, Pallas kernels for 2% -> 3%
where the time goes in v2:
time: 571 us; the launch traced here: 565 us
  Pallas kernels  215 us (38%)
  waiting for transfers between devices  186 us (33%)
  matrix products  89.6 us (16%)
  local copies, waits for them, and re-layouts  34 us (6%)
  between operations  14.3 us (3%)
  other arithmetic  14.1 us (2%)
  blocking collectives  12.1 us (2%)
    all_gather x3, waiting for transfers between devices, shards(): lax.all_gather(w, ('dp', 'seq'), axis=0, tiled=True)  168 us
    pallas_call x1, Pallas kernels, reduce_grads(): pl.pallas_call(body, out_shape=outs, in_specs=[pl.BlockSpec(memory_space=...  141 us
    pallas_call x5, Pallas kernels, call(): pl.pallas_call(body, out_shape=[jax.ShapeDtypeStruct(shape, kind) for sha...  73.8 us
    dot_general x4, matrix products, dot(): return jnp.dot(left, right, preferred_element_type=F32)  32.9 us
    dot_general x7, matrix products, dot_tn(): lax.dot_general(left, right, (((0,), (0,)), ((), ())), preferred_element_...  30.1 us
    dot_general x7, matrix products, dot_nt(): lax.dot_general(left, right, (((1,), (1,)), ((), ())), preferred_element_...  26.6 us
    all_gather x1, waiting for transfers between devices, shards(): state = before(lax.all_gather(state, 'seq'), 'seq').astype(BF16)  15.6 us
  transfers between devices with their start and end apart: 5, of which 4 were waited for; matrix products, arithmetic and copies ran while one was open for 15% of the time, Pallas kernels for 3%

profile of v2, /device:TPU:0, one launch (start us, length us, event | category | flops | bytes accessed | tf_op | source)
XLA Modules:
  0.0 565.0 jit_solution(6729368284833253883)
XLA Ops:
  7.2 0.0 all-gather.16.cloned.1.call-start
  7.2 1.4 convert_element_type.73
  8.7 5.2 shard_map.221
  13.9 7.7 %shard_map.222 = (bf16[16,64,256]{2,1,0:T(8,128)(2,1)}, f32[16,1,256]{2,1,0:T(1,128)}) custom-call(bf16[512,256]{1,0:T(8,128)(2,1)} %get-tuple-element.33.keys, bf16[512,1024]{1,0:T(8,128)(2,1)} %get-tuple-element.34.values, bf16[128,256]{1,0:T(8,128)(2,1)} %constant.39.clone.pick_a, bf16[128,256]{1,0:T(8,128)(2,1)} %constant.40.clone.pick_b, ...), custom_call_target="tpu_custom_call" | custom-call | tf_op jit(solution)/shard_map/pallas_call | solution.py:270
  21.6 0.0 all-gather.10.cloned.1.call-start
  21.7 0.7 all-gather.10.cloned.1.call-update
  22.4 0.0 all-gather.12.cloned.1.call-start
  22.4 0.7 all-gather.12.cloned.1.call-update
  23.1 0.0 all-gather.14.cloned.1.call-start
  23.2 0.5 all-gather.14.cloned.1.call-update
  23.7 0.0 all-gather.18.cloned.1.call-start
  23.7 6.6 %all-gather.1 = f32[64,1,256]{2,1,0:T(1,128)S(1)} all-gather(f32[16,1,256]{2,1,0:T(1,128)} %get-tuple-element.36), channel_id=3, replica_groups=mesh['dp'=8,'seq'=4] {'seq'}, dimensions={0}, use_global_device_ids=true | all-gather | bytes 81920 | tf_op jit(solution)/shard_map/all_gather | solution.py:673
  30.4 0.2 fusion.15
  30.5 0.6 reduce_sum.112.total
  31.2 0.3 fusion.9
  31.5 15.6 %all-gather.16.cloned.1.call-done = bf16[64,64,256]{2,1,0:T(8,128)(2,1)} async-done(((bf16[16,64,256]{2,1,0:T(8,128)(2,1)}), bf16[64,64,256]{2,1,0:T(8,128)(2,1)}) %all-gather.16.cloned.1.call-update) | async-done | bytes 2097168 | tf_op jit(solution)/shard_map/all_gather | solution.py:672
  47.1 3.0 fusion.6.state
  50.1 14.5 %shard_map.223 = (bf16[512,1024]{1,0:T(8,128)(2,1)}, f32[512,1024]{1,0:T(8,128)}) custom-call(bf16[512,256]{1,0:T(8,128)(2,1)} %get-tuple-element.32.query, bf16[512,256]{1,0:T(8,128)(2,1)} %get-tuple-element.33.keys, bf16[512,1024]{1,0:T(8,128)(2,1)} %get-tuple-element.34.values, bf16[128,256]{1,0:T(8,128)(2,1)} %constant.39.clone.pick_a, ...), custom_call_target="tpu_custom_call" | custom-call | tf_op jit(solution)/shard_map/pallas_call | solution.py:270
  64.6 2.6 multiply_reduce_fusion.2
  67.2 1.3 copy-done.3
  68.5 1.2 multiply_convert_fusion.2
  69.7 47.5 %all-gather.10.cloned.1.call-done = bf16[1024,2752]{1,0:T(8,128)(2,1)} async-done(((bf16[32,2752]{1,0:T(8,128)(2,1)}), bf16[1024,2752]{1,0:T(8,128)(2,1)}) %all-gather.10.cloned.1.call-update) | async-done | bytes 5636112 | tf_op jit(solution)/shard_map/all_gather | solution.py:654
  117.2 8.6 %fusion.19 = f32[512,2752]{0,1:T(8,128)} fusion(bf16[512,1024]{1,0:T(8,128)(2,1)} %multiply_convert_fusion.2, bf16[1024,2752]{1,0:T(8,128)(2,1)} %all-gather.10.cloned.1.call-done), kind=kOutput, calls=%fused_computation.60 | convolution fusion | flops 2885681152 | bytes 12320768 | tf_op jit(solution)/shard_map/dot_general | solution.py:45
  125.8 60.6 %all-gather.12.cloned.1.call-done = bf16[1024,2752]{1,0:T(8,128)(2,1)} async-done(((bf16[32,2752]{1,0:T(8,128)(2,1)}), bf16[1024,2752]{1,0:T(8,128)(2,1)}) %all-gather.12.cloned.1.call-update) | async-done | bytes 5636112 | tf_op jit(solution)/shard_map/all_gather | solution.py:654
  186.3 8.5 %fusion.20 = f32[512,2752]{0,1:T(8,128)} fusion(bf16[512,1024]{1,0:T(8,128)(2,1)} %multiply_convert_fusion.2, bf16[1024,2752]{1,0:T(8,128)(2,1)} %all-gather.12.cloned.1.call-done), kind=kOutput, calls=%fused_computation.61 | convolution fusion | flops 2885681152 | bytes 12320768 | tf_op jit(solution)/shard_map/dot_general | solution.py:45
  194.9 60.4 %all-gather.14.cloned.1.call-done = bf16[1024,2752]{1,0:T(8,128)(2,1)} async-done(((bf16[32,2752]{1,0:T(8,128)(2,1)}), bf16[1024,2752]{1,0:T(8,128)(2,1)}) %all-gather.14.cloned.1.call-update) | async-done | bytes 5636112 | tf_op jit(solution)/shard_map/all_gather | solution.py:654
  255.3 13.2 %multiply_convert_fusion = (bf16[512,2752]{0,1:T(8,128)(2,1)S(1)}, bf16[512,2752]{0,1:T(8,128)(2,1)S(1)}, bf16[512,2752]{0,1:T(8,128)(2,1)}) fusion(f32[512,2752]{0,1:T(8,128)} %fusion.19, f32[512,2752]{0,1:T(8,128)} %fusion.20, bf16[512,1024]{1,0:T(8,128)(2,1)} %param.24, bf16[1024,2752]{1,0:T(8,128)(2,1)} %all-gather.14.cloned.1.call-done), kind=kOutput, calls=%fused_computation.7 | convolution fusion | flops 2908225536 | bytes 26411008 | tf_op jit(solution)/shard_map/dot_general | solution.py:45
  268.6 7.3 %fusion.21 = f32[512,1024]{1,0:T(8,128)S(1)} fusion(bf16[512,2752]{0,1:T(8,128)(2,1)S(1)} %get-tuple-element.58, bf16[1024,2752]{1,0:T(8,128)(2,1)} %all-gather.10.cloned.1.call-done), kind=kOutput, calls=%fused_computation.62 | convolution fusion | flops 2885681152 | bytes 10551296 | tf_op jit(solution)/shard_map/dot_general | solution.py:49
  275.9 3.6 multiply_reduce_fusion
  279.6 0.5 fusion.7
  280.1 2.4 convolution_convert_fusion.5.d_mixed
  282.5 9.2 %shard_map.224 = (bf16[16,64,256]{2,1,0:T(8,128)(2,1)}, f32[16,1,256]{2,1,0:T(1,128)}) custom-call(bf16[512,256]{1,0:T(8,128)(2,1)} %get-tuple-element.32.query, bf16[512,1024]{1,0:T(8,128)(2,1)} %get-tuple-element.37.mixed, f32[512,1024]{1,0:T(8,128)} %get-tuple-element.38.inverse, bf16[512,1024]{1,0:T(8,128)(2,1)} %convolution_convert_fusion.5.d_mixed, ...), custom_call_target="tpu_custom_call" | custom-call | tf_op jit(solution)/shard_map/pallas_call | solution.py:270
  291.7 5.5 all-gather.3
  297.2 0.1 fusion.16
  297.3 0.6 reduce_sum.117.d_total
  297.9 7.3 %convolution_convert_fusion.1 = bf16[1024,2752]{0,1:T(8,128)(2,1)} fusion(bf16[512,2752]{0,1:T(8,128)(2,1)} %copy-done.31, bf16[512,1024]{1,0:T(8,128)(2,1)S(1)} %copy-done.12), kind=kOutput, calls=%fused_computation.2 | convolution fusion | flops 2888499200 | bytes 9502720 | tf_op jit(solution)/shard_map/dot_general | solution.py:53
  305.2 8.4 %copy.28 = bf16[1024,2752]{1,0:T(8,128)(2,1)} copy(bf16[1024,2752]{0,1:T(8,128)(2,1)} %convolution_convert_fusion.1) | data formatting | bytes 11272192 | tf_op jit(solution)/shard_map/convert_element_type | solution.py:697
  313.6 6.7 %convolution_convert_fusion = bf16[1024,2752]{0,1:T(8,128)(2,1)} fusion(bf16[512,2752]{0,1:T(8,128)(2,1)} %copy-done.29, bf16[512,1024]{1,0:T(8,128)(2,1)S(1)} %copy-done.12), kind=kOutput, calls=%fused_computation.1 | convolution fusion | flops 2888499200 | bytes 9502720 | tf_op jit(solution)/shard_map/dot_general | solution.py:53
  320.3 8.4 %copy.29 = bf16[1024,2752]{1,0:T(8,128)(2,1)} copy(bf16[1024,2752]{0,1:T(8,128)(2,1)} %convolution_convert_fusion) | data formatting | bytes 11272192 | tf_op jit(solution)/shard_map/convert_element_type | solution.py:698
  328.7 6.7 %fusion.4 = bf16[1024,2752]{0,1:T(8,128)(2,1)} fusion(bf16[512,2752]{0,1:T(8,128)(2,1)} %get-tuple-element.59, bf16[512,1024]{1,0:T(8,128)(2,1)S(1)} %copy-done.14), kind=kOutput, calls=%fused_computation.11 | convolution fusion | flops 2888499200 | bytes 9502720 | tf_op jit(solution)/shard_map/dot_general | solution.py:53
  335.4 8.5 %copy.30 = bf16[1024,2752]{1,0:T(8,128)(2,1)} copy(bf16[1024,2752]{0,1:T(8,128)(2,1)} %fusion.4) | data formatting | bytes 11272192 | tf_op jit(solution)/shard_map/convert_element_type | solution.py:693
  343.9 4.1 convolution_convert_fusion.4
  347.9 6.8 %add_convert_fusion = bf16[512,1024]{1,0:T(8,128)(2,1)} fusion(f32[512,1024]{1,0:T(8,128)S(1)} %copy-done.5, bf16[512,2752]{0,1:T(8,128)(2,1)S(1)} %copy-done.30, bf16[1024,2752]{1,0:T(8,128)(2,1)} %all-gather.14.cloned.1.call-done), kind=kOutput, calls=%fused_computation.32 | convolution fusion | flops 2886729728 | bytes 11599872 | tf_op jit(solution)/shard_map/dot_general | solution.py:49
  354.8 3.1 fusion.5.d_state
  357.8 37.2 %shard_map.225 = (bf16[512,256]{1,0:T(8,128)(2,1)}, bf16[512,256]{1,0:T(8,128)(2,1)}, bf16[512,1024]{1,0:T(8,128)(2,1)}) custom-call(bf16[512,256]{1,0:T(8,128)(2,1)} %get-tuple-element.32.query, bf16[512,256]{1,0:T(8,128)(2,1)} %get-tuple-element.33.keys, bf16[512,1024]{1,0:T(8,128)(2,1)} %get-tuple-element.34.values, ...), custom_call_target="tpu_custom_call" | custom-call | tf_op jit(solution)/shard_map/pallas_call | solution.py:270
  395.0 1.6 fusion.22
  396.6 0.1 copy-done.10
  396.7 2.7 fusion.23
  399.4 2.7 convolution_convert_fusion.3
  402.1 1.3 convolution_convert_fusion.7
  403.4 1.3 convolution_convert_fusion.6
  404.8 2.3 fusion.12
  407.0 0.6 select_maximum_fusion.refs_7_
  407.7 140.9 %shard_map.226 = (f32[32,2752]{1,0:T(8,128)}, f32[32,2752]{1,0:T(8,128)}, f32[32,2752]{1,0:T(8,128)}, f32[32,1024]{1,0:T(8,128)}, f32[32,1024]{1,0:T(8,128)}, /*...) custom-call(bf16[4,2,2,2,32,2752]{5,4,3,2,1,0:T(8,128)(2,1)} %bitcast.58, ...), custom_call_target="tpu_custom_call" | custom-call | tf_op jit(solution)/shard_map/pallas_call | solution.py:625
  548.5 0.8 dynamic-slice_bitcast_fusion
  549.3 0.5 slice_bitcast_fusion
  549.9 3.6 fusion.8
  553.5 0.6 copy.38
  554.1 0.6 copy.39
  554.7 0.7 copy.40
  555.4 0.7 copy.41
  556.0 0.7 copy.42
  556.8 0.7 copy.43
  557.5 0.7 copy.44
  (72 shorter events, 0.2 us)
Async XLA Ops:
  7.2 57.4 %copy-start = (bf16[1024,1024]{1,0:T(8,128)(2,1)S(1)}, bf16[1024,1024]{1,0:T(8,128)(2,1)}, u32[]{:S(2)}) copy-start(bf16[1024,1024]{1,0:T(8,128)(2,1)} %param.19) | copy-start | bytes 6291460
  7.2 39.9 %all-gather.16.cloned.1.call-start = ((), (), s32[]{:S(2)}) async-start(), calls=%async_computation.3 | async-start | bytes 2621440 | tf_op jit(solution)/shard_map/all_gather | solution.py:672
  13.9 17.3 %copy-start.25 = (bf16[1024]{0:T(1024)(128)(2,1)S(1)}, bf16[1024]{0:T(1024)(128)(2,1)}, u32[]{:S(2)}) copy-start(bf16[1024]{0:T(1024)(128)(2,1)} %param.20) | copy-start | bytes 6148
  13.9 17.3 %copy-start.2 = (bf16[512,1024]{1,0:T(8,128)(2,1)S(1)}, bf16[512,1024]{1,0:T(8,128)(2,1)}, u32[]{:S(2)}) copy-start(bf16[512,1024]{1,0:T(8,128)(2,1)} %tok.1) | copy-start | bytes 3145732
  21.6 95.6 %all-gather.10.cloned.1.call-start = ((), (), s32[]{:S(2)}) async-start(), calls=%async_computation | async-start | bytes 5947392 | tf_op jit(solution)/shard_map/all_gather | solution.py:654
  22.4 164.0 %all-gather.12.cloned.1.call-start = ((), (), s32[]{:S(2)}) async-start(), calls=%async_computation.1 | async-start | bytes 5947392 | tf_op jit(solution)/shard_map/all_gather | solution.py:654
  23.1 232.2 %all-gather.14.cloned.1.call-start = ((), (), s32[]{:S(2)}) async-start(), calls=%async_computation.2 | async-start | bytes 5947392 | tf_op jit(solution)/shard_map/all_gather | solution.py:654
  23.7 331.1 %all-gather.18.cloned.1.call-start = ((), (), s32[]{:S(2)}) async-start(), calls=%async_computation.4 | async-start | bytes 2621440 | tf_op jit(solution)/shard_map/all_gather | solution.py:708
  67.2 1.3 copy-start.3
  268.5 7.3 %copy-start.31 = (bf16[512,2752]{0,1:T(8,128)(2,1)}, bf16[512,2752]{0,1:T(8,128)(2,1)S(1)}, u32[]{:S(2)}) copy-start(bf16[512,2752]{0,1:T(8,128)(2,1)S(1)} %get-tuple-element.58) | copy-start | bytes 8454148
  268.5 7.4 %copy-start.29 = (bf16[512,2752]{0,1:T(8,128)(2,1)}, bf16[512,2752]{0,1:T(8,128)(2,1)S(1)}, u32[]{:S(2)}) copy-start(bf16[512,2752]{0,1:T(8,128)(2,1)S(1)} %get-tuple-element.57) | copy-start | bytes 8454148
  268.5 7.4 %copy-start.4 = (f32[512,1024]{1,0:T(8,128)S(1)}, f32[512,1024]{1,0:T(8,128)}, u32[]{:S(2)}) copy-start(f32[512,1024]{1,0:T(8,128)} %copy-done.3) | copy-start | bytes 6291460
  268.6 7.4 %copy-start.26 = (bf16[1024,2752]{1,0:T(8,128)(2,1)S(1)}, bf16[1024,2752]{1,0:T(8,128)(2,1)}, u32[]{:S(2)}) copy-start(bf16[1024,2752]{1,0:T(8,128)(2,1)} %all-gather.12.cloned.1.call-done) | copy-start | bytes 16908292
  275.9 3.6 copy-start.13
  280.1 2.4 copy-start.6
  282.5 15.4 %copy-start.12 = (bf16[512,1024]{1,0:T(8,128)(2,1)S(1)}, bf16[512,1024]{1,0:T(8,128)(2,1)}, u32[]{:S(2)}) copy-start(bf16[512,1024]{1,0:T(8,128)(2,1)} %multiply_convert_fusion.2) | copy-start | bytes 3145732
  320.3 8.4 %copy-start.14 = (bf16[512,1024]{1,0:T(8,128)(2,1)S(1)}, bf16[512,1024]{1,0:T(8,128)(2,1)}, u32[]{:S(2)}) copy-start(bf16[512,1024]{1,0:T(8,128)(2,1)} %param.24) | copy-start | bytes 3145732
  335.4 8.5 %copy-start.7 = (f32[512,1024]{1,0:T(8,128)S(1)}, f32[512,1024]{1,0:T(8,128)}, u32[]{:S(2)}) copy-start(f32[512,1024]{1,0:T(8,128)} %copy-done.6) | copy-start | bytes 6291460
  343.9 4.1 copy-start.5
  343.9 4.1 copy-start.30
  357.8 37.2 %copy-start.11 = (bf16[1024,256]{1,0:T(8,128)(2,1)S(1)}, bf16[1024,256]{1,0:T(8,128)(2,1)}, u32[]{:S(2)}) copy-start(bf16[1024,256]{1,0:T(8,128)(2,1)} %wq.1) | copy-start | bytes 1572868
  395.0 1.7 copy-start.10
  396.7 2.7 copy-start.27
  396.7 2.7 copy-start.28
  399.4 2.7 copy-start.19
  402.1 1.3 copy-start.18
  402.1 2.6 copy-start.9
  402.1 2.6 copy-start.22
  407.7 142.2 %copy-start.8 = (f32[512,1024]{1,0:T(8,128)S(1)}, f32[512,1024]{1,0:T(8,128)}, u32[]{:S(2)}) copy-start(f32[512,1024]{1,0:T(8,128)} %copy-done.6) | copy-start | bytes 6291460
  549.8 3.7 copy-start.24
  549.8 4.3 copy-start.23
  549.8 4.9 copy-start.21
  549.9 5.5 copy-start.20
  549.9 6.2 %copy-start.17 = (f32[32,2752]{1,0:T(8,128)S(1)}, f32[32,2752]{1,0:T(8,128)}, u32[]{:S(2)}) copy-start(f32[32,2752]{1,0:T(8,128)} %get-tuple-element.85) | copy-start | bytes 1056772
  549.9 6.9 %copy-start.16 = (f32[32,2752]{1,0:T(8,128)S(1)}, f32[32,2752]{1,0:T(8,128)}, u32[]{:S(2)}) copy-start(f32[32,2752]{1,0:T(8,128)} %get-tuple-element.86) | copy-start | bytes 1056772
  549.9 8.4 %copy-start.1 = (bf16[1024,1024]{1,0:T(8,128)(2,1)S(1)}, bf16[1024,1024]{1,0:T(8,128)(2,1)}, u32[]{:S(2)}) copy-start(bf16[1024,1024]{1,0:T(8,128)(2,1)} %param.19) | copy-start | bytes 6291460
  553.5 4.0 copy-start.15
Sparse Core Ops, SparseCore 0:
  21.7 25.2 all-gather.15
  49.9 67.2 all-gather.9
  120.1 66.2 all-gather.11
  189.0 66.2 all-gather.13
  291.8 21.5 all-gather.17

commit v3 on v1

--- a/solution.py
+++ b/solution.py
@@ -16,7 +16,7 @@
 QUAD = 1.0 / (4.0 * math.sqrt(2.0))
 F32 = jnp.float32
 BF16 = jnp.bfloat16
-VMEM_LIMIT = 58 << 20
+VMEM_LIMIT = 60 << 20
 
 
 def feature_tables():
@@ -113,7 +113,7 @@
     return row >= column
 
 
-def attend_body(query, keys, values, pick_a, pick_b, rows, state, total, mixed, inverse, block=256):
+def attend_body(query, keys, values, pick_a, pick_b, rows, state, total, mixed, inverse, between=None, block=256):
     pairs = values.shape[1] // LANES
     count = keys.shape[0]
 
@@ -146,6 +146,8 @@
                     invs = jnp.where(mask, invs, flip)
             mixed[start:stop, tile_at(pair)] = numer.astype(BF16)
             inverse[start:stop, tile_at(pair)] = invs
+        if between is not None:
+            between(pair)
         return carry
 
     lax.fori_loop(0, pairs, step, 0)
@@ -202,6 +204,7 @@
     q_sum,
     k_sum,
     v_sum,
+    between=None,
     block=256,
 ):
     pairs = values.shape[1] // LANES
@@ -259,6 +262,8 @@
             q_sum[:, place] += jnp.concatenate(grads_q, axis=0) * 0.25 + only(lanes, inter_q)
             k_sum[:, place] += jnp.concatenate(grads_k, axis=0) * 0.25 + only(lanes, inter_k)
         d_values[:, spot] = v_sum[...].astype(BF16)
+        if between is not None:
+            between(pair)
         return carry
 
     lax.fori_loop(0, pairs, step, 0)
@@ -291,7 +296,746 @@
     return jnp.sum(jnp.where(chosen, parts.astype(F32), 0.0), axis=0)
 
 
-def shards(
+MESH_ID = pl.DeviceIdType.MESH
+
+
+class Place:
+    def __init__(self):
+        self.dp, self.seq = lax.axis_index("dp"), lax.axis_index("seq")
+        self.z, self.y = self.dp // 2, self.dp % 2
+        self.x, self.core = self.seq // 2, self.seq % 2
+        self.zh, self.zl = self.z // 2, self.z % 2
+
+    def at(self, z=None, y=None, x=None, core=None):
+        z = self.z if z is None else z
+        y = self.y if y is None else y
+        x = self.x if x is None else x
+        core = self.core if core is None else core
+        return (z * 2 + y, x * 2 + core)
+
+    def mate(self):
+        return self.at(core=1 - self.core)
+
+    def across(self, axis):
+        return self.at(y=1 - self.y) if axis == "y" else self.at(x=1 - self.x)
+
+    def own(self, axis):
+        return self.y if axis == "y" else self.x
+
+
+def remote(source, target, sent, landed, device):
+    return pltpu.make_async_remote_copy(
+        src_ref=source,
+        dst_ref=target,
+        send_sem=sent,
+        recv_sem=landed,
+        device_id=device,
+        device_id_type=MESH_ID,
+    )
+
+
+def enter(place):
+    barrier = pltpu.get_barrier_semaphore()
+    others = [place.mate(), place.across("x"), place.across("y")]
+    for other in (1, 2, 3):
+        others.append(place.at(z=jnp.bitwise_xor(place.z, other)))
+    for device in others:
+        pl.semaphore_signal(barrier, inc=1, device_id=device, device_id_type=MESH_ID)
+    pl.semaphore_wait(barrier, len(others))
+
+
+class Clock:
+    def __init__(self):
+        self.entries, self.slot = [], 0
+
+    def add(self, run, start=0):
+        self.entries.append([max(start, self.slot), run])
+
+    def tick(self):
+        for entry in reversed(list(self.entries)):
+            if self.slot >= entry[0]:
+                pause = next(entry[1], None)
+                if pause is None:
+                    self.entries.remove(entry)
+                else:
+                    entry[0] = self.slot + pause
+        self.slot += 1
+
+    def drain(self):
+        while self.entries:
+            self.tick()
+
+
+def spread_steps(shard, whole, rows, columns, first, sems, place):
+    sent, landed, local = sems
+    zh, zl = place.zh, place.zl
+    every = slice(None)
+    third = "x" if first == "y" else "y"
+
+    def grid(one, three):
+        return (one, three) if first == "y" else (three, one)
+
+    def block(high, low, one, three, core=None):
+        core = place.core if core is None else core
+        return whole.at[(high, low) + grid(one, three) + (core, rows, columns)]
+
+    own1, own3 = place.own(first), place.own(third)
+    mine = shard.at[rows, columns]
+
+    def keep():
+        return pltpu.make_async_copy(mine, block(zh, zl, own1, own3), local)
+
+    def move(ref, spot, device):
+        return remote(ref, ref, sent.at[spot], landed.at[spot], device)
+
+    def far(high):
+        source = mine
+        return remote(
+            source, block(high, zl, own1, own3), sent.at[0], landed.at[0],
+            place.at(z=jnp.bitwise_xor(place.z, 2)),
+        )
+
+    def cross(three):
+        return move(block(every, zl, own1, three), 1, place.across(third))
+
+    def near(low):
+        return move(block(every, low, own1, every), 2, place.at(z=jnp.bitwise_xor(place.z, 1)))
+
+    def over(one):
+        return move(block(every, every, one, every), 3, place.across(first))
+
+    def mate(core):
+        return move(block(every, every, every, every, core), 4, place.mate())
+
+    keep().start()
+    far(zh).start()
+    yield 1
+    keep().wait()
+    far(1 - zh).wait_recv()
+    cross(own3).start()
+    yield 1
+    cross(1 - own3).wait_recv()
+    near(zl).start()
+    yield 1
+    near(1 - zl).wait_recv()
+    over(own1).start()
+    yield 2
+    over(1 - own1).wait_recv()
+    mate(place.core).start()
+    yield 1
+    mate(1 - place.core).wait_recv()
+    far(zh).wait_send()
+    cross(own3).wait_send()
+    near(zl).wait_send()
+    over(own1).wait_send()
+    mate(place.core).wait_send()
+
+
+def added(target, others, lead):
+    def step(index, carry):
+        spot, rest = [], index
+        for size in reversed(lead):
+            spot.insert(0, rest % size)
+            rest = rest // size
+        where = tuple(spot)
+        value = target[where]
+        for other in others:
+            value = value + other[where]
+        target[where] = value
+        return carry
+
+    lax.fori_loop(0, int(np.prod(lead)), step, 0)
+
+
+def reduce_steps(source, rows, columns, first, refs, sems, place, put):
+    mine, mates, over, near, cross, far = refs
+    sent, landed, local = sems
+    zh, zl = place.zh, place.zl
+    third = "x" if first == "y" else "y"
+    own1, own3 = place.own(first), place.own(third)
+    every = slice(None)
+
+    def share(core):
+        return source.at[every, every, every, every, core, rows, columns]
+
+    def pick(which):
+        return mine.at[:, :, which] if first == "y" else mine.at[:, :, :, which]
+
+    def fetch():
+        return pltpu.make_async_copy(share(place.core), mine, local)
+
+    def send(ref, target, spot, device):
+        return remote(ref, target, sent.at[spot], landed.at[spot], device)
+
+    def to_mate():
+        return send(share(1 - place.core), mates, 0, place.mate())
+
+    def to_over():
+        return send(pick(1 - own1), over, 1, place.across(first))
+
+    def to_near():
+        return send(over.at[:, 1 - zl], near, 2, place.at(z=jnp.bitwise_xor(place.z, 1)))
+
+    def to_cross():
+        return send(near.at[:, 1 - own3], cross, 3, place.across(third))
+
+    def to_far():
+        return send(cross.at[1 - zh], far, 4, place.at(z=jnp.bitwise_xor(place.z, 2)))
+
+    fetch().start()
+    to_mate().start()
+    yield 1
+    fetch().wait()
+    to_mate().wait_recv()
+    added(mine, [mates], (2, 2, 2, 2))
+    to_over().start()
+    yield 2
+    to_over().wait_recv()
+    added(over, [pick(own1)], (2, 2, 2))
+    to_near().start()
+    yield 1
+    to_over().wait_send()
+    to_near().wait_recv()
+    added(near, [over.at[:, zl]], (2, 2))
+    to_cross().start()
+    yield 1
+    to_cross().wait_recv()
+    added(cross, [near.at[:, own3]], (2,))
+    to_far().start()
+    yield 1
+    to_far().wait_recv()
+    put(cross[zh].astype(F32) + far[...].astype(F32))
+    to_mate().wait_send()
+    to_near().wait_send()
+    to_cross().wait_send()
+    to_far().wait_send()
+
+
+def reduce_shapes(rows, columns, count=(), keep=None):
+    keep = count if keep is None else keep
+    return [
+        pltpu.VMEM(keep + (2, 2, 2, 2, rows, columns), BF16),
+        pltpu.VMEM(count + (2, 2, 2, 2, rows, columns), BF16),
+        pltpu.VMEM(count + (2, 2, 2, rows, columns), BF16),
+        pltpu.VMEM(count + (2, 2, rows, columns), BF16),
+        pltpu.VMEM(count + (2, rows, columns), BF16),
+        pltpu.VMEM(count + (rows, columns), BF16),
+    ]
+
+
+def gain_steps(mine, slots, sent, landed, place):
+    partners = [place.mate(), place.across("x"), place.across("y")]
+    for other in (1, 2):
+        partners.append(place.at(z=jnp.bitwise_xor(place.z, other)))
+    for spot, partner in enumerate(partners):
+
+        def swap():
+            return remote(mine.at[spot], slots.at[spot], sent.at[spot], landed.at[spot], partner)
+
+        swap().start()
+        yield 1
+        swap().wait()
+        mine[spot + 1] = mine[spot] + slots[spot]
+
+
+def exchange_steps(state, total, near, far, sent, landed, place, reverse):
+    (near_state, near_total), (far_state, far_total) = near, far
+    half = state.shape[0] // 2
+    giving = place.x == (1 if reverse else 0)
+    taking = place.x == (0 if reverse else 1)
+    second = place.core == (0 if reverse else 1)
+
+    def to_mate():
+        return [
+            remote(state, near_state, sent.at[0], landed.at[0], place.mate()),
+            remote(total, near_total, sent.at[1], landed.at[1], place.mate()),
+        ]
+
+    def move(spot, core, device):
+        part = pl.ds(core * half, half)
+        return [
+            remote(ref.at[part], ref.at[part], sent.at[spot + i], landed.at[spot + i], device)
+            for i, ref in enumerate((far_state, far_total))
+        ]
+
+    def over():
+        return move(2, place.core, place.across("x"))
+
+    def share(core):
+        return move(4, core, place.mate())
+
+    for copy in to_mate():
+        copy.start()
+    yield
+    for copy in to_mate():
+        copy.wait_recv()
+
+    @pl.when(giving)
+    def _():
+        def add(index, carry):
+            head = place.core * half + index
+            far_state[head] = state[head] + near_state[head]
+            far_total[head] = total[head] + near_total[head]
+            return carry
+
+        lax.fori_loop(0, half, add, 0)
+        for copy in over():
+            copy.start()
+
+    yield
+
+    @pl.when(taking)
+    def _():
+        for copy in over():
+            copy.wait_recv()
+        for copy in share(place.core):
+            copy.start()
+
+    yield
+
+    @pl.when(taking)
+    def _():
+        for copy in share(1 - place.core):
+            copy.wait_recv()
+        for copy in share(place.core):
+            copy.wait_send()
+
+    for copy in to_mate():
+        copy.wait_send()
+
+    @pl.when(giving)
+    def _():
+        for copy in over():
+            copy.wait_send()
+
+    def fill(act):
+        def one(head, carry):
+            state[head], total[head] = act(head)
+            return carry
+
+        lax.fori_loop(0, 2 * half, one, 0)
+
+    @pl.when(jnp.logical_and(giving, second))
+    def _():
+        fill(lambda head: (near_state[head], near_total[head]))
+
+    @pl.when(jnp.logical_and(giving, jnp.logical_not(second)))
+    def _():
+        fill(lambda head: (jnp.zeros_like(state[head]), jnp.zeros_like(total[head])))
+
+    @pl.when(jnp.logical_and(taking, second))
+    def _():
+        fill(
+            lambda head: (
+                far_state[head] + near_state[head],
+                far_total[head] + near_total[head],
+            )
+        )
+
+    @pl.when(jnp.logical_and(taking, jnp.logical_not(second)))
+    def _():
+        fill(lambda head: (far_state[head], far_total[head]))
+
+    yield
+
+
+def normalize(value, gain):
+    return value * lax.rsqrt(jnp.mean(value * value, axis=-1, keepdims=True) + EPS) * gain
+
+
+GRID = (2, 2, 2, 2, 2)
+
+
+def shape(dims, kind):
+    return jax.ShapeDtypeStruct(dims, kind)
+
+
+def padded(columns):
+    return -(-columns // FEATS) * FEATS
+
+
+def front(tokens, gain, wq, wk, wv, wo, gain2, tables, shards3):
+    count, width = tokens.shape
+    heads = wq.shape[1] // KD
+    rows, columns = shards3[0].shape
+    full = padded(columns)
+    half = full // 2
+    tall = rows // 2
+
+    def body(
+        tok, gain, wq, wk, wv, wo, gain2, pick_a, pick_b, table, shard0, shard1, shard2,
+        whole0, whole1, whole2, normed, query, keys, values, mixed, inverse, state, total,
+        middle, low_mlp, near_state, near_total, far_state, far_total, ex_sent, ex_landed,
+        wide, sent, landed, local,
+    ):
+        place = Place()
+        enter(place)
+        wholes = (whole0, whole1, whole2)
+        for spot, shard in enumerate((shard0, shard1, shard2)):
+            wide[spot, :, columns:full] = jnp.zeros((rows, full - columns), BF16)
+            wide[spot, :, 0:columns] = shard[...]
+        clock = Clock()
+        order = 0
+        for part in range(2):
+            for weight in range(3):
+                for kind, first in enumerate("xy"):
+                    run = spread_steps(
+                        wide.at[weight], wholes[weight], pl.ds(kind * tall, tall),
+                        pl.ds(part * half, half), first,
+                        (sent.at[order], landed.at[order], local.at[order]), place,
+                    )
+                    clock.add(run, order)
+                    order += 1
+        clock.tick()
+        clock.tick()
+        project_body(tok, gain, wq, wk, wv, normed, query, keys, values)
+        clock.tick()
+        state_body(keys, values, pick_a, pick_b, table, state, total)
+        swap = exchange_steps(
+            state, total, (near_state, near_total), (far_state, far_total), ex_sent, ex_landed,
+            place, False,
+        )
+        next(swap)
+        clock.tick()
+        next(swap)
+        clock.tick()
+        next(swap)
+        next(swap)
+
+        def between(pair):
+            for spot in (1, 3, 5, 7):
+
+                @pl.when(pair == spot)
+                def _():
+                    clock.tick()
+
+        attend_body(query, keys, values, pick_a, pick_b, table, state, total, mixed, inverse, between)
+        middle[...] = tok[...].astype(F32) + dot(mixed[...], wo[...])
+        clock.tick()
+        low_mlp[...] = normalize(middle[...], gain2[...]).astype(BF16)
+        clock.drain()
+
+    vmem = pl.BlockSpec(memory_space=pltpu.VMEM)
+    free = pl.BlockSpec(memory_space=pl.ANY)
+    states = ((heads, VD, FEATS), BF16), ((heads, 1, FEATS), F32)
+    out_shape = [shape(GRID + (rows, full), BF16)] * 3 + [
+        shape((count, width), BF16),
+        shape((count, heads * KD), BF16),
+        shape((count, heads * KD), BF16),
+        shape((count, heads * VD), BF16),
+        shape((count, heads * VD), BF16),
+        shape((count, heads * VD), F32),
+        shape(*states[0]),
+        shape(*states[1]),
+        shape((count, width), F32),
+        shape((count, width), BF16),
+    ]
+    scratch = [pltpu.VMEM(*entry) for entry in states * 2]
+    scratch += [pltpu.SemaphoreType.DMA((6,))] * 2
+    scratch += [
+        pltpu.VMEM((3, rows, full), BF16),
+        pltpu.SemaphoreType.DMA((12, 5)),
+        pltpu.SemaphoreType.DMA((12, 5)),
+        pltpu.SemaphoreType.DMA((12,)),
+    ]
+    return pl.pallas_call(
+        body,
+        out_shape=out_shape,
+        in_specs=[vmem] * 13,
+        out_specs=[free] * 3 + [vmem] * 10,
+        scratch_shapes=scratch,
+        compiler_params=pltpu.CompilerParams(
+            collective_id=1, has_side_effects=True, vmem_limit_bytes=VMEM_LIMIT
+        ),
+    )(tokens, gain, wq, wk, wv, wo, gain2, *tables, *shards3)
+
+
+def rms_back(value, gain, grad):
+    scale = lax.rsqrt(jnp.mean(value * value, axis=-1, keepdims=True) + EPS)
+    unit = value * scale
+    inner = grad * gain
+    back = scale * (inner - unit * jnp.mean(inner * unit, axis=-1, keepdims=True))
+    return back, jnp.sum(grad * unit, axis=0, keepdims=True)
+
+
+def feed(low_mlp, out_grad, middle, mixed, wo, gain2, wholes):
+    count, width = low_mlp.shape
+    depth = wholes[0].shape[0]
+    full = wholes[0].shape[1]
+    tile = FEATS
+    steps = full // tile
+
+    def body(
+        low, og, mid, mix, wo, gain2, whole0, whole1, whole2,
+        grad0, grad1, grad2, out, d_mixed, d_middle, out_g, gain_part,
+        low_t, og_t, acc_out, acc_back, tiles, made, in_sem, out_sem,
+    ):
+        wholes_in, grads = (whole0, whole1, whole2), (grad0, grad1, grad2)
+
+        def columns(step):
+            return pl.ds(pl.multiple_of(step * tile, tile), tile)
+
+        def load(step, slot):
+            return [
+                pltpu.make_async_copy(ref.at[:, columns(step)], tiles.at[slot, i], in_sem.at[slot, i])
+                for i, ref in enumerate(wholes_in)
+            ]
+
+        def save(step, slot):
+            return [
+                pltpu.make_async_copy(made.at[slot, i], ref.at[:, columns(step)], out_sem.at[slot, i])
+                for i, ref in enumerate(grads)
+            ]
+
+        for copy in load(0, 0):
+            copy.start()
+        low_t[...] = low[...].T
+        og_t[...] = og[...].T
+        acc_out[...] = mid[...]
+        acc_back[...] = jnp.zeros_like(acc_back)
+
+        def step(index, carry):
+            slot = index % 2
+
+            @pl.when(index + 1 < steps)
+            def _():
+                for copy in load(index + 1, 1 - slot):
+                    copy.start()
+
+            for copy in load(index, slot):
+                copy.wait()
+
+            @pl.when(index >= 2)
+            def _():
+                for copy in save(index - 2, slot):
+                    copy.wait()
+
+            gate_w, up_w, down_w = (tiles.at[slot, i] for i in range(3))
+            gate = dot(low[...], gate_w[...])
+            upward = dot(low[...], up_w[...])
+            d_hidden = dot(og[...], down_w[...])
+            sig = 1.0 / (1.0 + jnp.exp(-gate))
+            silu = gate * sig
+            hidden = (silu * upward).astype(BF16)
+            d_gate = (d_hidden * upward * (sig * (1.0 + gate * (1.0 - sig)))).astype(BF16)
+            d_up = (d_hidden * silu).astype(BF16)
+            acc_out[...] += dot_nt(hidden, down_w[...])
+            acc_back[...] += dot_nt(d_gate, gate_w[...]) + dot_nt(d_up, up_w[...])
+            made[slot, 0] = dot(low_t[...], d_gate).astype(BF16)
+            made[slot, 1] = dot(low_t[...], d_up).astype(BF16)
+            made[slot, 2] = dot(og_t[...], hidden).astype(BF16)
+            for copy in save(index, slot):
+                copy.start()
+            return carry
+
+        lax.fori_loop(0, steps, step, 0)
+        out[...] = acc_out[...].astype(BF16)
+        back, part = rms_back(mid[...], gain2[...], acc_back[...])
+        gain_part[...] = part
+        d_middle[...] = og[...].astype(F32) + back
+        branch = d_middle[...].astype(BF16)
+        out_g[...] = dot_tn(mix[...], branch).astype(BF16)
+        d_mixed[...] = dot_nt(branch, wo[...]).astype(BF16)
+        for index in (steps - 2, steps - 1):
+            for copy in save(index, index % 2):
+                copy.wait()
+
+    vmem = pl.BlockSpec(memory_space=pltpu.VMEM)
+    free = pl.BlockSpec(memory_space=pl.ANY)
+    return pl.pallas_call(
+        body,
+        out_shape=[shape((depth, full), BF16)] * 3
+        + [
+            shape((count, width), BF16),
+            shape(mixed.shape, BF16),
+            shape((count, width), F32),
+            shape((mixed.shape[1], width), BF16),
+            shape((1, width), F32),
+        ],
+        in_specs=[vmem] * 6 + [free] * 3,
+        out_specs=[free] * 3 + [vmem] * 5,
+        scratch_shapes=[
+            pltpu.VMEM((width, count), BF16),
+            pltpu.VMEM((width, count), BF16),
+            pltpu.VMEM((count, width), F32),
+            pltpu.VMEM((count, width), F32),
+            pltpu.VMEM((2, 3, depth, tile), BF16),
+            pltpu.VMEM((2, 3, depth, tile), BF16),
+            pltpu.SemaphoreType.DMA((2, 3)),
+            pltpu.SemaphoreType.DMA((2, 3)),
+        ],
+        compiler_params=pltpu.CompilerParams(vmem_limit_bytes=VMEM_LIMIT),
+    )(low_mlp, out_grad, middle, mixed, wo, gain2, *wholes)
+
+
+def back(
+    tokens, gain, normed, query, keys, values, mixed, inverse, d_mixed, d_middle, tables,
+    state, total, wq, wk, wv, gain_part, ff_grads, out_g, columns,
+):
+    count, width = tokens.shape
+    heads = wq.shape[1] // KD
+    full = ff_grads[0].shape[1]
+    half = full // 2
+    rows = width // 32
+    tall = rows // 2
+    heads_wide, narrow = heads * VD, heads * KD
+    late = heads_wide + 2 * narrow
+    kept = 6
+
+    def body(
+        tok, gain, normed, query, keys, values, mixed, inverse, d_mixed, d_middle, pick_a, pick_b,
+        table, state, total, wq, wk, wv, gain_part, ff0, ff1, ff2, out_g,
+        g_ff0, g_ff1, g_ff2, g_out, g_value, g_query, g_keys, g_gain, g_tok,
+        d_state, d_total, near_state, near_total, far_state, far_total, ex_sent, ex_landed,
+        d_query, d_keys, d_values, q_sum, k_sum, v_sum, late_g,
+        gain_mine, gain_slots, gain_sent, gain_landed, *rest,
+    ):
+        ff_refs, out_refs, late_refs, (sent, landed, local) = rest[:6], rest[6:12], rest[12:18], rest[18:]
+        place = Place()
+        enter(place)
+        clock = Clock()
+        order = 0
+
+        def sems(index):
+            return sent.at[index], landed.at[index], local.at[index]
+
+        for part in range(2):
+            for weight, (source, target) in enumerate(zip((ff0, ff1, ff2), (g_ff0, g_ff1, g_ff2))):
+                for kind, first in enumerate("xy"):
+                    here = (part * half, min(columns, (part + 1) * half))
+
+                    def put(value, target=target, kind=kind, here=here):
+                        target[kind * tall : (kind + 1) * tall, here[0] : here[1]] = value[
+                            :, 0 : here[1] - here[0]
+                        ]
+
+                    refs = [ff_refs[0].at[order % kept]] + [ref.at[order] for ref in ff_refs[1:]]
+                    run = reduce_steps(
+                        source, pl.ds(kind * tall, tall), pl.ds(part * half, half), first, refs,
+                        sems(order), place, put,
+                    )
+                    clock.add(run, order)
+                    order += 1
+        for kind, first in enumerate("xy"):
+
+            def put_out(value, kind=kind):
+                g_out[kind * tall : (kind + 1) * tall, :] = value
+
+            run = reduce_steps(
+                out_g, pl.ds(kind * tall, tall), slice(None), first,
+                [ref.at[kind] for ref in out_refs], sems(order), place, put_out,
+            )
+            clock.add(run, order)
+            order += 1
+        clock.tick()
+        back_state_body(query, mixed, inverse, d_mixed, pick_a, pick_b, table, d_state, d_total)
+        swap = exchange_steps(
+            d_state, d_total, (near_state, near_total), (far_state, far_total), ex_sent, ex_landed,
+            place, True,
+        )
+        next(swap)
+        clock.tick()
+        next(swap)
+        clock.tick()
+        next(swap)
+        clock.tick()
+        next(swap)
+
+        def between(pair):
+            for spot in range(heads // 2):
+
+                @pl.when(pair == spot)
+                def _():
+                    clock.tick()
+
+        attend_back_body(
+            query, keys, values, mixed, inverse, d_mixed, pick_a, pick_b, table, state, total,
+            d_state, d_total, d_query, d_keys, d_values, q_sum, k_sum, v_sum, between,
+        )
+        grid = GRID + (rows,)
+        for start, ref in ((0, d_values), (heads_wide, d_query), (heads_wide + narrow, d_keys)):
+            wide = ref.shape[1]
+            late_g[:, :, :, :, :, :, start : start + wide] = (
+                dot_tn(normed[...], ref[...]).astype(BF16).reshape(grid + (wide,))
+            )
+        for kind, first in enumerate("xy"):
+
+            def put_late(value, kind=kind):
+                where = slice(kind * tall, (kind + 1) * tall)
+                g_value[where, :] = value[:, 0:heads_wide]
+                g_query[where, :] = value[:, heads_wide : heads_wide + narrow]
+                g_keys[where, :] = value[:, heads_wide + narrow : late]
+
+            run = reduce_steps(
+                late_g, pl.ds(kind * tall, tall), slice(None), first,
+                [ref.at[kind] for ref in late_refs], sems(order), place, put_late,
+            )
+            clock.add(run)
+            order += 1
+        clock.tick()
+        d_normed = dot_nt(d_query[...], wq[...])
+        d_normed += dot_nt(d_keys[...], wk[...]) + dot_nt(d_values[...], wv[...])
+        value, part = rms_back(tok[...].astype(F32), gain[...], d_normed)
+        g_tok[...] = d_middle[...] + value
+        gain_mine[0] = jnp.concatenate(
+            [part, gain_part[...], jnp.zeros((6, width), F32)], axis=0
+        )
+        clock.add(gain_steps(gain_mine, gain_slots, gain_sent, gain_landed, place))
+        clock.drain()
+        g_gain[...] = gain_mine[5]
+
+    vmem = pl.BlockSpec(memory_space=pltpu.VMEM)
+    free = pl.BlockSpec(memory_space=pl.ANY)
+    states = ((heads, VD, FEATS), BF16), ((heads, 1, FEATS), F32)
+    views = [g.reshape(GRID + (rows, g.shape[1])) for g in (*ff_grads, out_g)]
+    chunks = 16
+    scratch = [pltpu.VMEM(*entry) for entry in states * 3]
+    scratch += [pltpu.SemaphoreType.DMA((6,))] * 2
+    scratch += [
+        pltpu.VMEM((count, narrow), BF16),
+        pltpu.VMEM((count, narrow), BF16),
+        pltpu.VMEM((count, heads_wide), BF16),
+        pltpu.VMEM((count, narrow), F32),
+        pltpu.VMEM((count, narrow), F32),
+        pltpu.VMEM((count, LANES), F32),
+        pltpu.VMEM(GRID + (rows, late), BF16),
+        pltpu.VMEM((6, 8, width), F32),
+        pltpu.VMEM((5, 8, width), F32),
+        pltpu.SemaphoreType.DMA((5,)),
+        pltpu.SemaphoreType.DMA((5,)),
+    ]
+    scratch += reduce_shapes(tall, half, (12,), (kept,))
+    scratch += reduce_shapes(tall, width, (2,))
+    scratch += reduce_shapes(tall, late, (2,))
+    scratch += [
+        pltpu.SemaphoreType.DMA((chunks, 5)),
+        pltpu.SemaphoreType.DMA((chunks, 5)),
+        pltpu.SemaphoreType.DMA((chunks,)),
+    ]
+    return pl.pallas_call(
+        body,
+        out_shape=[shape((rows, columns), F32)] * 3
+        + [
+            shape((rows, width), F32),
+            shape((rows, heads_wide), F32),
+            shape((rows, narrow), F32),
+            shape((rows, narrow), F32),
+            shape((8, width), F32),
+            shape((count, width), F32),
+        ],
+        in_specs=[vmem] * 19 + [free] * 4,
+        out_specs=[vmem] * 9,
+        scratch_shapes=scratch,
+        compiler_params=pltpu.CompilerParams(
+            collective_id=0, has_side_effects=True, vmem_limit_bytes=VMEM_LIMIT
+        ),
+    )(
+        tokens, gain, normed, query, keys, values, mixed, inverse, d_mixed, d_middle, *tables,
+        state, total, wq, wk, wv, gain_part, *views,
+    )
+
+
+def general(
     tokens, attn_gain, w_query, w_key, w_value, w_output, mlp_gain, w_gate, w_up, w_down, out_grad
 ):
     count, width = tokens.shape
@@ -417,6 +1161,49 @@
     )
 
 
+def shards(
+    tokens, attn_gain, w_query, w_key, w_value, w_output, mlp_gain, w_gate, w_up, w_down, out_grad
+):
+    args = (
+        tokens, attn_gain, w_query, w_key, w_value, w_output, mlp_gain, w_gate, w_up, w_down, out_grad
+    )
+    if (lax.axis_size("dp"), lax.axis_size("seq")) != (8, 4):
+        return general(*args)
+    width = tokens.shape[1]
+    tables = feature_tables()
+    gain = attn_gain.astype(F32).reshape(1, width)
+    gain2 = mlp_gain.astype(F32).reshape(1, width)
+    (
+        *wholes, normed, query, keys, values, mixed, inverse, state, total, middle, low_mlp
+    ) = front(
+        tokens, gain, w_query, w_key, w_value, w_output, gain2, tables, (w_gate, w_up, w_down)
+    )
+    wholes = [whole.reshape(width, whole.shape[-1]) for whole in wholes]
+    *ff_grads, layer_out, d_mixed, d_middle, out_g, gain_part = feed(
+        low_mlp, out_grad, middle, mixed, w_output, gain2, wholes
+    )
+    gate_grad, up_grad, down_grad, output_grad, value_grad, query_grad, key_grad, gains, tok_grad = back(
+        tokens, gain, normed, query, keys, values, mixed, inverse, d_mixed, d_middle, tables,
+        state, total, w_query, w_key, w_value, gain_part, ff_grads, out_g, w_gate.shape[1],
+    )
+    share = width // 32
+    own = lax.axis_index("dp") * 4 + lax.axis_index("seq")
+    gains = lax.dynamic_slice(gains, (0, own * share), (2, share))
+    return (
+        layer_out,
+        tok_grad,
+        gains[0],
+        query_grad,
+        key_grad,
+        value_grad,
+        output_grad,
+        gains[1],
+        gate_grad,
+        up_grad,
+        down_grad,
+    )
+
+
 def solution(mesh):
     rows = P(("dp", "seq"), None)
     in_specs = (rows, P(), P(), P(), P(), P(), P(), rows, rows, rows, rows)

time: 767 us -> 307 us (0.40)
  waiting for transfers between devices: 508 us -> 0 us
  Pallas kernels: 73.5 us -> 295 us
  matrix products: 84.6 us -> 0 us
  local copies, waits for them, and re-layouts: 55 us -> 9.3 us
  between operations: 14.7 us -> 0.71 us
  blocking collectives: 12.6 us -> 0 us
  other arithmetic: 11.8 us -> 2.55 us
    unnamed x9 -> x0, waiting for transfers between devices: 309 us -> none
    pallas_call x5 -> x3, Pallas kernels: 73.5 us -> 295 us  [the longest x1 150 us: back(): pl.pallas_call(body, out_shape=[shape((rows, columns), F32)] * 3 + [shape...]
    all_gather x5 -> x0, waiting for transfers between devices: 199 us -> none  [the longest x3 169 us: shards(): lax.all_gather(w, ('dp', 'seq'), axis=0, tiled=True)]
    dot_general x18 -> x0, matrix products: 84.6 us -> none  [the longest x4 33.4 us: dot(): return jnp.dot(left, right, preferred_element_type=F32)]
    unnamed x70 -> x22, local copies, waits for them, and re-layouts: 49 us -> 8.04 us
    all_gather x2 -> x0, blocking collectives: 12.6 us -> none  [the longest x1 6.96 us: shards(): total = before(lax.all_gather(total, 'seq'), 'seq')]
  transfers between devices with their start and end apart: 7 -> 0, of which waited for: 7 -> 0; matrix products, arithmetic and copies ran while one was open for 11% -> 0% of each run, Pallas kernels for 2% -> 0%
where the time goes in v3:
time: 307 us
  Pallas kernels  295 us (96%)
  local copies, waits for them, and re-layouts  9.3 us (3%)
    pallas_call x1, Pallas kernels, back(): pl.pallas_call(body, out_shape=[shape((rows, columns), F32)] * 3 + [shape...  150 us
    pallas_call x1, Pallas kernels, front(): pl.pallas_call(body, out_shape=out_shape, in_specs=[vmem] * 13, out_specs...  104 us
    pallas_call x1, Pallas kernels, feed(): pl.pallas_call(body, out_shape=[shape((depth, full), BF16)] * 3 + [shape(...  40.7 us
    unnamed x22, local copies, waits for them, and re-layouts  8.04 us

profile of v3, /device:TPU:0, one launch (start us, length us, event | category | flops | bytes accessed | tf_op | source)
XLA Modules:
  0.0 307.2 jit_solution(439801629678092459)
XLA Ops:
  0.6 1.3 reshape.64
  1.9 1.3 reshape.66
  3.2 104.5 %shard_map.221 = (bf16[2,2,2,2,2,32,2816]{6,5,4,3,2,1,0:T(8,128)(2,1)}, bf16[2,2,2,2,2,32,2816]{6,5,4,3,2,1,0:T(8,128)(2,1)}, bf16[2,2,2,2,2,32,2816]{6,5,4,3,2,...) custom-call(bf16[512,1024]{1,0:T(8,128)(2,1)} %tok.3, ...), custom_call_target="tpu_custom_call" | custom-call | tf_op jit(solution)/shard_map/pallas_call | solution.py:741
  107.7 40.7 %shard_map.222 = (bf16[1024,2816]{1,0:T(8,128)(2,1)}, bf16[1024,2816]{1,0:T(8,128)(2,1)}, bf16[1024,2816]{1,0:T(8,128)(2,1)}, bf16[512,1024]{1,0:T(8,128)(2,1)},...) custom-call(bf16[512,1024]{1,0:T(8,128)(2,1)} %get-tuple-element.41.low, ...), custom_call_target="tpu_custom_call" | custom-call | tf_op jit(solution)/shard_map/pallas_call | solution.py:845
  148.3 149.6 %shard_map.223 = (f32[32,2752]{1,0:T(8,128)}, f32[32,2752]{1,0:T(8,128)}, f32[32,2752]{1,0:T(8,128)}, f32[32,1024]{1,0:T(8,128)}, f32[32,1024]{1,0:T(8,128)}, /*...) custom-call(bf16[512,1024]{1,0:T(8,128)(2,1)} %tok.3, f32[1,1024]{1,0:T(1,128)} %bitcast.21, ...), custom_call_target="tpu_custom_call" | custom-call | tf_op jit(solution)/shard_map/pallas_call | solution.py:1015
  297.9 0.7 constant_dynamic-slice_fusion
  298.6 0.5 slice_bitcast_fusion
  299.2 0.0 copy-start.6
  299.2 0.0 copy-start.5
  299.2 0.0 copy-start.4
  299.2 0.0 copy-start.3
  299.2 0.0 copy-start.2
  299.2 0.0 copy-start.1
  299.2 0.0 copy-start
  299.2 3.3 %copy.33 = f32[512,1024]{1,0:T(8,128)} copy(f32[512,1024]{1,0:T(8,128)} %get-tuple-element.85) | data formatting | bytes 4194304
  302.5 0.0 copy-done.6
  302.5 0.6 copy.34
  303.1 0.0 copy-done.5
  303.1 0.6 copy.35
  303.7 0.0 copy-done.4
  303.7 0.7 copy.36
  304.4 0.0 copy-done.3
  304.4 0.7 copy.37
  305.0 0.0 copy-done.2
  305.0 0.7 copy.38
  305.8 0.0 copy-done.1
  305.8 0.7 copy.39
  306.5 0.0 copy-done
  306.5 0.7 copy.40
Async XLA Ops:
  299.2 3.3 %copy-start.6 = (f32[32,256]{1,0:T(8,128)S(1)}, f32[32,256]{1,0:T(8,128)}, u32[]{:S(2)}) copy-start(f32[32,256]{1,0:T(8,128)} %get-tuple-element.87) | copy-start | bytes 98308
  299.2 3.9 %copy-start.5 = (f32[32,256]{1,0:T(8,128)S(1)}, f32[32,256]{1,0:T(8,128)}, u32[]{:S(2)}) copy-start(f32[32,256]{1,0:T(8,128)} %get-tuple-element.88) | copy-start | bytes 98308
  299.2 4.5 %copy-start.4 = (f32[32,1024]{1,0:T(8,128)S(1)}, f32[32,1024]{1,0:T(8,128)}, u32[]{:S(2)}) copy-start(f32[32,1024]{1,0:T(8,128)} %get-tuple-element.89) | copy-start | bytes 393220
  299.2 5.2 %copy-start.3 = (f32[32,1024]{1,0:T(8,128)S(1)}, f32[32,1024]{1,0:T(8,128)}, u32[]{:S(2)}) copy-start(f32[32,1024]{1,0:T(8,128)} %get-tuple-element.90) | copy-start | bytes 393220
  299.2 5.8 %copy-start.2 = (f32[32,2752]{1,0:T(8,128)S(1)}, f32[32,2752]{1,0:T(8,128)}, u32[]{:S(2)}) copy-start(f32[32,2752]{1,0:T(8,128)} %get-tuple-element.92) | copy-start | bytes 1056772
  299.2 6.6 %copy-start.1 = (f32[32,2752]{1,0:T(8,128)S(1)}, f32[32,2752]{1,0:T(8,128)}, u32[]{:S(2)}) copy-start(f32[32,2752]{1,0:T(8,128)} %get-tuple-element.93) | copy-start | bytes 1056772
  299.2 7.3 %copy-start = (f32[32,2752]{1,0:T(8,128)S(1)}, f32[32,2752]{1,0:T(8,128)}, u32[]{:S(2)}) copy-start(f32[32,2752]{1,0:T(8,128)} %get-tuple-element.94) | copy-start | bytes 1056772

commit v4 on v1

--- a/solution.py
+++ b/solution.py
@@ -16,7 +16,7 @@
 QUAD = 1.0 / (4.0 * math.sqrt(2.0))
 F32 = jnp.float32
 BF16 = jnp.bfloat16
-VMEM_LIMIT = 58 << 20
+VMEM_LIMIT = 62 << 20
 
 
 def feature_tables():
@@ -89,7 +89,7 @@
     values[...] = dot(normed[...], wv[...]).astype(BF16)
 
 
-def state_body(keys, values, pick_a, pick_b, rows, state, total):
+def state_body(keys, values, pick_a, pick_b, rows, state, total, between=None):
     pairs = values.shape[1] // LANES
     count = keys.shape[0]
 
@@ -102,6 +102,8 @@
             sums = dot(turned[half * VD : (half + 1) * VD, :], feat)
             state[head] = (sums * rows[3:4, :]).astype(BF16)
             total[head] = jnp.sum(feat.astype(F32), axis=0, keepdims=True) * rows[3:4, :]
+        if between is not None:
+            between(pair)
         return carry
 
     lax.fori_loop(0, pairs, step, 0)
@@ -113,7 +115,7 @@
     return row >= column
 
 
-def attend_body(query, keys, values, pick_a, pick_b, rows, state, total, mixed, inverse, block=256):
+def attend_body(query, keys, values, pick_a, pick_b, rows, state, total, mixed, inverse, between=None, block=256):
     pairs = values.shape[1] // LANES
     count = keys.shape[0]
 
@@ -146,12 +148,71 @@
                     invs = jnp.where(mask, invs, flip)
             mixed[start:stop, tile_at(pair)] = numer.astype(BF16)
             inverse[start:stop, tile_at(pair)] = invs
+        if between is not None:
+            between(pair)
         return carry
 
     lax.fori_loop(0, pairs, step, 0)
 
 
-def back_state_body(query, mixed, inverse, d_mixed, pick_a, pick_b, rows, d_state, d_total):
+def attend_inside(query, keys, values, numer, denoms, between, block=256):
+    pairs = values.shape[1] // LANES
+    count = keys.shape[0]
+
+    def step(pair, carry):
+        vals = values[:, tile_at(pair)]
+        for start in range(0, count, block):
+            stop = start + block
+            for half in range(2):
+                head = pair * 2 + half
+                masked = only(head_lanes(block, head % 8), query[start:stop, tile_at(head // 8)])
+                score = dot_nt(masked, keys[0:stop, tile_at(head // 8)]) * 0.25
+                weight = 1.0 + score + 0.5 * score * score
+                weight = jnp.where(causal(block, stop, start, 0), weight, 0.0)
+                flip = jnp.broadcast_to(jnp.sum(weight, axis=1, keepdims=True), (block, LANES))
+                both = dot(weight.astype(BF16), vals[0:stop, :])
+                if half == 0:
+                    whole, wides = both, flip
+                else:
+                    mask = half_lanes(block, 0)
+                    numer[start:stop, tile_at(pair)] = jnp.where(mask, whole, both)
+                    denoms[start:stop, tile_at(pair)] = jnp.where(mask, wides, flip)
+        between(pair)
+        return carry
+
+    lax.fori_loop(0, pairs, step, 0)
+
+
+def attend_before(query, pick_a, pick_b, rows, state, total, numer, inverse, mixed, between):
+    count = query.shape[0]
+    pairs = mixed.shape[1] // LANES
+
+    def step(pair, carry):
+        spot = tile_at(pair)
+        for half in range(2):
+            head = pair * 2 + half
+            masked = only(head_lanes(count, head % 8), query[:, tile_at(head // 8)])
+            feat = features_of(masked, pick_a[...], pick_b[...], rows[...])
+            inter = jnp.sum(feat.astype(F32) * total[head], axis=1, keepdims=True)
+            inter = jnp.broadcast_to(inter, (count, LANES))
+            across = dot_nt(feat, state[head])
+            across = jnp.concatenate([across, across], axis=1)
+            if half == 0:
+                whole, wides = across, inter
+            else:
+                mask = half_lanes(count, 0)
+                whole = jnp.where(mask, whole, across)
+                wides = jnp.where(mask, wides, inter)
+        flipped = 1.0 / (inverse[:, spot] + wides)
+        inverse[:, spot] = flipped
+        mixed[:, spot] = ((numer[:, spot] + whole) * flipped).astype(BF16)
+        between(pair)
+        return carry
+
+    lax.fori_loop(0, pairs, step, 0)
+
+
+def back_state_body(query, mixed, inverse, d_mixed, pick_a, pick_b, rows, d_state, d_total, between=None):
     pairs = mixed.shape[1] // LANES
     count = query.shape[0]
 
@@ -170,6 +231,8 @@
             d_total[head] = (
                 jnp.sum(feat.astype(F32) * d_denom, axis=0, keepdims=True) * rows[3:4, :]
             )
+        if between is not None:
+            between(pair)
         return carry
 
     lax.fori_loop(0, pairs, step, 0)
@@ -202,6 +265,7 @@
     q_sum,
     k_sum,
     v_sum,
+    between=None,
     block=256,
 ):
     pairs = values.shape[1] // LANES
@@ -259,11 +323,105 @@
             q_sum[:, place] += jnp.concatenate(grads_q, axis=0) * 0.25 + only(lanes, inter_q)
             k_sum[:, place] += jnp.concatenate(grads_k, axis=0) * 0.25 + only(lanes, inter_k)
         d_values[:, spot] = v_sum[...].astype(BF16)
+        if between is not None:
+            between(pair)
         return carry
 
     lax.fori_loop(0, pairs, step, 0)
     d_query[...] = q_sum[...].astype(BF16)
     d_keys[...] = k_sum[...].astype(BF16)
+
+
+def attend_back_inside(
+    query, keys, values, mixed, inverse, d_mixed, pick_a, pick_b, rows, state, total, q_sum, k_sum,
+    v_part, between, block=256,
+):
+    pairs = values.shape[1] // LANES
+    count = keys.shape[0]
+    q_sum[...] = jnp.zeros_like(q_sum)
+    k_sum[...] = jnp.zeros_like(k_sum)
+
+    def step(pair, carry):
+        spot = tile_at(pair)
+        d_numer = d_mixed[:, spot].astype(F32) * inverse[:, spot]
+        lost = d_numer * mixed[:, spot].astype(F32)
+        d_low = d_numer.astype(BF16)
+        turned = pltpu.roll(lost, VD, 1)
+        vals = values[:, spot]
+        for half in range(2):
+            head = pair * 2 + half
+            place = tile_at(head // 8)
+            mine = half_lanes(count, half)
+            lanes = head_lanes(count, head % 8)
+            d_denom = -jnp.sum(only(mine, lost), axis=1, keepdims=True)
+            d_wide = jnp.where(mine, d_numer, -turned).astype(BF16)
+            v_wide = jnp.where(mine, vals, jnp.ones_like(vals))
+            q_mask = only(lanes, query[:, place])
+            k_mask = only(lanes, keys[:, place])
+            grads_q, grads_k, grads_v = [], [], []
+            for start in range(0, count, block):
+                stop = start + block
+                score = dot_nt(q_mask[start:stop], k_mask[0:stop]) * 0.25
+                d_weight = dot_nt(d_wide[start:stop], v_wide[0:stop])
+                d_score = only(causal(block, stop, start, 0), d_weight * (1.0 + score))
+                grads_q.append(dot(d_score.astype(BF16), k_mask[0:stop]))
+                rest = count - start
+                score = dot_nt(k_mask[start:stop], q_mask[start:count]) * 0.25
+                mask = (
+                    lax.broadcasted_iota(jnp.int32, (block, rest), 0)
+                    <= lax.broadcasted_iota(jnp.int32, (block, rest), 1)
+                )
+                weight = only(mask, 1.0 + score + 0.5 * score * score)
+                d_weight = dot_nt(v_wide[start:stop], d_wide[start:count])
+                d_score = only(mask, d_weight * (1.0 + score))
+                grads_k.append(dot(d_score.astype(BF16), q_mask[start:count]))
+                grads_v.append(dot(weight.astype(BF16), d_low[start:count]))
+            first, second = halves_of(q_mask, pick_a[...], pick_b[...], rows[...])
+            d_feat = dot(d_low[:, half * VD : (half + 1) * VD], state[head]) + d_denom * total[head]
+            inter_q = feature_back(d_feat, first, second, pick_a[...], pick_b[...], rows[...])
+            whole_v = jnp.concatenate(grads_v, axis=0)
+            v_part[:, spot] = whole_v if half == 0 else jnp.where(mine, whole_v, v_part[:, spot])
+            q_sum[:, place] += jnp.concatenate(grads_q, axis=0) * 0.25 + only(lanes, inter_q)
+            k_sum[:, place] += jnp.concatenate(grads_k, axis=0) * 0.25
+            between(pair, half)
+        return carry
+
+    lax.fori_loop(0, pairs, step, 0)
+
+
+def attend_back_after(
+    keys, values, pick_a, pick_b, rows, d_state, d_total, k_sum, v_part, d_values, between, ended
+):
+    pairs = values.shape[1] // LANES
+    count = keys.shape[0]
+
+    def step(pair, carry):
+        spot = tile_at(pair)
+        vals = values[:, spot]
+        for half in range(2):
+            head = pair * 2 + half
+            place = tile_at(head // 8)
+            lanes = head_lanes(count, head % 8)
+            k_mask = only(lanes, keys[:, place])
+            first, second = halves_of(k_mask, pick_a[...], pick_b[...], rows[...])
+            feat = (first * second * rows[2:3, :]).astype(BF16)
+            d_feat = dot(vals[:, half * VD : (half + 1) * VD], d_state[head]) + d_total[head]
+            inter_k = feature_back(d_feat, first, second, pick_a[...], pick_b[...], rows[...])
+            inter_v = dot_nt(feat, d_state[head])
+            inter_v = jnp.concatenate([inter_v, inter_v], axis=1)
+            k_sum[:, place] += only(lanes, inter_k)
+            whole_v = v_part[:, spot] + inter_v
+            mask = half_lanes(count, half)
+            whole_v = whole_v if half == 0 else jnp.where(mask, whole_v, v_part[:, spot])
+            if half == 0:
+                v_part[:, spot] = jnp.where(mask, whole_v, v_part[:, spot])
+            else:
+                d_values[:, spot] = whole_v.astype(BF16)
+            between(pair, half)
+        ended(pair)
+        return carry
+
+    lax.fori_loop(0, pairs, step, 0)
 
 
 def call(body, shapes, *operands, scratch=()):
@@ -291,7 +449,880 @@
     return jnp.sum(jnp.where(chosen, parts.astype(F32), 0.0), axis=0)
 
 
-def shards(
+MESH_ID = pl.DeviceIdType.MESH
+
+
+class Place:
+    def __init__(self):
+        self.dp, self.seq = lax.axis_index("dp"), lax.axis_index("seq")
+        self.z, self.y = self.dp // 2, self.dp % 2
+        self.x, self.core = self.seq // 2, self.seq % 2
+        self.zh, self.zl = self.z // 2, self.z % 2
+
+    def at(self, z=None, y=None, x=None, core=None):
+        z = self.z if z is None else z
+        y = self.y if y is None else y
+        x = self.x if x is None else x
+        core = self.core if core is None else core
+        return (z * 2 + y, x * 2 + core)
+
+    def mate(self):
+        return self.at(core=1 - self.core)
+
+    def across(self, axis):
+        return self.at(y=1 - self.y) if axis == "y" else self.at(x=1 - self.x)
+
+    def own(self, axis):
+        return self.y if axis == "y" else self.x
+
+
+def remote(source, target, sent, landed, device):
+    return pltpu.make_async_remote_copy(
+        src_ref=source,
+        dst_ref=target,
+        send_sem=sent,
+        recv_sem=landed,
+        device_id=device,
+        device_id_type=MESH_ID,
+    )
+
+
+def enter(place):
+    barrier = pltpu.get_barrier_semaphore()
+    others = [place.mate(), place.across("x"), place.across("y")]
+    for other in (1, 2, 3):
+        others.append(place.at(z=jnp.bitwise_xor(place.z, other)))
+    for device in others:
+        pl.semaphore_signal(barrier, inc=1, device_id=device, device_id_type=MESH_ID)
+    pl.semaphore_wait(barrier, len(others))
+
+
+class Gather:
+    def __init__(self, shard, whole, rows, columns, first, sems, place):
+        self.shard, self.whole, self.rows, self.columns = shard, whole, rows, columns
+        self.first, self.third = first, "x" if first == "y" else "y"
+        self.sems, self.place = sems, place
+
+    def block(self, high, low, one, three, core=None):
+        core = self.place.core if core is None else core
+        grid = (one, three) if self.first == "y" else (three, one)
+        return self.whole.at[(high, low) + grid + (core, self.rows, self.columns)]
+
+    def move(self, ref, spot, device, source=None):
+        sent, landed, _ = self.sems
+        source = ref if source is None else source
+        return remote(source, ref, sent.at[spot], landed.at[spot], device)
+
+    def copies(self):
+        place, every = self.place, slice(None)
+        own1, own3 = place.own(self.first), place.own(self.third)
+        mine = self.shard.at[self.rows, self.columns]
+        block = self.block
+        zh, zl = place.zh, place.zl
+
+        def keep():
+            return pltpu.make_async_copy(mine, block(zh, zl, own1, own3), self.sems[2])
+
+        def far(high):
+            device = place.at(z=jnp.bitwise_xor(place.z, 2))
+            return self.move(block(high, zl, own1, own3), 0, device, mine)
+
+        def cross(three):
+            return self.move(block(every, zl, own1, three), 1, place.across(self.third))
+
+        def near(low):
+            device = place.at(z=jnp.bitwise_xor(place.z, 1))
+            return self.move(block(every, low, own1, every), 2, device)
+
+        def over(one):
+            return self.move(block(every, every, one, every), 3, place.across(self.first))
+
+        def mate(core):
+            return self.move(block(every, every, every, every, core), 4, place.mate())
+
+        return keep, [
+            (far, zh, 1 - zh),
+            (cross, own3, 1 - own3),
+            (near, zl, 1 - zl),
+            (over, own1, 1 - own1),
+            (mate, place.core, 1 - place.core),
+        ]
+
+    def step(self, index):
+        keep, stages = self.copies()
+        if index == 0:
+            keep().start()
+        if index == 1:
+            keep().wait()
+        if index > 0:
+            act, _, theirs = stages[index - 1]
+            act(theirs).wait_recv()
+        if index < 5:
+            act, own, _ = stages[index]
+            act(own).start()
+        else:
+            for act, own, _ in stages:
+                act(own).wait_send()
+
+
+class Pool:
+    def __init__(self, refs, sems, free, place, chunks):
+        self.refs, self.sems, self.free, self.place, self.chunks = refs, sems, free, place, chunks
+        self.kept, self.landing = refs[0].shape[0], refs[1].shape[0]
+
+
+class Chunk:
+    def __init__(self, pool, order, source, rows, columns, first, put):
+        self.pool, self.place, self.put = pool, pool.place, put
+        self.order = order
+        self.source, self.rows, self.columns, self.first = source, rows, columns, first
+        self.third = "x" if first == "y" else "y"
+        self.width = columns.size
+
+    def ref(self, kind):
+        spot = self.order
+        if kind == 0:
+            spot = spot % self.pool.kept
+        if kind == 1:
+            spot = spot % self.pool.landing
+        return self.pool.refs[kind].at[spot]
+
+    def cut(self, ref):
+        return ref.at[(slice(None),) * (len(ref.shape) - 1) + (pl.ds(0, self.width),)]
+
+    def share(self, core):
+        every = slice(None)
+        return self.source.at[every, every, every, every, core, self.rows, self.columns]
+
+    def pick(self, which):
+        mine = self.ref(0)
+        return mine.at[:, :, which] if self.first == "y" else mine.at[:, :, :, which]
+
+    def fetch(self):
+        return pltpu.make_async_copy(
+            self.share(self.place.core), self.cut(self.ref(0)), self.pool.sems[2].at[self.order]
+        )
+
+    def send(self, ref, target, spot, device):
+        sent, landed = self.pool.sems[0].at[self.order, spot], self.pool.sems[1].at[self.order, spot]
+        return remote(ref, self.cut(target), sent, landed, device)
+
+    def to_mate(self):
+        return self.send(self.share(1 - self.place.core), self.ref(1), 0, self.place.mate())
+
+    def to_over(self):
+        own = self.place.own(self.first)
+        return self.send(
+            self.cut(self.pick(1 - own)), self.ref(2), 1, self.place.across(self.first)
+        )
+
+    def to_near(self):
+        place = self.place
+        source = self.cut(self.ref(2).at[:, 1 - place.zl])
+        return self.send(source, self.ref(3), 2, place.at(z=jnp.bitwise_xor(place.z, 1)))
+
+    def to_cross(self):
+        own = self.place.own(self.third)
+        source = self.cut(self.ref(3).at[:, 1 - own])
+        return self.send(source, self.ref(4), 3, self.place.across(self.third))
+
+    def to_far(self):
+        place = self.place
+        source = self.cut(self.ref(4).at[1 - place.zh])
+        return self.send(source, self.ref(5), 4, place.at(z=jnp.bitwise_xor(place.z, 2)))
+
+    def view(self, ref):
+        return self.cut(ref)
+
+    def step(self, index):
+        pool, place, order = self.pool, self.place, self.order
+        if index == 0:
+            if order >= pool.landing:
+                pl.semaphore_wait(pool.free, 1)
+            self.fetch().start()
+            self.to_mate().start()
+        elif index == 1:
+            self.fetch().wait()
+            self.to_mate().wait_recv()
+            mine = self.cut(self.ref(0))
+            mine[...] = mine[...] + self.cut(self.ref(1))[...]
+            if order + pool.landing < pool.chunks:
+                pl.semaphore_signal(
+                    pool.free, inc=1, device_id=place.mate(), device_id_type=MESH_ID
+                )
+            self.to_over().start()
+        elif index == 2:
+            self.to_over().wait()
+            over = self.cut(self.ref(2))
+            over[...] = over[...] + self.cut(self.pick(place.own(self.first)))[...]
+            self.to_near().start()
+        elif index == 3:
+            self.to_near().wait_recv()
+            near = self.cut(self.ref(3))
+            near[...] = near[...] + self.cut(self.ref(2).at[:, place.zl])[...]
+            self.to_cross().start()
+        elif index == 4:
+            self.to_cross().wait_recv()
+            cross = self.cut(self.ref(4))
+            cross[...] = cross[...] + self.cut(self.ref(3).at[:, place.own(self.third)])[...]
+            self.to_far().start()
+        else:
+            self.to_far().wait_recv()
+            final = self.cut(self.ref(4).at[place.zh])[...].astype(F32)
+            self.put(final + self.cut(self.ref(5))[...].astype(F32))
+            self.to_mate().wait_send()
+            self.to_near().wait_send()
+            self.to_cross().wait_send()
+            self.to_far().wait_send()
+
+
+class Gains:
+    def __init__(self, mine, slots, sent, landed, place):
+        self.mine, self.slots, self.sent, self.landed, self.place = mine, slots, sent, landed, place
+
+    def swap(self, spot):
+        place = self.place
+        partner = [
+            place.mate,
+            lambda: place.across("x"),
+            lambda: place.across("y"),
+            lambda: place.at(z=jnp.bitwise_xor(place.z, 1)),
+            lambda: place.at(z=jnp.bitwise_xor(place.z, 2)),
+        ][spot]()
+        return remote(
+            self.mine.at[spot], self.slots.at[spot], self.sent.at[spot], self.landed.at[spot], partner
+        )
+
+    def step(self, index):
+        if index > 0:
+            self.swap(index - 1).wait()
+            self.mine[index] = self.mine[index - 1] + self.slots[index - 1]
+        if index < 5:
+            self.swap(index).start()
+
+
+class Exchange:
+    def __init__(self, state, total, near, far, sent, landed, place, reverse):
+        self.state, self.total, self.near, self.far = state, total, near, far
+        self.sent, self.landed, self.place, self.reverse = sent, landed, place, reverse
+        self.half = state.shape[0] // 2
+
+    def move(self, source, target, spot, device):
+        return remote(source, target, self.sent.at[spot], self.landed.at[spot], device)
+
+    def to_mate(self):
+        pairs = zip((self.state, self.total), self.near)
+        return [self.move(a, b, i, self.place.mate()) for i, (a, b) in enumerate(pairs)]
+
+    def part(self, spot, core, device):
+        part = pl.ds(core * self.half, self.half)
+        return [
+            self.move(ref.at[part], ref.at[part], spot + i, device) for i, ref in enumerate(self.far)
+        ]
+
+    def over(self):
+        return self.part(2, self.place.core, self.place.across("x"))
+
+    def share(self, core):
+        return self.part(4, core, self.place.mate())
+
+    def step(self, index):
+        place, reverse = self.place, self.reverse
+        giving = place.x == (1 if reverse else 0)
+        taking = place.x == (0 if reverse else 1)
+        second = place.core == (0 if reverse else 1)
+        state, total = self.state, self.total
+        (near_state, near_total), (far_state, far_total) = self.near, self.far
+        if index == 0:
+            for copy in self.to_mate():
+                copy.start()
+        elif index == 1:
+            for copy in self.to_mate():
+                copy.wait_recv()
+
+            @pl.when(giving)
+            def _():
+                part = pl.ds(place.core * self.half, self.half)
+                far_state[part] = state[part] + near_state[part]
+                far_total[part] = total[part] + near_total[part]
+                for copy in self.over():
+                    copy.start()
+
+        elif index == 2:
+
+            @pl.when(taking)
+            def _():
+                for copy in self.over():
+                    copy.wait_recv()
+                for copy in self.share(place.core):
+                    copy.start()
+
+        else:
+
+            @pl.when(taking)
+            def _():
+                for copy in self.share(1 - place.core):
+                    copy.wait_recv()
+                for copy in self.share(place.core):
+                    copy.wait_send()
+
+            for copy in self.to_mate():
+                copy.wait_send()
+
+            @pl.when(giving)
+            def _():
+                for copy in self.over():
+                    copy.wait_send()
+
+            @pl.when(jnp.logical_and(giving, second))
+            def _():
+                state[...] = near_state[...]
+                total[...] = near_total[...]
+
+            @pl.when(jnp.logical_and(giving, jnp.logical_not(second)))
+            def _():
+                state[...] = jnp.zeros_like(state)
+                total[...] = jnp.zeros_like(total)
+
+            @pl.when(jnp.logical_and(taking, second))
+            def _():
+                state[...] = far_state[...] + near_state[...]
+                total[...] = far_total[...] + near_total[...]
+
+            @pl.when(jnp.logical_and(taking, jnp.logical_not(second)))
+            def _():
+                state[...] = far_state[...]
+                total[...] = far_total[...]
+
+
+class Work:
+    def __init__(self):
+        self.kinds = ([], [], [], [])
+
+    def pause(self, name):
+        for code in PLAN.get(name, ()):
+            self.kinds[code // 1000][code % 1000 // 10].step(code % 10)
+
+    def between(self, prefix, count, halves=False):
+        def hook(index, half=""):
+            for spot in range(count):
+                name = f"{prefix}{spot}{half}"
+                if name in PLAN:
+
+                    @pl.when(index == spot)
+                    def _():
+                        self.pause(name)
+
+        return hook
+
+
+PLAN = {
+    's': (0, 10, 20, 30, 40,),
+    'qk': (50, 1, 60,),
+    'v': (2, 11, 21,),
+    'st0': (31, 70, 80,),
+    'st1': (41,),
+    'st2': (90,),
+    'st3': (51,),
+    'st4': (12, 61,),
+    'st6': (3,),
+    'st7': (22,),
+    'e0': (2000,),
+    'a0': (71,),
+    'a1': (32, 81, 2001,),
+    'a3': (42,),
+    'a4': (4, 13,),
+    'a5': (52, 23,),
+    'a6': (5,),
+    'a7': (62, 33,),
+    'e0w': (72, 91, 14, 2002, 43, 53, 15, 82, 2003,),
+    'b1': (34,),
+    'b2': (24,),
+    'b3': (63, 100,),
+    'b4': (92,),
+    'b5': (35,),
+    'b6': (25,),
+    'b7': (73,),
+    'po': (54, 110, 120,),
+    'nm': (44, 83, 130,),
+    'p0': (55, 101, 140, 45,),
+    'm0': (74, 93, 150, 160,),
+    't0': (64, 102, 111,),
+    'm1': (75, 121, 131,),
+    't1': (65, 141, 170,),
+    'm2': (84, 151, 94, 161, 112, 122, 85, 103, 95, 132, 171, 113, 142, 123, 152, 104, 133, 105, 162, 114, 143, 172, 115,),
+    't2': (124,),
+    'm3': (153,),
+    't3': (125, 134,),
+    'm4': (163,),
+    't4': (135, 144, 173, 1000, 1010, 1020, 1030,),
+    't5': (145, 154, 1001, 1040,),
+    'm6': (1011, 164, 1050, 1021, 155, 174, 165, 1031, 1002, 175,),
+    't6': (1041,),
+    'm7': (1003, 1012,),
+    't7': (1022, 1051,),
+    'm8': (1013, 1004, 1032,),
+    't8': (1042, 1023, 1060, 1070, 1080, 1090,),
+    'm9': (1005, 1014, 1052,),
+    't9': (1033, 1024, 1061, 1071, 1100, 1110,),
+    'm10': (1015, 1034,),
+    'ft': (1025, 1035, 1043, 1053, 1081, 1072, 1091,),
+    'dm': (1062, 1120, 1130,),
+    'c2': (1044,),
+    'c3': (1054, 1073,),
+    'c5': (1101, 1111,),
+    'c6': (1092,),
+    'c7': (1045,),
+    'e1': (2010,),
+    'og': (1055, 1074, 1082, 1063, 1140, 2011, 1150,),
+    'd01': (1075, 1112,),
+    'd10': (1064, 1083, 1102,),
+    'd11': (1093,),
+    'd20': (1084, 1113,),
+    'd21': (2012, 1065, 1121, 1131, 1160, 1170,),
+    'd30': (2013, 1094, 1085, 1114,),
+    'd31': (1103,),
+    'd40': (1095, 1141, 1151,),
+    'd41': (1115, 1132,),
+    'd50': (1104,),
+    'd51': (1122, 1161, 1180, 1190, 1171,),
+    'd61': (1105, 1142, 1200,),
+    'd70': (1152, 1210,),
+    'd71': (1123, 1133, 1181,),
+    'f00': (1191,),
+    'f01': (1162,),
+    'f11': (1134, 1143, 1153,),
+    'f20': (1124, 1201, 1211,),
+    'f21': (1172,),
+    'la': (1135, 1144, 1154, 1163, 1220, 1230, 1125,),
+    'f41': (1182,),
+    'f50': (1173, 1192, 1221,),
+    'f51': (1145, 1164, 1231,),
+    'f60': (1202, 1155,),
+    'f61': (1174,),
+    'f70': (1183, 1212, 1193,),
+    'lb': (1165, 1203, 1240, 1250,),
+    'dn': (1175, 1184, 1194, 1204, 1213, 1222, 1241, 1251,),
+    'z': (1185, 1195, 1214, 1232, 3000, 1205, 1223, 3001, 1215, 1252, 1242, 3002, 1233, 1224, 3003, 1253, 1234, 1243, 1254, 1225, 3004, 1235, 1244, 1255, 3005, 1245,),
+}
+
+
+def normalize(value, gain):
+    return value * lax.rsqrt(jnp.mean(value * value, axis=-1, keepdims=True) + EPS) * gain
+
+
+GRID = (2, 2, 2, 2, 2)
+PARTS = (3, 7, 11)
+BAND = 128
+TILE = 256
+
+
+def shape(dims, kind):
+    return jax.ShapeDtypeStruct(dims, kind)
+
+
+def padded(columns):
+    return -(-columns // TILE) * TILE
+
+
+def bands(count, act, size=BAND):
+    def step(index, carry):
+        act(pl.ds(pl.multiple_of(index * size, size), size))
+        return carry
+
+    lax.fori_loop(0, count // size, step, 0)
+
+
+def rms_back(value, gain, grad):
+    scale = lax.rsqrt(jnp.mean(value * value, axis=-1, keepdims=True) + EPS)
+    unit = value * scale
+    inner = grad * gain
+    back = scale * (inner - unit * jnp.mean(inner * unit, axis=-1, keepdims=True))
+    return back, jnp.sum(grad * unit, axis=0, keepdims=True)
+
+
+def front_phase(work, r):
+    def norm(band):
+        r.normed[band, :] = normalize(r.tok[band, :].astype(F32), r.gain[...]).astype(BF16)
+
+    bands(r.count, norm)
+    r.query[...] = dot(r.normed[...], r.wq[...]).astype(BF16)
+    r.keys[...] = dot(r.normed[...], r.wk[...]).astype(BF16)
+    work.pause("qk")
+
+    def project(band):
+        r.values[:, band] = dot(r.normed[...], r.wv[:, band]).astype(BF16)
+
+    bands(r.heads * VD, project, TILE)
+    work.pause("v")
+    pairs = r.heads // 2
+    tables = r.pick_a, r.pick_b, r.table
+    state_body(r.keys, r.values, *tables, r.state, r.total, work.between("st", pairs))
+    work.pause("e0")
+    attend_inside(r.query, r.keys, r.values, r.middle, r.inverse, work.between("a", pairs))
+    work.pause("e0w")
+    attend_before(
+        r.query, *tables, r.state, r.total, r.middle, r.inverse, r.mixed, work.between("b", pairs)
+    )
+
+    def project_out(band):
+        r.middle[:, band] = r.tok[:, band].astype(F32) + dot(r.mixed[...], r.wo[:, band])
+
+    bands(r.width, project_out, TILE)
+    work.pause("po")
+
+    def norm_again(band):
+        r.low[band, :] = normalize(r.middle[band, :], r.gain2[...]).astype(BF16)
+
+    bands(r.count, norm_again)
+    work.pause("nm")
+
+
+def feed_phase(work, r, tiles, made, low_t, og_t, acc_out, acc_back, in_sem, out_sem):
+    steps = PARTS[-1]
+
+    def columns(step):
+        return pl.ds(pl.multiple_of(step * TILE, TILE), TILE)
+
+    def load(step, slot):
+        return [
+            pltpu.make_async_copy(ref.at[:, columns(step)], tiles.at[slot, i], in_sem.at[slot, i])
+            for i, ref in enumerate(r.wholes_flat)
+        ]
+
+    def save(step, slot):
+        return [
+            pltpu.make_async_copy(made.at[slot, i], ref.at[:, columns(step)], out_sem.at[slot, i])
+            for i, ref in enumerate(r.grads_flat)
+        ]
+
+    low_t[...] = r.low[...].T
+    og_t[...] = r.og[...].T
+    acc_out[...] = r.middle[...]
+    acc_back[...] = jnp.zeros_like(acc_back)
+    work.pause("p0")
+    for copy in load(0, 0):
+        copy.start()
+    in_tile, after_tile = work.between("m", steps), work.between("t", steps)
+
+    def step(index, carry):
+        slot = index % 2
+        for copy in load(index, slot):
+            copy.wait()
+
+        @pl.when(index >= 1)
+        def _():
+            for copy in save(index - 1, 1 - slot):
+                copy.wait()
+
+        gate_w, up_w, down_w = (tiles.at[slot, i] for i in range(3))
+        gate = dot(r.low[...], gate_w[...])
+        upward = dot(r.low[...], up_w[...])
+        d_hidden = dot(r.og[...], down_w[...])
+        sig = 1.0 / (1.0 + jnp.exp(-gate))
+        silu = gate * sig
+        hidden = (silu * upward).astype(BF16)
+        d_gate = (d_hidden * upward * (sig * (1.0 + gate * (1.0 - sig)))).astype(BF16)
+        d_up = (d_hidden * silu).astype(BF16)
+        acc_out[...] += dot_nt(hidden, down_w[...])
+        in_tile(index)
+
+        @pl.when(index + 1 < steps)
+        def _():
+            for copy in load(index + 1, 1 - slot):
+                copy.start()
+
+        acc_back[...] += dot_nt(d_gate, gate_w[...]) + dot_nt(d_up, up_w[...])
+        made[slot, 0] = dot(low_t[...], d_gate).astype(BF16)
+        made[slot, 1] = dot(low_t[...], d_up).astype(BF16)
+        made[slot, 2] = dot(og_t[...], hidden).astype(BF16)
+        for copy in save(index, slot):
+            copy.start()
+        after_tile(index)
+        return carry
+
+    lax.fori_loop(0, steps, step, 0)
+
+    def store_out(band):
+        r.out[band, :] = acc_out[band, :].astype(BF16)
+
+    bands(r.count, store_out)
+    r.gain_mine[0] = jnp.zeros(r.gain_mine.shape[1:], F32)
+
+    def middle_back(band):
+        value, part = rms_back(r.middle[band, :], r.gain2[...], acc_back[band, :])
+        r.gain_mine[0, 1:2, :] += part
+        value = r.og[band, :].astype(F32) + value
+        r.middle[band, :] = value
+        r.low[band, :] = value.astype(BF16)
+
+    bands(r.count, middle_back)
+    for copy in save(steps - 1, (steps - 1) % 2):
+        copy.wait()
+    work.pause("ft")
+
+    def mixed_back(band):
+        r.d_mixed[:, band] = dot_nt(r.low[...], r.wo[band, :]).astype(BF16)
+
+    bands(r.heads * VD, mixed_back, TILE)
+    work.pause("dm")
+
+
+def back_phase(work, r, d_query, d_keys, d_values, q_sum, k_sum, turned, v_part):
+    heads_wide, narrow = r.heads * VD, r.heads * KD
+    pairs = r.heads // 2
+    tables = r.pick_a, r.pick_b, r.table
+    back_state_body(
+        r.query, r.mixed, r.inverse, r.d_mixed, *tables, r.d_state, r.d_total,
+        work.between("c", pairs),
+    )
+    work.pause("e1")
+    turned[...] = r.mixed[...].T
+
+    def out_grads(band):
+        r.out_g[:, band] = dot(turned[...], r.low[:, band]).astype(BF16)
+
+    bands(r.width, out_grads, TILE)
+    work.pause("og")
+    turned[...] = r.normed[...].T
+    attend_back_inside(
+        r.query, r.keys, r.values, r.mixed, r.inverse, r.d_mixed, *tables, r.state, r.total,
+        q_sum, k_sum, v_part, work.between("d", pairs),
+    )
+    work.pause("e1w")
+    grid = GRID + (r.rows,)
+
+    def late(part):
+        v_wide, narrow_half = heads_wide // 2, narrow // 2
+        base, at = part * r.late, 0
+        q_part = slice(part * narrow_half, (part + 1) * narrow_half)
+        d_query[:, q_part] = q_sum[:, q_part].astype(BF16)
+        d_keys[:, q_part] = k_sum[:, q_part].astype(BF16)
+        for ref, wide in ((d_values, v_wide), (d_query, narrow_half), (d_keys, narrow_half)):
+            for start in range(0, wide, TILE):
+                size = min(TILE, wide - start)
+                low = part * wide + start
+                value = dot(turned[...], ref[:, low : low + size]).astype(BF16)
+                spot = base + at + start
+                r.late_g[:, :, :, :, :, :, spot : spot + size] = value.reshape(grid + (size,))
+            at += wide
+
+    def ended(pair):
+        @pl.when(pair == pairs // 2 - 1)
+        def _():
+            late(0)
+            work.pause("la")
+
+    attend_back_after(
+        r.keys, r.values, *tables, r.d_state, r.d_total, k_sum, v_part, d_values,
+        work.between("f", pairs), ended,
+    )
+    late(1)
+    work.pause("lb")
+
+    def back_norm(band):
+        v_part[:, band] = (
+            dot_nt(d_query[...], r.wq[band, :])
+            + dot_nt(d_keys[...], r.wk[band, :])
+            + dot_nt(d_values[...], r.wv[band, :])
+        )
+
+    bands(r.width, back_norm, TILE)
+    work.pause("dn")
+
+    def tokens_back(band):
+        value, part = rms_back(r.tok[band, :].astype(F32), r.gain[...], v_part[band, :])
+        r.gain_mine[0, 0:1, :] += part
+        r.middle[band, :] = r.middle[band, :] + value
+
+    bands(r.count, tokens_back)
+
+
+class Refs:
+    pass
+
+
+def layer(tokens, gain, wq, wk, wv, wo, gain2, tables, shards3, out_grad):
+    count, width = tokens.shape
+    heads = wq.shape[1] // KD
+    rows, columns = shards3[0].shape
+    full = padded(columns)
+    tall = rows // 2
+    heads_wide, narrow = heads * VD, heads * KD
+    late = heads_wide // 2 + narrow
+    edges = [0] + [part * TILE for part in PARTS]
+    widest = max(late, width // 2, *[high - low for low, high in zip(edges, edges[1:])])
+    chunks = 6 * len(PARTS) + 8
+    gathers = 6 * len(PARTS)
+    states = ((heads, VD, FEATS), BF16), ((heads, 1, FEATS), F32)
+    sem = pltpu.SemaphoreType.DMA
+
+    inputs = dict(
+        tok=tokens, gain=gain, wq=wq, wk=wk, wv=wv, wo=wo, gain2=gain2, pick_a=tables[0],
+        pick_b=tables[1], table=tables[2], shard0=shards3[0], shard1=shards3[1],
+        shard2=shards3[2], og=out_grad,
+    )
+    free_outs = dict(
+        whole0=shape((width, full), BF16), whole1=shape((width, full), BF16),
+        whole2=shape((width, full), BF16), grad0=shape((width, full), BF16),
+        grad1=shape((width, full), BF16), grad2=shape((width, full), BF16),
+    )
+    outs = dict(
+        out=shape((count, width), BF16),
+        middle=shape((count, width), F32),
+        g0=shape((rows, columns), F32), g1=shape((rows, columns), F32),
+        g2=shape((rows, columns), F32), g_out=shape((rows, width), F32),
+        g_value=shape((rows, heads_wide), F32), g_query=shape((rows, narrow), F32),
+        g_keys=shape((rows, narrow), F32), g_gain=shape((8, width), F32),
+    )
+    scratch = dict(
+        normed=pltpu.VMEM((count, width), BF16),
+        query=pltpu.VMEM((count, narrow), BF16),
+        keys=pltpu.VMEM((count, narrow), BF16),
+        values=pltpu.VMEM((count, heads_wide), BF16),
+        mixed=pltpu.VMEM((count, heads_wide), BF16),
+        inverse=pltpu.VMEM((count, heads_wide), F32),
+        state=pltpu.VMEM(*states[0]), total=pltpu.VMEM(*states[1]),
+        d_state=pltpu.VMEM(*states[0]), d_total=pltpu.VMEM(*states[1]),
+        near_state=pltpu.VMEM(*states[0]), near_total=pltpu.VMEM(*states[1]),
+        far_state=pltpu.VMEM(*states[0]), far_total=pltpu.VMEM(*states[1]),
+        ex_sent=sem((6,)), ex_landed=sem((6,)),
+        low=pltpu.VMEM((count, width), BF16),
+        d_mixed=pltpu.VMEM((count, heads_wide), BF16),
+        out_g=pltpu.VMEM((width, width), BF16),
+        late_g=pltpu.VMEM(GRID + (rows, 2 * late), BF16),
+        wide=pltpu.VMEM((3, rows, full), BF16),
+        ag_sent=sem((gathers, 5)), ag_landed=sem((gathers, 5)), ag_local=sem((gathers,)),
+        gain_mine=pltpu.VMEM((6, 8, width), F32),
+        gain_slots=pltpu.VMEM((5, 8, width), F32),
+        gain_sent=sem((5,)), gain_landed=sem((5,)),
+        p0=pltpu.VMEM((6, 2, 2, 2, 2, tall, widest), BF16),
+        p1=pltpu.VMEM((6, 2, 2, 2, 2, tall, widest), BF16),
+        p2=pltpu.VMEM((chunks, 2, 2, 2, tall, widest), BF16),
+        p3=pltpu.VMEM((chunks, 2, 2, tall, widest), BF16),
+        p4=pltpu.VMEM((chunks, 2, tall, widest), BF16),
+        p5=pltpu.VMEM((chunks, tall, widest), BF16),
+        rs_sent=sem((chunks, 5)), rs_landed=sem((chunks, 5)), rs_local=sem((chunks,)),
+        credit=pltpu.SemaphoreType.REGULAR,
+    )
+    names = list(inputs) + list(free_outs) + list(outs) + list(scratch)
+
+    def body(*refs):
+        r = Refs()
+        for name, ref in zip(names, refs):
+            setattr(r, name, ref)
+        r.count, r.width, r.heads, r.rows, r.late = count, width, heads, rows, late
+        r.place = place = Place()
+        r.wholes_flat = [r.whole0, r.whole1, r.whole2]
+        r.grads_flat = [r.grad0, r.grad1, r.grad2]
+        grid = GRID + (rows,)
+        wholes = [ref.reshape(grid + (full,)) for ref in r.wholes_flat]
+        grads = [ref.reshape(grid + (full,)) for ref in r.grads_flat]
+        enter(place)
+        work = Work()
+        gather_list, sum_list, exchange_list, gain_list = work.kinds
+        for spot, shard in enumerate((r.shard0, r.shard1, r.shard2)):
+            r.wide[spot, :, columns:full] = jnp.zeros((rows, full - columns), BF16)
+            r.wide[spot, :, 0:columns] = shard[...]
+        for low, high in zip(edges, edges[1:]):
+            for weight in range(3):
+                for kind, first in enumerate("xy"):
+                    order = len(gather_list)
+                    gather_list.append(
+                        Gather(
+                            r.wide.at[weight], wholes[weight], pl.ds(kind * tall, tall),
+                            pl.ds(low, high - low), first,
+                            (r.ag_sent.at[order], r.ag_landed.at[order], r.ag_local.at[order]), place,
+                        )
+                    )
+        pool = Pool(
+            [r.p0, r.p1, r.p2, r.p3, r.p4, r.p5], (r.rs_sent, r.rs_landed, r.rs_local), r.credit,
+            place, chunks,
+        )
+
+        def sums(source, low, high, target):
+            for kind, first in enumerate("xy"):
+
+                def put(value, kind=kind):
+                    target(slice(kind * tall, (kind + 1) * tall), value)
+
+                chunk_rows, chunk_columns = pl.ds(kind * tall, tall), pl.ds(low, high - low)
+                sum_list.append(
+                    Chunk(pool, len(sum_list), source, chunk_rows, chunk_columns, first, put)
+                )
+
+        def into(ref, low, high):
+            def put(where, value):
+                ref[where, low:high] = value[:, 0 : high - low]
+
+            return put
+
+        for low, high in zip(edges, edges[1:]):
+            for source, target in zip(grads, (r.g0, r.g1, r.g2)):
+                sums(source, low, high, into(target, low, min(high, columns)))
+        half = width // 2
+        for low in (0, half):
+            sums(r.out_g.reshape(grid + (width,)), low, low + half, into(r.g_out, low, low + half))
+        v_wide, narrow_half = heads_wide // 2, narrow // 2
+        for part in range(2):
+
+            def put_late(where, value, part=part):
+                at = 0
+                for ref, wide in ((r.g_value, v_wide), (r.g_query, narrow_half), (r.g_keys, narrow_half)):
+                    ref[where, part * wide : (part + 1) * wide] = value[:, at : at + wide]
+                    at += wide
+
+            sums(r.late_g, part * late, (part + 1) * late, put_late)
+        for state, total, reverse in ((r.state, r.total, False), (r.d_state, r.d_total, True)):
+            exchange_list.append(
+                Exchange(
+                    state, total, (r.near_state, r.near_total), (r.far_state, r.far_total),
+                    r.ex_sent, r.ex_landed, place, reverse,
+                )
+            )
+        gain_list.append(Gains(r.gain_mine, r.gain_slots, r.gain_sent, r.gain_landed, place))
+        work.pause("s")
+        front_phase(work, r)
+        pl.run_scoped(
+            lambda *buffers: feed_phase(work, r, *buffers),
+            pltpu.VMEM((2, 3, width, TILE), BF16),
+            pltpu.VMEM((2, 3, width, TILE), BF16),
+            pltpu.VMEM((width, count), BF16),
+            pltpu.VMEM((width, count), BF16),
+            pltpu.VMEM((count, width), F32),
+            pltpu.VMEM((count, width), F32),
+            sem((2, 3)),
+            sem((2, 3)),
+        )
+        pl.run_scoped(
+            lambda *buffers: back_phase(work, r, *buffers),
+            pltpu.VMEM((count, narrow), BF16),
+            pltpu.VMEM((count, narrow), BF16),
+            pltpu.VMEM((count, heads_wide), BF16),
+            pltpu.VMEM((count, narrow), F32),
+            pltpu.VMEM((count, narrow), F32),
+            pltpu.VMEM((width, count), BF16),
+            pltpu.VMEM((count, width), F32),
+        )
+        work.pause("z")
+        r.g_gain[...] = r.gain_mine[5]
+
+    vmem = pl.BlockSpec(memory_space=pltpu.VMEM)
+    free = pl.BlockSpec(memory_space=pl.ANY)
+    results = pl.pallas_call(
+        body,
+        out_shape=list(free_outs.values()) + list(outs.values()),
+        in_specs=[vmem] * len(inputs),
+        out_specs=[free] * len(free_outs) + [vmem] * len(outs),
+        scratch_shapes=list(scratch.values()),
+        compiler_params=pltpu.CompilerParams(
+            collective_id=0, has_side_effects=True, vmem_limit_bytes=VMEM_LIMIT
+        ),
+    )(*inputs.values())
+    return results[len(free_outs) :]
+
+
+def general(
     tokens, attn_gain, w_query, w_key, w_value, w_output, mlp_gain, w_gate, w_up, w_down, out_grad
 ):
     count, width = tokens.shape
@@ -417,6 +1448,43 @@
     )
 
 
+def shards(
+    tokens, attn_gain, w_query, w_key, w_value, w_output, mlp_gain, w_gate, w_up, w_down, out_grad
+):
+    args = (
+        tokens, attn_gain, w_query, w_key, w_value, w_output, mlp_gain, w_gate, w_up, w_down, out_grad
+    )
+    if (lax.axis_size("dp"), lax.axis_size("seq")) != (8, 4):
+        return general(*args)
+    width = tokens.shape[1]
+    tables = feature_tables()
+    gain = attn_gain.astype(F32).reshape(1, width)
+    gain2 = mlp_gain.astype(F32).reshape(1, width)
+    (
+        layer_out, tok_grad, gate_grad, up_grad, down_grad, output_grad, value_grad, query_grad,
+        key_grad, gains,
+    ) = layer(
+        tokens, gain, w_query, w_key, w_value, w_output, gain2, tables, (w_gate, w_up, w_down),
+        out_grad,
+    )
+    share = width // 32
+    own = lax.axis_index("dp") * 4 + lax.axis_index("seq")
+    gains = lax.dynamic_slice(gains, (0, own * share), (2, share))
+    return (
+        layer_out,
+        tok_grad,
+        gains[0],
+        query_grad,
+        key_grad,
+        value_grad,
+        output_grad,
+        gains[1],
+        gate_grad,
+        up_grad,
+        down_grad,
+    )
+
+
 def solution(mesh):
     rows = P(("dp", "seq"), None)
     in_specs = (rows, P(), P(), P(), P(), P(), P(), rows, rows, rows, rows)

time: 767 us -> 225 us (0.29)
  waiting for transfers between devices: 508 us -> 0 us
  Pallas kernels: 73.5 us -> 210 us
  matrix products: 84.6 us -> 0 us
  local copies, waits for them, and re-layouts: 55 us -> 11.6 us
  between operations: 14.7 us -> 0.72 us
  blocking collectives: 12.6 us -> 0 us
  other arithmetic: 11.8 us -> 2.55 us
    unnamed x9 -> x0, waiting for transfers between devices: 309 us -> none
    all_gather x5 -> x0, waiting for transfers between devices: 199 us -> none  [the longest x3 169 us: shards(): lax.all_gather(w, ('dp', 'seq'), axis=0, tiled=True)]
    pallas_call x5 -> x1, Pallas kernels: 73.5 us -> 210 us  [layer(): pl.pallas_call(body, out_shape=list(free_outs.values()) + list(outs.value...]
    dot_general x18 -> x0, matrix products: 84.6 us -> none  [the longest x4 33.4 us: dot(): return jnp.dot(left, right, preferred_element_type=F32)]
    unnamed x70 -> x23, local copies, waits for them, and re-layouts: 49 us -> 10.2 us
    all_gather x2 -> x0, blocking collectives: 12.6 us -> none  [the longest x1 6.96 us: shards(): total = before(lax.all_gather(total, 'seq'), 'seq')]
  transfers between devices with their start and end apart: 7 -> 0, of which waited for: 7 -> 0; matrix products, arithmetic and copies ran while one was open for 11% -> 0% of each run, Pallas kernels for 2% -> 0%
where the time goes in v4:
time: 225 us
  Pallas kernels  210 us (93%)
  local copies, waits for them, and re-layouts  11.6 us (5%)
  other arithmetic  2.55 us (1%)
    pallas_call x1, Pallas kernels, layer(): pl.pallas_call(body, out_shape=list(free_outs.values()) + list(outs.value...  210 us
    unnamed x23, local copies, waits for them, and re-layouts  10.2 us

profile of v4, /device:TPU:0, one launch (start us, length us, event | category | flops | bytes accessed | tf_op | source)
XLA Modules:
  0.0 224.5 jit_solution(5365122288589547622)
XLA Ops:
  0.6 1.3 reshape.36
  1.9 1.3 reshape.38
  3.2 209.7 %shard_map.221 = (bf16[1024,2816]{1,0:T(8,128)(2,1)}, bf16[1024,2816]{1,0:T(8,128)(2,1)}, bf16[1024,2816]{1,0:T(8,128)(2,1)}, bf16[1024,2816]{1,0:T(8,128)(2,1)}...) custom-call(bf16[512,1024]{1,0:T(8,128)(2,1)} %refs_0_.1, ...), custom_call_target="tpu_custom_call" | custom-call | tf_op jit(solution)/shard_map/pallas_call | solution.py:1312
  212.9 0.0 copy-start.6
  212.9 0.0 copy-start.5
  212.9 0.0 copy-start.4
  212.9 0.0 copy-start.3
  212.9 0.0 copy-start.2
  213.0 0.0 copy-start.1
  213.0 0.0 copy-start
  213.0 0.9 constant_dynamic-slice_fusion
  213.8 0.5 slice_bitcast_fusion
  214.3 2.3 %copy.34 = bf16[512,1024]{1,0:T(8,128)(2,1)} copy(bf16[512,1024]{1,0:T(8,128)(2,1)} %get-tuple-element.44) | data formatting | bytes 2097152
  216.6 3.2 %copy.35 = f32[512,1024]{1,0:T(8,128)} copy(f32[512,1024]{1,0:T(8,128)} %get-tuple-element.45) | data formatting | bytes 4194304
  219.8 0.0 copy-done.6
  219.8 0.6 copy.36
  220.4 0.0 copy-done.5
  220.4 0.6 copy.37
  221.0 0.0 copy-done.4
  221.0 0.7 copy.38
  221.7 0.0 copy-done.3
  221.7 0.7 copy.39
  222.3 0.0 copy-done.2
  222.3 0.7 copy.40
  223.1 0.0 copy-done.1
  223.1 0.7 copy.41
  223.8 0.0 copy-done
  223.8 0.7 copy.42
Async XLA Ops:
  212.9 6.9 %copy-start.6 = (f32[32,256]{1,0:T(8,128)S(1)}, f32[32,256]{1,0:T(8,128)}, u32[]{:S(2)}) copy-start(f32[32,256]{1,0:T(8,128)} %get-tuple-element.47) | copy-start | bytes 98308
  212.9 7.5 %copy-start.5 = (f32[32,256]{1,0:T(8,128)S(1)}, f32[32,256]{1,0:T(8,128)}, u32[]{:S(2)}) copy-start(f32[32,256]{1,0:T(8,128)} %get-tuple-element.48) | copy-start | bytes 98308
  212.9 8.1 %copy-start.4 = (f32[32,1024]{1,0:T(8,128)S(1)}, f32[32,1024]{1,0:T(8,128)}, u32[]{:S(2)}) copy-start(f32[32,1024]{1,0:T(8,128)} %get-tuple-element.49) | copy-start | bytes 393220
  212.9 8.7 %copy-start.3 = (f32[32,1024]{1,0:T(8,128)S(1)}, f32[32,1024]{1,0:T(8,128)}, u32[]{:S(2)}) copy-start(f32[32,1024]{1,0:T(8,128)} %get-tuple-element.50) | copy-start | bytes 393220
  212.9 9.4 %copy-start.2 = (f32[32,2752]{1,0:T(8,128)S(1)}, f32[32,2752]{1,0:T(8,128)}, u32[]{:S(2)}) copy-start(f32[32,2752]{1,0:T(8,128)} %get-tuple-element.52) | copy-start | bytes 1056772
  213.0 10.1 %copy-start.1 = (f32[32,2752]{1,0:T(8,128)S(1)}, f32[32,2752]{1,0:T(8,128)}, u32[]{:S(2)}) copy-start(f32[32,2752]{1,0:T(8,128)} %get-tuple-element.53) | copy-start | bytes 1056772
  213.0 10.8 %copy-start = (f32[32,2752]{1,0:T(8,128)S(1)}, f32[32,2752]{1,0:T(8,128)}, u32[]{:S(2)}) copy-start(f32[32,2752]{1,0:T(8,128)} %get-tuple-element.54) | copy-start | bytes 1056772

commit v5 on v4

--- a/solution.py
+++ b/solution.py
@@ -1,3 +1,4 @@
+import functools
 import math
 
 import jax
@@ -383,7 +384,7 @@
             v_part[:, spot] = whole_v if half == 0 else jnp.where(mine, whole_v, v_part[:, spot])
             q_sum[:, place] += jnp.concatenate(grads_q, axis=0) * 0.25 + only(lanes, inter_q)
             k_sum[:, place] += jnp.concatenate(grads_k, axis=0) * 0.25
-            between(pair, half)
+        between(pair)
         return carry
 
     lax.fori_loop(0, pairs, step, 0)
@@ -417,7 +418,7 @@
                 v_part[:, spot] = jnp.where(mask, whole_v, v_part[:, spot])
             else:
                 d_values[:, spot] = whole_v.astype(BF16)
-            between(pair, half)
+        between(pair)
         ended(pair)
         return carry
 
@@ -489,9 +490,8 @@
 
 def enter(place):
     barrier = pltpu.get_barrier_semaphore()
-    others = [place.mate(), place.across("x"), place.across("y")]
-    for other in (1, 2, 3):
-        others.append(place.at(z=jnp.bitwise_xor(place.z, other)))
+    others = [(place.dp, jnp.bitwise_xor(place.seq, other)) for other in range(1, 4)]
+    others += [(jnp.bitwise_xor(place.dp, other), place.seq) for other in range(1, 8)]
     for device in others:
         pl.semaphore_signal(barrier, inc=1, device_id=device, device_id_type=MESH_ID)
     pl.semaphore_wait(barrier, len(others))
@@ -680,25 +680,29 @@
     def __init__(self, mine, slots, sent, landed, place):
         self.mine, self.slots, self.sent, self.landed, self.place = mine, slots, sent, landed, place
 
-    def swap(self, spot):
+    def swaps(self, index):
         place = self.place
-        partner = [
-            place.mate,
-            lambda: place.across("x"),
-            lambda: place.across("y"),
-            lambda: place.at(z=jnp.bitwise_xor(place.z, 1)),
-            lambda: place.at(z=jnp.bitwise_xor(place.z, 2)),
-        ][spot]()
-        return remote(
-            self.mine.at[spot], self.slots.at[spot], self.sent.at[spot], self.landed.at[spot], partner
-        )
+        if index == 0:
+            partners = [(place.dp, jnp.bitwise_xor(place.seq, k)) for k in range(1, 4)]
+        else:
+            partners = [(jnp.bitwise_xor(place.dp, k), place.seq) for k in range(1, 8)]
+        for spot, partner in enumerate(partners):
+            spot += 3 * index
+            yield spot, remote(
+                self.mine.at[index], self.slots.at[spot], self.sent.at[spot], self.landed.at[spot],
+                partner,
+            )
 
     def step(self, index):
         if index > 0:
-            self.swap(index - 1).wait()
-            self.mine[index] = self.mine[index - 1] + self.slots[index - 1]
-        if index < 5:
-            self.swap(index).start()
+            value = self.mine[index - 1]
+            for spot, swap in self.swaps(index - 1):
+                swap.wait()
+                value = value + self.slots[spot]
+            self.mine[index] = value
+        if index < 2:
+            for _, swap in self.swaps(index):
+                swap.start()
 
 
 class Exchange:
@@ -817,93 +821,81 @@
 
 
 PLAN = {
-    's': (0, 10, 20, 30, 40,),
-    'qk': (50, 1, 60,),
-    'v': (2, 11, 21,),
-    'st0': (31, 70, 80,),
-    'st1': (41,),
-    'st2': (90,),
-    'st3': (51,),
-    'st4': (12, 61,),
-    'st6': (3,),
-    'st7': (22,),
+    's': (0, 10, 20,),
+    'qk': (30,),
+    'v': (40, 1, 50,),
+    'st1': (60,),
+    'st2': (11,),
+    'st3': (70,),
+    'st4': (21,),
+    'st5': (2,),
+    'st6': (31,),
     'e0': (2000,),
-    'a0': (71,),
-    'a1': (32, 81, 2001,),
-    'a3': (42,),
-    'a4': (4, 13,),
-    'a5': (52, 23,),
-    'a6': (5,),
-    'a7': (62, 33,),
-    'e0w': (72, 91, 14, 2002, 43, 53, 15, 82, 2003,),
-    'b1': (34,),
-    'b2': (24,),
-    'b3': (63, 100,),
-    'b4': (92,),
-    'b5': (35,),
-    'b6': (25,),
-    'b7': (73,),
-    'po': (54, 110, 120,),
-    'nm': (44, 83, 130,),
-    'p0': (55, 101, 140, 45,),
-    'm0': (74, 93, 150, 160,),
-    't0': (64, 102, 111,),
-    'm1': (75, 121, 131,),
-    't1': (65, 141, 170,),
-    'm2': (84, 151, 94, 161, 112, 122, 85, 103, 95, 132, 171, 113, 142, 123, 152, 104, 133, 105, 162, 114, 143, 172, 115,),
-    't2': (124,),
-    'm3': (153,),
-    't3': (125, 134,),
-    'm4': (163,),
-    't4': (135, 144, 173, 1000, 1010, 1020, 1030,),
-    't5': (145, 154, 1001, 1040,),
-    'm6': (1011, 164, 1050, 1021, 155, 174, 165, 1031, 1002, 175,),
-    't6': (1041,),
-    'm7': (1003, 1012,),
-    't7': (1022, 1051,),
-    'm8': (1013, 1004, 1032,),
-    't8': (1042, 1023, 1060, 1070, 1080, 1090,),
-    'm9': (1005, 1014, 1052,),
-    't9': (1033, 1024, 1061, 1071, 1100, 1110,),
-    'm10': (1015, 1034,),
-    'ft': (1025, 1035, 1043, 1053, 1081, 1072, 1091,),
-    'dm': (1062, 1120, 1130,),
-    'c2': (1044,),
-    'c3': (1054, 1073,),
-    'c5': (1101, 1111,),
-    'c6': (1092,),
-    'c7': (1045,),
+    'a0': (41,),
+    'a1': (12, 51,),
+    'a2': (2001, 61,),
+    'a4': (22,),
+    'a6': (3,),
+    'a7': (32,),
+    'e0w': (13, 42, 2002, 71, 2003, 52,),
+    'b0': (23,),
+    'b2': (33,),
+    'b3': (62,),
+    'b4': (4,),
+    'b5': (14,),
+    'b6': (72,),
+    'b7': (43,),
+    'po': (5, 15, 53, 80,),
+    'p0': (34, 90, 100, 24, 63, 110, 120, 73, 35, 25, 130, 140, 54, 150, 81, 44, 91, 160, 101, 170, 111, 55, 45,),
+    'm0': (121, 131,),
+    't0': (64, 74, 141,),
+    'm1': (82, 92, 151, 161,),
+    't1': (171,),
+    'm2': (65, 75, 102,),
+    'm3': (83, 112, 93, 122, 132, 103, 142, 113, 84, 152, 123, 94, 162, 85, 133, 95, 172, 104, 143, 114, 153, 105, 124, 163, 115,),
+    't3': (134,),
+    'm4': (125, 173, 1000, 1010, 1020, 1030,),
+    't4': (135, 144,),
+    'm5': (154, 1001, 1040,),
+    't5': (1011, 164, 1021,),
+    'm6': (1031,),
+    't6': (145, 174,),
+    'm7': (155, 1041, 165, 1002, 1050, 175,),
+    't7': (1012,),
+    'm8': (1051, 1060,),
+    'm9': (1003, 1022, 1061, 1070, 1032, 1080,),
+    'm10': (1013, 1071,),
+    't10': (1042, 1081, 1090,),
+    'ft': (1023, 1052, 1100,),
+    'dm': (1004, 1091,),
+    'c1': (1033, 1062, 1110,),
+    'c2': (1014, 1101,),
+    'c4': (1043, 1072, 1120,),
+    'c5': (1005, 1111, 1024,),
     'e1': (2010,),
-    'og': (1055, 1074, 1082, 1063, 1140, 2011, 1150,),
-    'd01': (1075, 1112,),
-    'd10': (1064, 1083, 1102,),
-    'd11': (1093,),
-    'd20': (1084, 1113,),
-    'd21': (2012, 1065, 1121, 1131, 1160, 1170,),
-    'd30': (2013, 1094, 1085, 1114,),
-    'd31': (1103,),
-    'd40': (1095, 1141, 1151,),
-    'd41': (1115, 1132,),
-    'd50': (1104,),
-    'd51': (1122, 1161, 1180, 1190, 1171,),
-    'd61': (1105, 1142, 1200,),
-    'd70': (1152, 1210,),
-    'd71': (1123, 1133, 1181,),
-    'f00': (1191,),
-    'f01': (1162,),
-    'f11': (1134, 1143, 1153,),
-    'f20': (1124, 1201, 1211,),
-    'f21': (1172,),
-    'la': (1135, 1144, 1154, 1163, 1220, 1230, 1125,),
-    'f41': (1182,),
-    'f50': (1173, 1192, 1221,),
-    'f51': (1145, 1164, 1231,),
-    'f60': (1202, 1155,),
-    'f61': (1174,),
-    'f70': (1183, 1212, 1193,),
-    'lb': (1165, 1203, 1240, 1250,),
-    'dn': (1175, 1184, 1194, 1204, 1213, 1222, 1241, 1251,),
-    'z': (1185, 1195, 1214, 1232, 3000, 1205, 1223, 3001, 1215, 1252, 1242, 3002, 1233, 1224, 3003, 1253, 1234, 1243, 1254, 1225, 3004, 1235, 1244, 1255, 3005, 1245,),
+    'og': (2011, 1015, 1034, 1082, 1130,),
+    'd0': (1025, 1044, 1035, 1053, 1063, 1092, 1140,),
+    'd1': (1045, 1073, 1083, 1102, 1121, 1131, 1150,),
+    'd2': (2012, 1064, 1084, 1093, 1112, 1160,),
+    'd3': (2013, 1065, 1085, 1054, 1074, 1103, 1132, 1141, 1151, 1161,),
+    'd4': (1055, 1094, 1104, 1122, 1170, 1180,),
+    'd5': (1075, 1113, 1095, 1133, 1152, 1142, 1171, 1181, 1190, 1200,),
+    'd6': (1105, 1123, 1191,),
+    'd7': (1114, 1134, 1143, 1153, 1162, 1172, 1201, 1210,),
+    'lq': (1220,),
+    'f0': (1182, 1230,),
+    'f1': (1115, 1124, 1135, 1154, 1211, 1221,),
+    'f2': (1163,),
+    'f3': (1192, 1144, 1231,),
+    'l1': (1173, 1222, 1240,),
+    'f4': (1183, 1202, 1250,),
+    'f5': (1125, 1174, 1155, 1241,),
+    'f6': (1184, 1193, 1212, 1251, 1145,),
+    'l2': (1164, 1223, 1260, 1270,),
+    'f7': (1203, 1232,),
+    'l3': (1175, 1261, 1242, 1185, 1271, 1280, 1290,),
+    'dn': (1165, 1194, 1204, 1224, 1213, 1233, 1252, 1262, 1243, 1281, 1291, 1272,),
+    'z': (1195, 1205, 1225, 1214, 1234, 1244, 3000, 1282, 1292, 1253, 3001, 1263, 1273, 1254, 1215, 1264, 1235, 1245, 1274, 1283, 1293, 3002, 1284, 1294, 1255, 1265, 1275, 1285, 1295,),
 }
 
 
@@ -912,7 +904,7 @@
 
 
 GRID = (2, 2, 2, 2, 2)
-PARTS = (3, 7, 11)
+PARTS = (4, 8, 11)
 BAND = 128
 TILE = 256
 
@@ -942,10 +934,13 @@
 
 
 def front_phase(work, r):
+    r.ready("tok")
+
     def norm(band):
-        r.normed[band, :] = normalize(r.tok[band, :].astype(F32), r.gain[...]).astype(BF16)
+        r.normed[band, :] = normalize(r.tok[band, :].astype(F32), r.gain_row[...]).astype(BF16)
 
     bands(r.count, norm)
+    r.ready("wq", "wk", "wv", "og", "wo")
     r.query[...] = dot(r.normed[...], r.wq[...]).astype(BF16)
     r.keys[...] = dot(r.normed[...], r.wk[...]).astype(BF16)
     work.pause("qk")
@@ -972,7 +967,7 @@
     work.pause("po")
 
     def norm_again(band):
-        r.low[band, :] = normalize(r.middle[band, :], r.gain2[...]).astype(BF16)
+        r.low[band, :] = normalize(r.middle[band, :], r.gain2_row[...]).astype(BF16)
 
     bands(r.count, norm_again)
     work.pause("nm")
@@ -1010,10 +1005,12 @@
         for copy in load(index, slot):
             copy.wait()
 
-        @pl.when(index >= 1)
+        crossing = functools.reduce(jnp.logical_or, [index + 1 == edge for edge in PARTS])
+
+        @pl.when(jnp.logical_not(crossing))
         def _():
-            for copy in save(index - 1, 1 - slot):
-                copy.wait()
+            for copy in load(index + 1, 1 - slot):
+                copy.start()
 
         gate_w, up_w, down_w = (tiles.at[slot, i] for i in range(3))
         gate = dot(r.low[...], gate_w[...])
@@ -1025,9 +1022,15 @@
         d_gate = (d_hidden * upward * (sig * (1.0 + gate * (1.0 - sig)))).astype(BF16)
         d_up = (d_hidden * silu).astype(BF16)
         acc_out[...] += dot_nt(hidden, down_w[...])
+
+        @pl.when(index >= 1)
+        def _():
+            for copy in save(index - 1, 1 - slot):
+                copy.wait()
+
         in_tile(index)
 
-        @pl.when(index + 1 < steps)
+        @pl.when(jnp.logical_and(crossing, index + 1 < steps))
         def _():
             for copy in load(index + 1, 1 - slot):
                 copy.start()
@@ -1047,11 +1050,12 @@
         r.out[band, :] = acc_out[band, :].astype(BF16)
 
     bands(r.count, store_out)
-    r.gain_mine[0] = jnp.zeros(r.gain_mine.shape[1:], F32)
+    r.ends[0]().start()
+    r.gain_sum[...] = jnp.zeros(r.gain_sum.shape, F32)
 
     def middle_back(band):
-        value, part = rms_back(r.middle[band, :], r.gain2[...], acc_back[band, :])
-        r.gain_mine[0, 1:2, :] += part
+        value, part = rms_back(r.middle[band, :], r.gain2_row[...], acc_back[band, :])
+        r.gain_sum[1:2, :] += part
         value = r.og[band, :].astype(F32) + value
         r.middle[band, :] = value
         r.low[band, :] = value.astype(BF16)
@@ -1091,34 +1095,38 @@
     )
     work.pause("e1w")
     grid = GRID + (r.rows,)
-
-    def late(part):
-        v_wide, narrow_half = heads_wide // 2, narrow // 2
-        base, at = part * r.late, 0
-        q_part = slice(part * narrow_half, (part + 1) * narrow_half)
-        d_query[:, q_part] = q_sum[:, q_part].astype(BF16)
-        d_keys[:, q_part] = k_sum[:, q_part].astype(BF16)
-        for ref, wide in ((d_values, v_wide), (d_query, narrow_half), (d_keys, narrow_half)):
-            for start in range(0, wide, TILE):
-                size = min(TILE, wide - start)
-                low = part * wide + start
-                value = dot(turned[...], ref[:, low : low + size]).astype(BF16)
-                spot = base + at + start
+    late_refs = dict(q=(d_query, q_sum), k=(d_keys, k_sum), v=(d_values, None))
+
+    def late(index):
+        spot = sum(high - low for group in r.late_groups[:index] for _, low, high in group)
+        for name, low, high in r.late_groups[index]:
+            ref, wide = late_refs[name]
+            if wide is not None:
+                ref[:, low:high] = wide[:, low:high].astype(BF16)
+            for start in range(low, high, TILE):
+                stop = min(start + TILE, high)
+                value = dot(turned[...], ref[:, start:stop]).astype(BF16)
+                size = stop - start
                 r.late_g[:, :, :, :, :, :, spot : spot + size] = value.reshape(grid + (size,))
-            at += wide
+                spot += size
+
+    late(0)
+    work.pause("lq")
 
     def ended(pair):
-        @pl.when(pair == pairs // 2 - 1)
-        def _():
-            late(0)
-            work.pause("la")
+        for spot, index in ((pairs // 2 - 1, 1), (pairs - 2, 2)):
+
+            @pl.when(pair == spot)
+            def _(index=index):
+                late(index)
+                work.pause(f"l{index}")
 
     attend_back_after(
         r.keys, r.values, *tables, r.d_state, r.d_total, k_sum, v_part, d_values,
         work.between("f", pairs), ended,
     )
-    late(1)
-    work.pause("lb")
+    late(3)
+    work.pause("l3")
 
     def back_norm(band):
         v_part[:, band] = (
@@ -1131,11 +1139,18 @@
     work.pause("dn")
 
     def tokens_back(band):
-        value, part = rms_back(r.tok[band, :].astype(F32), r.gain[...], v_part[band, :])
-        r.gain_mine[0, 0:1, :] += part
+        value, part = rms_back(r.tok[band, :].astype(F32), r.gain_row[...], v_part[band, :])
+        r.gain_sum[0:1, :] += part
         r.middle[band, :] = r.middle[band, :] + value
 
     bands(r.count, tokens_back)
+    quarter = r.width // 4
+    for which in range(2):
+        for part in range(4):
+            spot = 4 * which + part
+            r.gain_mine[0, spot : spot + 1, :] = r.gain_sum[
+                which : which + 1, part * quarter : (part + 1) * quarter
+            ]
 
 
 class Refs:
@@ -1149,33 +1164,47 @@
     full = padded(columns)
     tall = rows // 2
     heads_wide, narrow = heads * VD, heads * KD
-    late = heads_wide // 2 + narrow
+    last = heads_wide - 2 * VD
+    late_groups = (
+        (("q", 0, narrow),),
+        (("v", 0, heads_wide // 2), ("k", 0, narrow // 2)),
+        (("v", heads_wide // 2, last),),
+        (("v", last, heads_wide), ("k", narrow // 2, narrow)),
+    )
+    late_sizes = [sum(high - low for _, low, high in group) for group in late_groups]
     edges = [0] + [part * TILE for part in PARTS]
-    widest = max(late, width // 2, *[high - low for low, high in zip(edges, edges[1:])])
-    chunks = 6 * len(PARTS) + 8
+    widest = max(*late_sizes, width // 2, *[high - low for low, high in zip(edges, edges[1:])])
+    chunks = 6 * len(PARTS) + 4 + 2 * len(late_groups)
     gathers = 6 * len(PARTS)
     states = ((heads, VD, FEATS), BF16), ((heads, 1, FEATS), F32)
     sem = pltpu.SemaphoreType.DMA
 
-    inputs = dict(
-        tok=tokens, gain=gain, wq=wq, wk=wk, wv=wv, wo=wo, gain2=gain2, pick_a=tables[0],
-        pick_b=tables[1], table=tables[2], shard0=shards3[0], shard1=shards3[1],
-        shard2=shards3[2], og=out_grad,
+    loads = dict(
+        shard0=shards3[0], shard1=shards3[1], shard2=shards3[2], tok=tokens, wq=wq, wk=wk, wv=wv,
+        og=out_grad, wo=wo,
+    )
+    inputs = {name + "_in": value for name, value in loads.items()}
+    inputs |= dict(
+        gain=gain, gain2=gain2, pick_a=tables[0], pick_b=tables[1], table=tables[2]
     )
     free_outs = dict(
         whole0=shape((width, full), BF16), whole1=shape((width, full), BF16),
         whole2=shape((width, full), BF16), grad0=shape((width, full), BF16),
         grad1=shape((width, full), BF16), grad2=shape((width, full), BF16),
+        out_end=shape((count, width), BF16), tok_end=shape((count, width), F32),
     )
     outs = dict(
-        out=shape((count, width), BF16),
-        middle=shape((count, width), F32),
         g0=shape((rows, columns), F32), g1=shape((rows, columns), F32),
         g2=shape((rows, columns), F32), g_out=shape((rows, width), F32),
         g_value=shape((rows, heads_wide), F32), g_query=shape((rows, narrow), F32),
-        g_keys=shape((rows, narrow), F32), g_gain=shape((8, width), F32),
-    )
-    scratch = dict(
+        g_keys=shape((rows, narrow), F32), g_gain=shape((8, width // 4), F32),
+    )
+    scratch = {name: pltpu.VMEM(value.shape, value.dtype) for name, value in loads.items()}
+    scratch |= dict(
+        out=pltpu.VMEM((count, width), BF16),
+        middle=pltpu.VMEM((count, width), F32),
+        load_sem=sem((len(loads),)), end_sem=sem((2,)),
+        gain_row=pltpu.VMEM((1, width), F32), gain2_row=pltpu.VMEM((1, width), F32),
         normed=pltpu.VMEM((count, width), BF16),
         query=pltpu.VMEM((count, narrow), BF16),
         keys=pltpu.VMEM((count, narrow), BF16),
@@ -1190,14 +1219,15 @@
         low=pltpu.VMEM((count, width), BF16),
         d_mixed=pltpu.VMEM((count, heads_wide), BF16),
         out_g=pltpu.VMEM((width, width), BF16),
-        late_g=pltpu.VMEM(GRID + (rows, 2 * late), BF16),
+        late_g=pltpu.VMEM(GRID + (rows, sum(late_sizes)), BF16),
         wide=pltpu.VMEM((3, rows, full), BF16),
         ag_sent=sem((gathers, 5)), ag_landed=sem((gathers, 5)), ag_local=sem((gathers,)),
-        gain_mine=pltpu.VMEM((6, 8, width), F32),
-        gain_slots=pltpu.VMEM((5, 8, width), F32),
-        gain_sent=sem((5,)), gain_landed=sem((5,)),
-        p0=pltpu.VMEM((6, 2, 2, 2, 2, tall, widest), BF16),
-        p1=pltpu.VMEM((6, 2, 2, 2, 2, tall, widest), BF16),
+        gain_sum=pltpu.VMEM((8, width), F32),
+        gain_mine=pltpu.VMEM((3, 8, width // 4), F32),
+        gain_slots=pltpu.VMEM((10, 8, width // 4), F32),
+        gain_sent=sem((10,)), gain_landed=sem((10,)),
+        p0=pltpu.VMEM((5, 2, 2, 2, 2, tall, widest), BF16),
+        p1=pltpu.VMEM((4, 2, 2, 2, 2, tall, widest), BF16),
         p2=pltpu.VMEM((chunks, 2, 2, 2, tall, widest), BF16),
         p3=pltpu.VMEM((chunks, 2, 2, tall, widest), BF16),
         p4=pltpu.VMEM((chunks, 2, tall, widest), BF16),
@@ -1211,15 +1241,31 @@
         r = Refs()
         for name, ref in zip(names, refs):
             setattr(r, name, ref)
-        r.count, r.width, r.heads, r.rows, r.late = count, width, heads, rows, late
+        r.count, r.width, r.heads, r.rows = count, width, heads, rows
+        r.late_groups = late_groups
         r.place = place = Place()
         r.wholes_flat = [r.whole0, r.whole1, r.whole2]
         r.grads_flat = [r.grad0, r.grad1, r.grad2]
         grid = GRID + (rows,)
         wholes = [ref.reshape(grid + (full,)) for ref in r.wholes_flat]
         grads = [ref.reshape(grid + (full,)) for ref in r.grads_flat]
+        def load(name):
+            spot = list(loads).index(name)
+            source = getattr(r, name + "_in")
+            return pltpu.make_async_copy(source, getattr(r, name), r.load_sem.at[spot])
+
+        r.ready = lambda *wanted: [load(name).wait() for name in wanted]
+        r.ends = [
+            lambda: pltpu.make_async_copy(r.out, r.out_end, r.end_sem.at[0]),
+            lambda: pltpu.make_async_copy(r.middle, r.tok_end, r.end_sem.at[1]),
+        ]
+        for name in loads:
+            load(name).start()
         enter(place)
         work = Work()
+        r.gain_row[...] = r.gain[...].astype(F32).reshape(1, width)
+        r.gain2_row[...] = r.gain2[...].astype(F32).reshape(1, width)
+        r.ready("shard0", "shard1", "shard2")
         gather_list, sum_list, exchange_list, gain_list = work.kinds
         for spot, shard in enumerate((r.shard0, r.shard1, r.shard2)):
             r.wide[spot, :, columns:full] = jnp.zeros((rows, full - columns), BF16)
@@ -1240,8 +1286,8 @@
             place, chunks,
         )
 
-        def sums(source, low, high, target):
-            for kind, first in enumerate("xy"):
+        def sums(source, low, high, target, firsts="xy"):
+            for kind, first in enumerate(firsts):
 
                 def put(value, kind=kind):
                     target(slice(kind * tall, (kind + 1) * tall), value)
@@ -1262,17 +1308,20 @@
                 sums(source, low, high, into(target, low, min(high, columns)))
         half = width // 2
         for low in (0, half):
-            sums(r.out_g.reshape(grid + (width,)), low, low + half, into(r.g_out, low, low + half))
-        v_wide, narrow_half = heads_wide // 2, narrow // 2
-        for part in range(2):
-
-            def put_late(where, value, part=part):
+            target = into(r.g_out, low, low + half)
+            sums(r.out_g.reshape(grid + (width,)), low, low + half, target, "yy")
+        late_ends = dict(q=r.g_query, k=r.g_keys, v=r.g_value)
+        spot = 0
+        for group, size in zip(late_groups, late_sizes):
+
+            def put_late(where, value, group=group):
                 at = 0
-                for ref, wide in ((r.g_value, v_wide), (r.g_query, narrow_half), (r.g_keys, narrow_half)):
-                    ref[where, part * wide : (part + 1) * wide] = value[:, at : at + wide]
-                    at += wide
-
-            sums(r.late_g, part * late, (part + 1) * late, put_late)
+                for name, low, high in group:
+                    late_ends[name][where, low:high] = value[:, at : at + high - low]
+                    at += high - low
+
+            sums(r.late_g, spot, spot + size, put_late)
+            spot += size
         for state, total, reverse in ((r.state, r.total, False), (r.d_state, r.d_total, True)):
             exchange_list.append(
                 Exchange(
@@ -1304,22 +1353,57 @@
             pltpu.VMEM((width, count), BF16),
             pltpu.VMEM((count, width), F32),
         )
+        r.ends[1]().start()
         work.pause("z")
-        r.g_gain[...] = r.gain_mine[5]
+        r.ends[0]().wait()
+        r.ends[1]().wait()
+        r.g_gain[...] = r.gain_mine[2]
 
     vmem = pl.BlockSpec(memory_space=pltpu.VMEM)
     free = pl.BlockSpec(memory_space=pl.ANY)
     results = pl.pallas_call(
         body,
         out_shape=list(free_outs.values()) + list(outs.values()),
-        in_specs=[vmem] * len(inputs),
+        in_specs=[free] * len(loads) + [vmem] * 5,
         out_specs=[free] * len(free_outs) + [vmem] * len(outs),
         scratch_shapes=list(scratch.values()),
         compiler_params=pltpu.CompilerParams(
             collective_id=0, has_side_effects=True, vmem_limit_bytes=VMEM_LIMIT
         ),
     )(*inputs.values())
-    return results[len(free_outs) :]
+    return results[6:]
+
+
+def hand_over(results, gains):
+    quarter = gains.shape[1]
+    share = quarter // 8
+    count = len(results)
+
+    def body(*refs):
+        sources, gain, targets = refs[:count], refs[count], refs[count + 1 : 2 * count + 1]
+        first, second, sems = refs[2 * count + 1 :]
+        copies = [
+            pltpu.make_async_copy(a, b, sems.at[i]) for i, (a, b) in enumerate(zip(sources, targets))
+        ]
+        for copy in copies:
+            copy.start()
+        own = lax.axis_index("dp") * 4 + lax.axis_index("seq")
+        turned = pltpu.roll(gain[...], lax.rem(quarter - own % 8 * share, quarter), 1)[:, 0:share]
+        row = lax.broadcasted_iota(jnp.int32, turned.shape, 0)
+        for ref, start in ((first, 0), (second, 4)):
+            ref[...] = jnp.sum(only(row == start + own // 8, turned), axis=0, keepdims=True)
+        for copy in copies:
+            copy.wait()
+
+    vmem = pl.BlockSpec(memory_space=pltpu.VMEM)
+    free = pl.BlockSpec(memory_space=pl.ANY)
+    return pl.pallas_call(
+        body,
+        out_shape=[shape(value.shape, value.dtype) for value in results] + [shape((1, share), F32)] * 2,
+        in_specs=[vmem] * (count + 1),
+        out_specs=[free] * count + [vmem] * 2,
+        scratch_shapes=[pltpu.SemaphoreType.DMA((count,))],
+    )(*results, gains)
 
 
 def general(
@@ -1456,29 +1540,21 @@
     )
     if (lax.axis_size("dp"), lax.axis_size("seq")) != (8, 4):
         return general(*args)
-    width = tokens.shape[1]
-    tables = feature_tables()
-    gain = attn_gain.astype(F32).reshape(1, width)
-    gain2 = mlp_gain.astype(F32).reshape(1, width)
-    (
-        layer_out, tok_grad, gate_grad, up_grad, down_grad, output_grad, value_grad, query_grad,
-        key_grad, gains,
-    ) = layer(
-        tokens, gain, w_query, w_key, w_value, w_output, gain2, tables, (w_gate, w_up, w_down),
-        out_grad,
-    )
-    share = width // 32
-    own = lax.axis_index("dp") * 4 + lax.axis_index("seq")
-    gains = lax.dynamic_slice(gains, (0, own * share), (2, share))
+    *results, gains = layer(
+        tokens, attn_gain, w_query, w_key, w_value, w_output, mlp_gain, feature_tables(),
+        (w_gate, w_up, w_down), out_grad,
+    )
+    *results, gain_grad, gain2_grad = hand_over(results, gains)
+    layer_out, tok_grad, gate_grad, up_grad, down_grad, output_grad, value_grad, query_grad, key_grad = results
     return (
         layer_out,
         tok_grad,
-        gains[0],
+        gain_grad.reshape(-1),
         query_grad,
         key_grad,
         value_grad,
         output_grad,
-        gains[1],
+        gain2_grad.reshape(-1),
         gate_grad,
         up_grad,
         down_grad,

time: 225 us -> 202 us (0.90)
  local copies, waits for them, and re-layouts: 11.6 us -> 0 us
  Pallas kernels: 210 us -> 201 us
  other arithmetic: 2.55 us -> 0 us
    pallas_call x1, Pallas kernels: 210 us -> 196 us  [layer(): pl.pallas_call(body, out_shape=list(free_outs.values()) + list(outs.value...]
    unnamed x23 -> x0, local copies, waits for them, and re-layouts: 10.2 us -> none
    pallas_call x0 -> x1, Pallas kernels: none -> 4.96 us  [hand_over(): pl.pallas_call(body, out_shape=[shape(value.shape, value.dtype) for value...]
    reshape x2 -> x0, other arithmetic: 2.55 us -> none  [the longest x1 1.28 us: shards(): gain = attn_gain.astype(F32).reshape(1, width)]
where the time goes in v5:
time: 202 us
  Pallas kernels  201 us (100%)
    pallas_call x1, Pallas kernels, layer(): pl.pallas_call(body, out_shape=list(free_outs.values()) + list(outs.value...  196 us
    pallas_call x1, Pallas kernels, hand_over(): pl.pallas_call(body, out_shape=[shape(value.shape, value.dtype) for value...  4.96 us

profile of v5, /device:TPU:0, one launch (start us, length us, event | category | flops | bytes accessed | tf_op | source)
XLA Modules:
  0.0 201.8 jit_solution(3963246726918465001)
XLA Ops:
  0.6 196.0 %shard_map.221 = (bf16[1024,2816]{1,0:T(8,128)(2,1)}, bf16[1024,2816]{1,0:T(8,128)(2,1)}, bf16[1024,2816]{1,0:T(8,128)(2,1)}, bf16[1024,2816]{1,0:T(8,128)(2,1)}...) custom-call(bf16[32,2752]{1,0:T(8,128)(2,1)} %refs_0_.1, ...), custom_call_target="tpu_custom_call" | custom-call | tf_op jit(solution)/shard_map/pallas_call | solution.py:1364
  196.6 5.0 %shard_map.222 = (bf16[512,1024]{1,0:T(8,128)(2,1)}, f32[512,1024]{1,0:T(8,128)}, f32[32,2752]{1,0:T(8,128)}, f32[32,2752]{1,0:T(8,128)}, f32[32,2752]{1,0:T(8,1...) custom-call(bf16[512,1024]{1,0:T(8,128)(2,1)} %get-tuple-element.32., ...), custom_call_target="tpu_custom_call" | custom-call | tf_op jit(solution)/shard_map/pallas_call | solution.py:1400

commit v6 on v5

--- a/solution.py
+++ b/solution.py
@@ -156,7 +156,33 @@
     lax.fori_loop(0, pairs, step, 0)
 
 
-def attend_inside(query, keys, values, numer, denoms, between, block=256):
+def spare_lane(rows, spot):
+    lane = lax.broadcasted_iota(jnp.int32, (rows, LANES), 1)
+    return lane == lax.rem(spot * KD + KD, LANES)
+
+
+def query_side(value, spot):
+    rows = value.shape[0]
+    quarter = only(head_lanes(rows, spot), value * 0.25)
+    return jnp.where(spare_lane(rows, spot), jnp.ones_like(value), quarter)
+
+
+def key_side(value, spot):
+    return jnp.where(spare_lane(value.shape[0], spot), jnp.ones_like(value), value)
+
+
+def triangle(value, start, block, upper=False):
+    row = lax.broadcasted_iota(jnp.int32, (block, block), 0)
+    column = lax.broadcasted_iota(jnp.int32, (block, block), 1)
+    keep = row <= column if upper else row >= column
+    pieces = [value[:, 0:start]] if start > 0 else []
+    pieces.append(only(keep, value[:, start : start + block]))
+    if start + block < value.shape[1]:
+        pieces.append(value[:, start + block :])
+    return jnp.concatenate(pieces, axis=1) if len(pieces) > 1 else pieces[0]
+
+
+def attend_inside(query, keys, values, numer, denoms, between, block=512):
     pairs = values.shape[1] // LANES
     count = keys.shape[0]
 
@@ -166,10 +192,11 @@
             stop = start + block
             for half in range(2):
                 head = pair * 2 + half
-                masked = only(head_lanes(block, head % 8), query[start:stop, tile_at(head // 8)])
-                score = dot_nt(masked, keys[0:stop, tile_at(head // 8)]) * 0.25
-                weight = 1.0 + score + 0.5 * score * score
-                weight = jnp.where(causal(block, stop, start, 0), weight, 0.0)
+                place = tile_at(head // 8)
+                plus = dot_nt(
+                    query_side(query[start:stop, place], head % 8), key_side(keys[0:stop, place], head % 8)
+                )
+                weight = triangle(0.5 * plus * plus + 0.5, start, block)
                 flip = jnp.broadcast_to(jnp.sum(weight, axis=1, keepdims=True), (block, LANES))
                 both = dot(weight.astype(BF16), vals[0:stop, :])
                 if half == 0:
@@ -335,7 +362,7 @@
 
 def attend_back_inside(
     query, keys, values, mixed, inverse, d_mixed, pick_a, pick_b, rows, state, total, q_sum, k_sum,
-    v_part, between, block=256,
+    v_part, between, block=512,
 ):
     pairs = values.shape[1] // LANES
     count = keys.shape[0]
@@ -354,36 +381,40 @@
             place = tile_at(head // 8)
             mine = half_lanes(count, half)
             lanes = head_lanes(count, head % 8)
-            d_denom = -jnp.sum(only(mine, lost), axis=1, keepdims=True)
             d_wide = jnp.where(mine, d_numer, -turned).astype(BF16)
             v_wide = jnp.where(mine, vals, jnp.ones_like(vals))
-            q_mask = only(lanes, query[:, place])
-            k_mask = only(lanes, keys[:, place])
+            q_tile, k_tile = query[:, place], keys[:, place]
+            q_mask = only(lanes, q_tile)
+            q_quarter, k_quarter = q_mask * 0.25, only(lanes, k_tile) * 0.25
+            q_plus, k_plus = query_side(q_tile, head % 8), key_side(k_tile, head % 8)
             grads_q, grads_k, grads_v = [], [], []
             for start in range(0, count, block):
                 stop = start + block
-                score = dot_nt(q_mask[start:stop], k_mask[0:stop]) * 0.25
+                plus = dot_nt(q_plus[start:stop], k_plus[0:stop])
                 d_weight = dot_nt(d_wide[start:stop], v_wide[0:stop])
-                d_score = only(causal(block, stop, start, 0), d_weight * (1.0 + score))
-                grads_q.append(dot(d_score.astype(BF16), k_mask[0:stop]))
-                rest = count - start
-                score = dot_nt(k_mask[start:stop], q_mask[start:count]) * 0.25
-                mask = (
-                    lax.broadcasted_iota(jnp.int32, (block, rest), 0)
-                    <= lax.broadcasted_iota(jnp.int32, (block, rest), 1)
-                )
-                weight = only(mask, 1.0 + score + 0.5 * score * score)
+                d_score = triangle(d_weight * plus, start, block)
+                grads_q.append(dot(d_score.astype(BF16), k_quarter[0:stop]))
+                plus = dot_nt(k_plus[start:stop], q_plus[start:count])
+                weight = triangle(0.5 * plus * plus + 0.5, 0, block, True)
                 d_weight = dot_nt(v_wide[start:stop], d_wide[start:count])
-                d_score = only(mask, d_weight * (1.0 + score))
-                grads_k.append(dot(d_score.astype(BF16), q_mask[start:count]))
+                d_score = triangle(d_weight * plus, 0, block, True)
+                grads_k.append(dot(d_score.astype(BF16), q_quarter[start:count]))
                 grads_v.append(dot(weight.astype(BF16), d_low[start:count]))
             first, second = halves_of(q_mask, pick_a[...], pick_b[...], rows[...])
-            d_feat = dot(d_low[:, half * VD : (half + 1) * VD], state[head]) + d_denom * total[head]
+            high = total[head].astype(BF16)
+            rest = (total[head] - high.astype(F32)).astype(BF16)
+            sums = [jnp.broadcast_to(part, (VD, FEATS)) for part in (high, rest)]
+            zero = jnp.zeros((VD, FEATS), BF16)
+            own = [state[head], sums[0]], [zero, sums[1]]
+            order = [part for group in own for part in (group if half == 0 else group[::-1])]
+            d_feat = dot(
+                jnp.concatenate([d_wide, d_wide], axis=1), jnp.concatenate(order, axis=0)
+            )
             inter_q = feature_back(d_feat, first, second, pick_a[...], pick_b[...], rows[...])
             whole_v = jnp.concatenate(grads_v, axis=0)
             v_part[:, spot] = whole_v if half == 0 else jnp.where(mine, whole_v, v_part[:, spot])
-            q_sum[:, place] += jnp.concatenate(grads_q, axis=0) * 0.25 + only(lanes, inter_q)
-            k_sum[:, place] += jnp.concatenate(grads_k, axis=0) * 0.25
+            q_sum[:, place] += jnp.concatenate(grads_q, axis=0) + only(lanes, inter_q)
+            k_sum[:, place] += jnp.concatenate(grads_k, axis=0)
         between(pair)
         return carry
 
@@ -821,81 +852,78 @@
 
 
 PLAN = {
-    's': (0, 10, 20,),
-    'qk': (30,),
-    'v': (40, 1, 50,),
-    'st1': (60,),
-    'st2': (11,),
-    'st3': (70,),
-    'st4': (21,),
-    'st5': (2,),
-    'st6': (31,),
+    's': (0, 10,),
+    'qk': (20,),
+    'v': (30,),
+    'st0': (1, 40,),
+    'st2': (11, 50,),
+    'st4': (21, 60,),
+    'st6': (2, 31,),
     'e0': (2000,),
     'a0': (41,),
-    'a1': (12, 51,),
-    'a2': (2001, 61,),
+    'a1': (51,),
+    'a2': (2001, 12, 61,),
     'a4': (22,),
-    'a6': (3,),
     'a7': (32,),
-    'e0w': (13, 42, 2002, 71, 2003, 52,),
-    'b0': (23,),
-    'b2': (33,),
-    'b3': (62,),
-    'b4': (4,),
-    'b5': (14,),
-    'b6': (72,),
-    'b7': (43,),
-    'po': (5, 15, 53, 80,),
-    'p0': (34, 90, 100, 24, 63, 110, 120, 73, 35, 25, 130, 140, 54, 150, 81, 44, 91, 160, 101, 170, 111, 55, 45,),
-    'm0': (121, 131,),
-    't0': (64, 74, 141,),
-    'm1': (82, 92, 151, 161,),
-    't1': (171,),
-    'm2': (65, 75, 102,),
-    'm3': (83, 112, 93, 122, 132, 103, 142, 113, 84, 152, 123, 94, 162, 85, 133, 95, 172, 104, 143, 114, 153, 105, 124, 163, 115,),
-    't3': (134,),
-    'm4': (125, 173, 1000, 1010, 1020, 1030,),
-    't4': (135, 144,),
-    'm5': (154, 1001, 1040,),
-    't5': (1011, 164, 1021,),
-    'm6': (1031,),
-    't6': (145, 174,),
-    'm7': (155, 1041, 165, 1002, 1050, 175,),
-    't7': (1012,),
-    'm8': (1051, 1060,),
-    'm9': (1003, 1022, 1061, 1070, 1032, 1080,),
+    'e0w': (3, 13, 2002, 42, 2003,),
+    'b0': (23, 52,),
+    'b4': (4, 14, 43, 62,),
+    'b7': (33, 70,),
+    'po': (5, 15, 80,),
+    'nm': (90,),
+    'p0': (24, 63, 100, 110, 53, 44, 120, 25, 130, 34, 140, 45, 71, 150, 91, 81, 160, 35, 111, 170, 64, 101, 131, 72, 121, 54, 151, 141, 65, 161, 82, 171, 55,),
+    't0': (73, 92,),
+    't1': (83, 102,),
+    't2': (93, 112,),
+    'm3': (122, 74, 103, 132, 84, 113, 75, 142, 123, 94, 85, 152, 133, 162, 104, 95, 143, 172, 114, 105, 153, 124, 163, 115,),
+    't3': (125, 134,),
+    'm4': (144, 173, 1000, 1010, 1020, 1030,),
+    't4': (135,),
+    'm5': (145, 154,),
+    't5': (164, 1001, 1011, 1040,),
+    'm6': (1021,),
+    't6': (174, 1031,),
+    'm7': (155, 165, 1041, 175,),
+    't7': (1002, 1012, 1050,),
+    'm8': (1060,),
+    't8': (1051,),
+    'm9': (1003, 1061, 1022, 1070,),
+    't9': (1032, 1080,),
     'm10': (1013, 1071,),
-    't10': (1042, 1081, 1090,),
-    'ft': (1023, 1052, 1100,),
-    'dm': (1004, 1091,),
-    'c1': (1033, 1062, 1110,),
-    'c2': (1014, 1101,),
-    'c4': (1043, 1072, 1120,),
-    'c5': (1005, 1111, 1024,),
+    't10': (1023, 1081,),
+    'ft': (1042, 1052, 1090, 1100,),
+    'dm': (1004, 1033,),
+    'c0': (1091,),
+    'c1': (1101,),
+    'c2': (1043, 1062, 1110,),
+    'c4': (1014, 1072, 1120,),
+    'c5': (1053, 1024, 1111,),
+    'c6': (1005,),
+    'c7': (1121,),
     'e1': (2010,),
-    'og': (2011, 1015, 1034, 1082, 1130,),
-    'd0': (1025, 1044, 1035, 1053, 1063, 1092, 1140,),
-    'd1': (1045, 1073, 1083, 1102, 1121, 1131, 1150,),
-    'd2': (2012, 1064, 1084, 1093, 1112, 1160,),
-    'd3': (2013, 1065, 1085, 1054, 1074, 1103, 1132, 1141, 1151, 1161,),
-    'd4': (1055, 1094, 1104, 1122, 1170, 1180,),
-    'd5': (1075, 1113, 1095, 1133, 1152, 1142, 1171, 1181, 1190, 1200,),
-    'd6': (1105, 1123, 1191,),
-    'd7': (1114, 1134, 1143, 1153, 1162, 1172, 1201, 1210,),
-    'lq': (1220,),
-    'f0': (1182, 1230,),
-    'f1': (1115, 1124, 1135, 1154, 1211, 1221,),
-    'f2': (1163,),
-    'f3': (1192, 1144, 1231,),
-    'l1': (1173, 1222, 1240,),
-    'f4': (1183, 1202, 1250,),
-    'f5': (1125, 1174, 1155, 1241,),
-    'f6': (1184, 1193, 1212, 1251, 1145,),
-    'l2': (1164, 1223, 1260, 1270,),
-    'f7': (1203, 1232,),
-    'l3': (1175, 1261, 1242, 1185, 1271, 1280, 1290,),
-    'dn': (1165, 1194, 1204, 1224, 1213, 1233, 1252, 1262, 1243, 1281, 1291, 1272,),
-    'z': (1195, 1205, 1225, 1214, 1234, 1244, 3000, 1282, 1292, 1253, 3001, 1263, 1273, 1254, 1215, 1264, 1235, 1245, 1274, 1283, 1293, 3002, 1284, 1294, 1255, 1265, 1275, 1285, 1295,),
+    'og': (2011, 1015, 1063, 1082, 1130,),
+    'd0': (1025, 1034, 1044, 1092, 1131, 1140,),
+    'd1': (1035, 1073, 1083, 1102, 1054, 1112, 1045, 1141, 1150, 1160,),
+    'd2': (1064, 1093, 1151, 1161, 1122, 1170,),
+    'd3': (1055, 1084, 1103, 1132, 1171, 1180,),
+    'd4': (2012, 1065, 1074, 1113, 1123, 1152, 1181,),
+    'd5': (2013, 1075, 1085, 1104, 1133, 1142, 1190, 1200,),
+    'd6': (1105, 1094, 1124, 1153, 1172, 1191, 1201, 1143,),
+    'd7': (1095, 1125, 1114, 1134, 1162, 1182, 1210,),
+    'lq': (1154, 1192, 1220, 1230,),
+    'f0': (1173, 1211,),
+    'f1': (1115, 1202, 1135, 1221, 1231,),
+    'f2': (1144, 1174, 1163,),
+    'f3': (1183, 1222, 1212,),
+    'l1': (1155, 1240, 1250, 1232,),
+    'f4': (1164, 1184, 1193, 1203,),
+    'f5': (1145, 1241, 1251,),
+    'f6': (1175, 1194, 1204, 1223,),
+    'l2': (1213, 1260, 1270,),
+    'f7': (1233, 1165,),
+    'l3': (1185, 1261, 1280, 1271, 1242, 1252, 1290,),
+    'dn': (1195, 1205, 1214, 1224, 1234, 1243, 1262, 1272, 1281, 1291,),
+    'z': (1215, 1225, 1244, 1253, 1235, 3000, 1282, 1263, 1292, 1273, 1254, 3001, 1245, 1264, 1283, 1293, 1274, 1255, 1284, 3002, 1294, 1265, 1275, 1285, 1295,),
 }
 
 
@@ -905,6 +933,8 @@
 
 GRID = (2, 2, 2, 2, 2)
 PARTS = (4, 8, 11)
+GATHER_PARTS = (4, 8, 11)
+TURNED = ((0, 1),)
 BAND = 128
 TILE = 256
 
@@ -1005,7 +1035,7 @@
         for copy in load(index, slot):
             copy.wait()
 
-        crossing = functools.reduce(jnp.logical_or, [index + 1 == edge for edge in PARTS])
+        crossing = functools.reduce(jnp.logical_or, [index + 1 == edge for edge in GATHER_PARTS])
 
         @pl.when(jnp.logical_not(crossing))
         def _():
@@ -1175,7 +1205,8 @@
     edges = [0] + [part * TILE for part in PARTS]
     widest = max(*late_sizes, width // 2, *[high - low for low, high in zip(edges, edges[1:])])
     chunks = 6 * len(PARTS) + 4 + 2 * len(late_groups)
-    gathers = 6 * len(PARTS)
+    gather_edges = [0] + [part * TILE for part in GATHER_PARTS]
+    gathers = 6 * len(GATHER_PARTS)
     states = ((heads, VD, FEATS), BF16), ((heads, 1, FEATS), F32)
     sem = pltpu.SemaphoreType.DMA
 
@@ -1270,9 +1301,9 @@
         for spot, shard in enumerate((r.shard0, r.shard1, r.shard2)):
             r.wide[spot, :, columns:full] = jnp.zeros((rows, full - columns), BF16)
             r.wide[spot, :, 0:columns] = shard[...]
-        for low, high in zip(edges, edges[1:]):
+        for part, (low, high) in enumerate(zip(gather_edges, gather_edges[1:])):
             for weight in range(3):
-                for kind, first in enumerate("xy"):
+                for kind, first in enumerate("yy" if (part, weight) in TURNED else "xy"):
                     order = len(gather_list)
                     gather_list.append(
                         Gather(

time: 202 us -> 200 us (0.990)
  no operation moved by 1% of the time
where the time goes in v6:
time: 200 us
  Pallas kernels  199 us (100%)
    pallas_call x1, Pallas kernels, layer(): pl.pallas_call(body, out_shape=list(free_outs.values()) + list(outs.value...  194 us
    pallas_call x1, Pallas kernels, hand_over(): pl.pallas_call(body, out_shape=[shape(value.shape, value.dtype) for value...  4.96 us

profile of v6, /device:TPU:0, one launch (start us, length us, event | category | flops | bytes accessed | tf_op | source)
XLA Modules:
  0.0 200.1 jit_solution(5618399350572531265)
XLA Ops:
  0.6 194.4 %shard_map.221 = (bf16[1024,2816]{1,0:T(8,128)(2,1)}, bf16[1024,2816]{1,0:T(8,128)(2,1)}, bf16[1024,2816]{1,0:T(8,128)(2,1)}, bf16[1024,2816]{1,0:T(8,128)(2,1)}...) custom-call(bf16[32,2752]{1,0:T(8,128)(2,1)} %refs_0_.1, ...), custom_call_target="tpu_custom_call" | custom-call | tf_op jit(solution)/shard_map/pallas_call | solution.py:1395
  195.0 5.0 %shard_map.222 = (bf16[512,1024]{1,0:T(8,128)(2,1)}, f32[512,1024]{1,0:T(8,128)}, f32[32,2752]{1,0:T(8,128)}, f32[32,2752]{1,0:T(8,128)}, f32[32,2752]{1,0:T(8,1...) custom-call(bf16[512,1024]{1,0:T(8,128)(2,1)} %get-tuple-element.32., ...), custom_call_target="tpu_custom_call" | custom-call | tf_op jit(solution)/shard_map/pallas_call | solution.py:1431

commit v7 on v6

--- a/solution.py
+++ b/solution.py
@@ -970,7 +970,7 @@
         r.normed[band, :] = normalize(r.tok[band, :].astype(F32), r.gain_row[...]).astype(BF16)
 
     bands(r.count, norm)
-    r.ready("wq", "wk", "wv", "og", "wo")
+    r.ready("wq", "wk", "wv")
     r.query[...] = dot(r.normed[...], r.wq[...]).astype(BF16)
     r.keys[...] = dot(r.normed[...], r.wk[...]).astype(BF16)
     work.pause("qk")
@@ -990,6 +990,8 @@
         r.query, *tables, r.state, r.total, r.middle, r.inverse, r.mixed, work.between("b", pairs)
     )
 
+    r.ready("wo")
+
     def project_out(band):
         r.middle[:, band] = r.tok[:, band].astype(F32) + dot(r.mixed[...], r.wo[:, band])
 
@@ -1021,6 +1023,7 @@
             for i, ref in enumerate(r.grads_flat)
         ]
 
+    r.ready("og")
     low_t[...] = r.low[...].T
     og_t[...] = r.og[...].T
     acc_out[...] = r.middle[...]

time: 200 us -> 200 us (level)
  no operation moved by 1% of the time
where the time goes in v7:
time: 200 us
  Pallas kernels  199 us (100%)
    pallas_call x1, Pallas kernels, layer(): pl.pallas_call(body, out_shape=list(free_outs.values()) + list(outs.value...  194 us
    pallas_call x1, Pallas kernels, hand_over(): pl.pallas_call(body, out_shape=[shape(value.shape, value.dtype) for value...  4.96 us

profile of v7, /device:TPU:0, one launch (start us, length us, event | category | flops | bytes accessed | tf_op | source)
XLA Modules:
  0.0 200.2 jit_solution(1815275864053315470)
XLA Ops:
  0.6 194.4 %shard_map.221 = (bf16[1024,2816]{1,0:T(8,128)(2,1)}, bf16[1024,2816]{1,0:T(8,128)(2,1)}, bf16[1024,2816]{1,0:T(8,128)(2,1)}, bf16[1024,2816]{1,0:T(8,128)(2,1)}...) custom-call(bf16[32,2752]{1,0:T(8,128)(2,1)} %refs_0_.1, ...), custom_call_target="tpu_custom_call" | custom-call | tf_op jit(solution)/shard_map/pallas_call | solution.py:1398
  195.1 5.0 %shard_map.222 = (bf16[512,1024]{1,0:T(8,128)(2,1)}, f32[512,1024]{1,0:T(8,128)}, f32[32,2752]{1,0:T(8,128)}, f32[32,2752]{1,0:T(8,128)}, f32[32,2752]{1,0:T(8,1...) custom-call(bf16[512,1024]{1,0:T(8,128)(2,1)} %get-tuple-element.32., ...), custom_call_target="tpu_custom_call" | custom-call | tf_op jit(solution)/shard_map/pallas_call | solution.py:1434

commit v8 on v7

--- a/solution.py
+++ b/solution.py
@@ -853,77 +853,82 @@
 
 PLAN = {
     's': (0, 10,),
-    'qk': (20,),
-    'v': (30,),
-    'st0': (1, 40,),
-    'st2': (11, 50,),
-    'st4': (21, 60,),
-    'st6': (2, 31,),
+    'qk': (20, 30,),
+    'v': (40, 1,),
+    'st1': (50,),
+    'st2': (11,),
+    'st3': (60,),
+    'st4': (21,),
+    'st5': (2,),
+    'st6': (31,),
     'e0': (2000,),
     'a0': (41,),
-    'a1': (51,),
-    'a2': (2001, 12, 61,),
-    'a4': (22,),
-    'a7': (32,),
-    'e0w': (3, 13, 2002, 42, 2003,),
-    'b0': (23, 52,),
-    'b4': (4, 14, 43, 62,),
-    'b7': (33, 70,),
-    'po': (5, 15, 80,),
-    'nm': (90,),
-    'p0': (24, 63, 100, 110, 53, 44, 120, 25, 130, 34, 140, 45, 71, 150, 91, 81, 160, 35, 111, 170, 64, 101, 131, 72, 121, 54, 151, 141, 65, 161, 82, 171, 55,),
-    't0': (73, 92,),
-    't1': (83, 102,),
-    't2': (93, 112,),
-    'm3': (122, 74, 103, 132, 84, 113, 75, 142, 123, 94, 85, 152, 133, 162, 104, 95, 143, 172, 114, 105, 153, 124, 163, 115,),
-    't3': (125, 134,),
-    'm4': (144, 173, 1000, 1010, 1020, 1030,),
-    't4': (135,),
-    'm5': (145, 154,),
-    't5': (164, 1001, 1011, 1040,),
-    'm6': (1021,),
-    't6': (174, 1031,),
-    'm7': (155, 165, 1041, 175,),
+    'a1': (12, 51,),
+    'a2': (2001, 61,),
+    'a3': (22,),
+    'a6': (32,),
+    'a7': (3,),
+    'e0w': (13, 42, 2002, 23, 2003, 52,),
+    'b2': (62,),
+    'b3': (14,),
+    'b4': (4, 43,),
+    'b5': (33,),
+    'b6': (70,),
+    'b7': (15, 80,),
+    'po': (5, 90,),
+    'nm': (24, 100,),
+    'p0': (53, 63, 110, 120, 44, 25, 130, 140, 71, 34, 150, 45, 91, 81, 160, 170, 111, 101, 35, 64, 131, 121, 141, 72, 54, 151, 92, 65, 161, 171, 55,),
+    'm0': (82,),
+    't0': (73,),
+    'm1': (102,),
+    'm2': (93, 112,),
+    't2': (83,),
+    'm3': (122, 74, 132, 103, 113, 142, 75, 152, 94, 84, 162, 133, 123, 95, 172, 85, 114, 153, 104, 143, 115, 105,),
+    't3': (124, 134, 163, 173,),
+    'm4': (1000, 1010, 1020, 1030,),
+    't4': (125,),
+    'm5': (135, 144, 154, 1001, 1040,),
+    't5': (1011, 1021,),
+    'm6': (164, 174, 1031,),
+    't6': (145,),
+    'm7': (155, 1041, 165, 175,),
     't7': (1002, 1012, 1050,),
     'm8': (1060,),
     't8': (1051,),
-    'm9': (1003, 1061, 1022, 1070,),
+    'm9': (1003, 1022, 1061, 1070,),
     't9': (1032, 1080,),
-    'm10': (1013, 1071,),
-    't10': (1023, 1081,),
-    'ft': (1042, 1052, 1090, 1100,),
-    'dm': (1004, 1033,),
+    'm10': (1071,),
+    't10': (1013,),
+    'ft': (1023, 1042, 1052, 1081, 1090, 1100,),
+    'dm': (1004,),
     'c0': (1091,),
-    'c1': (1101,),
-    'c2': (1043, 1062, 1110,),
-    'c4': (1014, 1072, 1120,),
-    'c5': (1053, 1024, 1111,),
-    'c6': (1005,),
-    'c7': (1121,),
+    'c2': (1033, 1062, 1110,),
+    'c3': (1101, 1014,),
+    'c4': (1043, 1072, 1120,),
+    'c6': (1005, 1024, 1111,),
     'e1': (2010,),
-    'og': (2011, 1015, 1063, 1082, 1130,),
-    'd0': (1025, 1034, 1044, 1092, 1131, 1140,),
-    'd1': (1035, 1073, 1083, 1102, 1054, 1112, 1045, 1141, 1150, 1160,),
-    'd2': (1064, 1093, 1151, 1161, 1122, 1170,),
-    'd3': (1055, 1084, 1103, 1132, 1171, 1180,),
-    'd4': (2012, 1065, 1074, 1113, 1123, 1152, 1181,),
-    'd5': (2013, 1075, 1085, 1104, 1133, 1142, 1190, 1200,),
-    'd6': (1105, 1094, 1124, 1153, 1172, 1191, 1201, 1143,),
-    'd7': (1095, 1125, 1114, 1134, 1162, 1182, 1210,),
-    'lq': (1154, 1192, 1220, 1230,),
-    'f0': (1173, 1211,),
-    'f1': (1115, 1202, 1135, 1221, 1231,),
-    'f2': (1144, 1174, 1163,),
-    'f3': (1183, 1222, 1212,),
-    'l1': (1155, 1240, 1250, 1232,),
-    'f4': (1164, 1184, 1193, 1203,),
-    'f5': (1145, 1241, 1251,),
-    'f6': (1175, 1194, 1204, 1223,),
-    'l2': (1213, 1260, 1270,),
-    'f7': (1233, 1165,),
-    'l3': (1185, 1261, 1280, 1271, 1242, 1252, 1290,),
-    'dn': (1195, 1205, 1214, 1224, 1234, 1243, 1262, 1272, 1281, 1291,),
-    'z': (1215, 1225, 1244, 1253, 1235, 3000, 1282, 1263, 1292, 1273, 1254, 3001, 1245, 1264, 1283, 1293, 1274, 1255, 1284, 3002, 1294, 1265, 1275, 1285, 1295,),
+    'og': (2011, 1015, 1082, 1130,),
+    'd0': (1025, 1034, 1044, 1063, 1092, 1140,),
+    'd1': (1035, 1053, 1073, 1083, 1102, 1121, 1045, 1131, 1150,),
+    'd2': (1064, 1084, 1112, 2012, 1093, 1160,),
+    'd3': (2013, 1065, 1085, 1054, 1074, 1103, 1132, 1141, 1151,),
+    'd4': (1055, 1104, 1113, 1094, 1122, 1161, 1170, 1180,),
+    'd5': (1075, 1105, 1133, 1152, 1171, 1181, 1142, 1190, 1200,),
+    'd6': (1095, 1114, 1123, 1191,),
+    'd7': (1134, 1143, 1153, 1162, 1172, 1201, 1115, 1210,),
+    'lq': (1220,),
+    'f0': (1124, 1135, 1182, 1154, 1211, 1221, 1230,),
+    'f2': (1163, 1192,),
+    'f3': (1144, 1173, 1222, 1125, 1231,),
+    'l1': (1183, 1240,),
+    'f4': (1155, 1174, 1193, 1202, 1250,),
+    'f5': (1145, 1184, 1223, 1241, 1212,),
+    'f6': (1175, 1164, 1194, 1203, 1251,),
+    'l2': (1185, 1224, 1232, 1260, 1270,),
+    'f7': (1213, 1165,),
+    'l3': (1195, 1242, 1261, 1225, 1271, 1280, 1290,),
+    'dn': (1204, 1214, 1233, 1243, 1252, 1262, 1272, 1281, 1291,),
+    'z': (1205, 1215, 1234, 1244, 3000, 1282, 1292, 1253, 3001, 1263, 1273, 1254, 1235, 1264, 1245, 1283, 1274, 1293, 3002, 1284, 1294, 1255, 1265, 1275, 1285, 1295,),
 }
 
 

time: 200 us -> 202 us (1.010)
    pallas_call x1, Pallas kernels: 194 us -> 196 us  [layer(): pl.pallas_call(body, out_shape=list(free_outs.values()) + list(outs.value...]
where the time goes in v8:
time: 202 us
  Pallas kernels  201 us (100%)
    pallas_call x1, Pallas kernels, layer(): pl.pallas_call(body, out_shape=list(free_outs.values()) + list(outs.value...  196 us
    pallas_call x1, Pallas kernels, hand_over(): pl.pallas_call(body, out_shape=[shape(value.shape, value.dtype) for value...  4.96 us

profile of v8, /device:TPU:0, one launch (start us, length us, event | category | flops | bytes accessed | tf_op | source)
XLA Modules:
  0.0 202.2 jit_solution(7608086834997725202)
XLA Ops:
  0.6 196.4 %shard_map.221 = (bf16[1024,2816]{1,0:T(8,128)(2,1)}, bf16[1024,2816]{1,0:T(8,128)(2,1)}, bf16[1024,2816]{1,0:T(8,128)(2,1)}, bf16[1024,2816]{1,0:T(8,128)(2,1)}...) custom-call(bf16[32,2752]{1,0:T(8,128)(2,1)} %refs_0_.1, ...), custom_call_target="tpu_custom_call" | custom-call | tf_op jit(solution)/shard_map/pallas_call | solution.py:1403
  197.1 5.0 %shard_map.222 = (bf16[512,1024]{1,0:T(8,128)(2,1)}, f32[512,1024]{1,0:T(8,128)}, f32[32,2752]{1,0:T(8,128)}, f32[32,2752]{1,0:T(8,128)}, f32[32,2752]{1,0:T(8,1...) custom-call(bf16[512,1024]{1,0:T(8,128)(2,1)} %get-tuple-element.32., ...), custom_call_target="tpu_custom_call" | custom-call | tf_op jit(solution)/shard_map/pallas_call | solution.py:1439
